TPU v7x, 512 devices: a whole 4x4x16 slice. The times are simulated.
512 devices in a mesh: dp: 16 (over x, y), tm: 32 (over z, core).
Axes of the slice: x: 4, y: 4, z: 16, core: 2. Of those that a mesh axis runs over, the one named last changes fastest.
Arguments:
- records: bfloat16 [16, 4096, 1024], P('dp', 'tm'), may hold values from -6 to 6
- x_weight: bfloat16 [1024, 512], replicated, may hold values from -0.1875 to 0.1875
- bc_weight: bfloat16 [1024, 256], replicated, may hold values from -0.1875 to 0.1875
- decay_codes: int32 [16, 4096, 8], P('dp', 'tm'), may hold values from 0 to 524
- out_grad: bfloat16 [16, 4096, 512], P('dp', 'tm'), may hold values from -6 to 6
Outputs:
- y_out: bfloat16 [16, 4096, 512], P('dp', 'tm')
- x_grad: float32 [1024, 512], P('tm')
- bc_grad: float32 [1024, 256], P('tm')
All inputs are finite; a program needn't handle non-finite values.
Results may differ from a plain program's by a relative error of at most 0.0085.
Values sent between devices are 32-bit elements; how exact they have to be, the bound alone decides.
No kernel may reach another device: no remote copies, remote signals or barrier semaphores. Data moves between devices by JAX's collectives and lax.ppermute only.
A program may use at most 64 MiB of HBM per device.

v0:
```python
import jax
import jax.numpy as jnp
from jax import lax
from jax.sharding import PartitionSpec as P

SPAN = 128


highest = lax.Precision.HIGHEST


def entering(part, axis, combine, identity, reverse):
    count = lax.axis_size(axis)
    place = lax.axis_index(axis)
    ahead = count - 1 - place if reverse else place
    gathered = jax.tree.map(lambda a: lax.all_gather(a, axis), part)
    state = jax.tree.map(lambda a, e: jnp.zeros_like(a) + jnp.asarray(e, a.dtype), part, identity)

    def one(turn, state):
        source = count - 1 - turn if reverse else turn
        return combine(
            state, jax.tree.map(lambda a: lax.dynamic_index_in_dim(a, source, 0, False), gathered)
        )

    return lax.fori_loop(0, ahead, one, state)


def span_kernel(log_decay):
    running = jnp.cumsum(log_decay, axis=1)
    length = log_decay.shape[1]
    causal = lax.broadcasted_iota(jnp.int32, (length, length), 0) >= lax.broadcasted_iota(
        jnp.int32, (length, length), 1
    )
    causal = causal[None, None, :, :]
    heads_first = jnp.transpose(running, (0, 2, 1))
    gaps = heads_first[:, :, :, None] - heads_first[:, :, None, :]
    kernel = jnp.where(causal, jnp.exp(jnp.where(causal, gaps, 0.0)), 0.0)
    return (running, kernel)


def block_scores(readout, inject):
    return jnp.einsum(
        "rtn,rsn->rts",
        readout.astype(jnp.bfloat16),
        inject.astype(jnp.bfloat16),
        preferred_element_type=jnp.float32,
    )


def forward_span(carry_state, pieces):
    mixer_f, inject, readout, cot_heads, log_decay = pieces
    running, kernel = span_kernel(log_decay)
    scores = block_scores(readout, inject)
    mixing = kernel * scores[:, None, :, :]
    decayed = jnp.exp(running)
    within = jnp.einsum("rhts,rshp->rthp", mixing, mixer_f, precision=highest)
    carried = decayed[..., None] * jnp.einsum(
        "rhpn,rtn->rthp", carry_state, readout, precision=highest
    )
    pair_dots = jnp.einsum("rthp,rshp->rhts", cot_heads, mixer_f, precision=highest)
    grad_read = jnp.einsum("rhts,rsn->rtn", kernel * pair_dots, inject, precision=highest)
    grad_read = grad_read + jnp.einsum(
        "rthp,rhpn->rtn", decayed[..., None] * cot_heads, carry_state, precision=highest
    )
    to_end = jnp.exp(running[:, -1:, :] - running)
    new_state = jnp.exp(running[:, -1, :])[:, :, None, None] * carry_state
    new_state = new_state + jnp.einsum(
        "rshp,rsn->rhpn", to_end[..., None] * mixer_f, inject, precision=highest
    )
    return (new_state, (within + carried, grad_read))


def reverse_span(adjoint, pieces):
    mixer_f, inject, readout, cot_heads, log_decay = pieces
    running, kernel = span_kernel(log_decay)
    scores = block_scores(readout, inject)
    mixing = kernel * scores[:, None, :, :]
    pair_dots = jnp.einsum("rthp,rshp->rhts", cot_heads, mixer_f, precision=highest)
    to_end = jnp.exp(running[:, -1:, :] - running)
    grad_mixer = jnp.einsum("rhts,rthp->rshp", mixing, cot_heads, precision=highest)
    grad_mixer = grad_mixer + to_end[..., None] * jnp.einsum(
        "rhpn,rsn->rshp", adjoint, inject, precision=highest
    )
    grad_inject = jnp.einsum("rhts,rtn->rsn", kernel * pair_dots, readout, precision=highest)
    grad_inject = grad_inject + jnp.einsum(
        "rshp,rhpn->rsn", to_end[..., None] * mixer_f, adjoint, precision=highest
    )
    new_adjoint = jnp.exp(running[:, -1, :])[:, :, None, None] * adjoint
    new_adjoint = new_adjoint + jnp.einsum(
        "rthp,rtn->rhpn", jnp.exp(running)[..., None] * cot_heads, readout, precision=highest
    )
    return (new_adjoint, (grad_mixer, grad_inject))


def to_blocks(array, frames):
    return array.reshape((frames // SPAN, 1, SPAN) + array.shape[1:])


def combine_pair(earlier, later_one):
    return (earlier[0] * later_one[0], later_one[0][:, :, None, None] * earlier[1] + later_one[1])


def body(records, x_weight, bc_weight, decay_codes, out_grad):
    signal = records[0]
    codes = decay_codes[0]
    frames_dev, model_dim = signal.shape
    head_count = codes.shape[1]
    mixer_dim = x_weight.shape[1]
    head_size = mixer_dim // head_count
    state_size = bc_weight.shape[1] // 2
    tm_count = lax.axis_size("tm")
    groups = lax.axis_size("dp")
    out_scale = (state_size * frames_dev * tm_count) ** (-0.5)
    grad_scale = (groups * frames_dev * tm_count) ** (-0.5)
    decay_unit = 1.0 / (32.0 * frames_dev * tm_count)
    mixer_in = jnp.dot(signal, x_weight, preferred_element_type=jnp.float32).astype(jnp.bfloat16)
    state_proj = jnp.dot(signal, bc_weight, preferred_element_type=jnp.float32).astype(jnp.bfloat16)
    log_decay = -decay_unit * codes.astype(jnp.float32)
    cotangent = out_grad[0].astype(jnp.float32) * out_scale
    mixer_f = mixer_in.astype(jnp.float32).reshape(frames_dev, head_count, head_size)
    inject = state_proj[:, :state_size].astype(jnp.float32)
    readout = state_proj[:, state_size:].astype(jnp.float32)
    cot_heads = cotangent.reshape(frames_dev, head_count, head_size)
    blocks = (
        to_blocks(mixer_f, frames_dev),
        to_blocks(inject, frames_dev),
        to_blocks(readout, frames_dev),
        to_blocks(cot_heads, frames_dev),
        to_blocks(log_decay, frames_dev),
    )
    zero_state = jnp.zeros((1, head_count, head_size, state_size), jnp.float32)
    end_state, (local_out, local_read) = lax.scan(forward_span, zero_state, blocks)
    start_adjoint, (local_grad, local_inject) = lax.scan(
        reverse_span, zero_state, blocks, reverse=True
    )
    running = jnp.cumsum(log_decay, axis=0)
    device_log = running[-1]
    identity = (jnp.ones((1, head_count), jnp.float32), zero_state)
    carry_in = entering(
        (jnp.exp(device_log)[None], end_state), "tm", combine_pair, identity, False
    )[1][0]
    adjoint_in = entering(
        (jnp.exp(device_log)[None], start_adjoint), "tm", combine_pair, identity, True
    )[1][0]
    decayed = jnp.exp(running)
    to_end = jnp.exp(device_log[None] - running)
    output = local_out.reshape(frames_dev, head_count, head_size)
    output = output + decayed[..., None] * jnp.einsum(
        "hpn,tn->thp", carry_in, readout, precision=highest
    )
    grad_read = local_read.reshape(frames_dev, state_size)
    grad_read = grad_read + jnp.einsum(
        "thp,hpn->tn", decayed[..., None] * cot_heads, carry_in, precision=highest
    )
    grad_mixer = local_grad.reshape(frames_dev, head_count, head_size)
    grad_mixer = grad_mixer + to_end[..., None] * jnp.einsum(
        "hpn,tn->thp", adjoint_in, inject, precision=highest
    )
    grad_inject = local_inject.reshape(frames_dev, state_size)
    grad_inject = grad_inject + jnp.einsum(
        "thp,hpn->tn", to_end[..., None] * mixer_f, adjoint_in, precision=highest
    )
    grad_mix = grad_mixer.reshape(frames_dev, mixer_dim).astype(jnp.bfloat16)
    grad_proj = jnp.concatenate([grad_inject, grad_read], axis=1).astype(jnp.bfloat16)
    grad_cat = jnp.concatenate([grad_mix, grad_proj], axis=1)
    grad_share = lax.psum_scatter(
        lax.dot_general(
            signal, grad_cat, (((0,), (0,)), ((), ())), preferred_element_type=jnp.float32
        ),
        "tm",
        scatter_dimension=0,
        tiled=True,
    )
    grad_share = lax.psum(grad_share, "dp")
    grad_share = grad_share * grad_scale
    y_out = output.reshape(frames_dev, mixer_dim).astype(jnp.bfloat16)[None]
    return (y_out, grad_share[:, :mixer_dim], grad_share[:, mixer_dim:])


def solution(mesh):
    return jax.shard_map(
        body,
        mesh=mesh,
        in_specs=(P("dp", "tm", None), P(), P(), P("dp", "tm", None), P("dp", "tm", None)),
        out_specs=(P("dp", "tm", None), P("tm", None), P("tm", None)),
        check_vma=False,
    )
```

profile of v0, /device:TPU:32, one launch (start us, length us, event | category | flops | bytes accessed | tf_op | source)
XLA Modules:
  0.0 444.9 jit_solution(17753559127679987640)
XLA Ops:
  9.1 1.4 convolution_convert_fusion.1
  10.5 1.3 convert_multiply_fusion
  11.9 1.0 convolution_add_fusion.1
  13.0 1.0 copy.79
  14.1 1.0 convolution_add_fusion
  15.5 33.9 %all-gather.3 = f32[32,1,8]{2,1,0:T(1,128)S(1)} all-gather(f32[1,1,8]{2,1,0:T(1,128)S(1)} %get-tuple-element.267), channel_id=2, replica_groups=mesh['dp'=16,'tm'=32] {'tm'}, dimensions={0}, use_global_device_ids=true | all-gather | bytes 1056 | tf_op jit(solution)/shard_map/all_gather | solution.py:16
  52.1 44.4 %all-gather.7.cloned.1.call-done = f32[256,64,128]{2,1,0:T(8,128)} async-done(((f32[8,64,128]{2,1,0:T(8,128)}), f32[256,64,128]{2,1,0:T(8,128)}) %all-gather.7.cloned.1.call-update) | async-done | bytes 8388624 | tf_op jit(solution)/shard_map/all_gather | solution.py:16
  96.6 2.2 while.16
  96.6 1.1 bitcast_add_fusion.4
  97.7 1.1 bitcast_add_fusion.4
  98.8 76.1 %all-gather.9.cloned.1.call-done = f32[256,64,128]{2,1,0:T(8,128)} async-done(((f32[8,64,128]{2,1,0:T(8,128)}), f32[256,64,128]{2,1,0:T(8,128)}) %all-gather.9.cloned.1.call-update) | async-done | bytes 8388624 | tf_op jit(solution)/shard_map/all_gather | solution.py:16
  174.9 31.9 %while.17 = (s32[]{:T(128)}, f32[1,8,64,128]{3,2,1,0:T(8,128)S(1)}, s32[]{:T(128)}, f32[32,1,8]{2,1,0:T(1,128)S(1)}, f32[32,1,8,64,128]{4,3,2,1,0:T(8,128)}, /*index=5*/s32[]{:T(128)}, s32[]{:T(128)}, s32[]{:T(128)}, s32[]{:T(128)}) while((s32[]{:T(128)}, f32[1,8,64,128]{3,2,1,0:T(8,128)S(1)}, s32[]{:T(128)}, f32[32,1,8]{2,1,0:T(1,128)S(1)}, ...), condition=%wide.region_5.6_spmd, body=%wide.region_4.5_spmd.sunk | while | flops 131078 | bytes 786683 | solution.py:25
  174.9 1.1 bitcast_add_fusion.5
  176.0 1.1 bitcast_add_fusion.5
  177.1 1.1 bitcast_add_fusion.5
  178.2 1.1 bitcast_add_fusion.5
  179.3 1.1 bitcast_add_fusion.5
  180.4 1.1 bitcast_add_fusion.5
  181.5 1.1 bitcast_add_fusion.5
  182.6 1.1 bitcast_add_fusion.5
  183.7 1.1 bitcast_add_fusion.5
  184.8 1.1 bitcast_add_fusion.5
  185.9 1.1 bitcast_add_fusion.5
  187.0 1.1 bitcast_add_fusion.5
  188.1 1.1 bitcast_add_fusion.5
  189.2 1.1 bitcast_add_fusion.5
  190.4 1.1 bitcast_add_fusion.5
  191.5 1.1 bitcast_add_fusion.5
  192.6 1.1 bitcast_add_fusion.5
  193.7 1.1 bitcast_add_fusion.5
  194.8 1.1 bitcast_add_fusion.5
  195.9 1.1 bitcast_add_fusion.5
  197.0 1.1 bitcast_add_fusion.5
  198.1 1.1 bitcast_add_fusion.5
  199.2 1.1 bitcast_add_fusion.5
  200.3 1.1 bitcast_add_fusion.5
  201.4 1.1 bitcast_add_fusion.5
  202.5 1.1 bitcast_add_fusion.5
  203.6 1.1 bitcast_add_fusion.5
  204.7 1.1 bitcast_add_fusion.5
  205.8 1.1 bitcast_add_fusion.5
  208.8 2.2 convolution_bitcast_fusion
  211.1 3.5 copy.87
  215.7 101.2 %reduce-scatter.4.cloned.1.call-done = f32[32,768]{1,0:T(8,128)} async-done(((f32[1024,768]{1,0:T(8,128)}), f32[32,768]{1,0:T(8,128)}) %reduce-scatter.4.cloned.1.call-update) | async-done | bytes 98320
  316.9 1.8 copy.88
  319.0 0.8 copy.84
  319.7 116.2 %all-reduce.2.cloned.1.call-done = f32[32,768]{0,1:T(8,128)} async-done(((f32[32,768]{0,1:T(8,128)}), f32[32,768]{0,1:T(8,128)}) %all-reduce.2.cloned.1.call-update) | async-done | bytes 98320 | tf_op jit(solution)/shard_map/psum | solution.py:174
  435.9 1.0 broadcast_multiply_fusion
  (86 shorter events, 10.2 us)
Async XLA Ops:
  7.2 3.3 copy-start
  7.2 89.4 %all-gather.7.cloned.1.call-start = ((), (), s32[]{:S(2)}) async-start(), calls=%async_computation.2 | async-start | bytes 8650752 | tf_op jit(solution)/shard_map/all_gather | solution.py:16
  12.9 161.9 %all-gather.9.cloned.1.call-start = ((), (), s32[]{:S(2)}) async-start(), calls=%async_computation.3 | async-start | bytes 8650752 | tf_op jit(solution)/shard_map/all_gather | solution.py:16
  14.1 194.7 %copy-start.1 = (bf16[1,128,1024]{2,1,0:T(8,128)(2,1)S(1)}, bf16[1,128,1024]{2,1,0:T(8,128)(2,1)}, u32[]{:S(2)}) copy-start(bf16[1,128,1024]{2,1,0:T(8,128)(2,1)} %param.9) | copy-start | bytes 786436
  15.1 301.7 %reduce-scatter.4.cloned.1.call-start = ((), (), s32[]{:S(2)}) async-start(), calls=%async_computation.4 | async-start | bytes 3244032
  214.6 221.3 %all-reduce.2.cloned.1.call-start = ((), (), s32[]{:S(2)}) async-start(), calls=%async_computation.1 | async-start | bytes 786432 | tf_op jit(solution)/shard_map/psum | solution.py:174
Sparse Core Ops, SparseCore 0:
  13.0 83.4 all-gather.6
  98.7 76.1 all-gather.8
  214.7 102.0 reduce-scatter.3
  320.3 115.5 all-reduce.1
where the time goes:
time: 446 us; the launch traced here: 445 us
  waiting for transfers between devices  338 us (76%)
  other arithmetic  35.2 us (8%)
  blocking collectives  33.9 us (8%)
  between operations  14 us (3%)
  matrix products  12.6 us (3%)
  local copies, waits for them, and re-layouts  10 us (2%)
    all_gather x2, waiting for transfers between devices, entering(): gathered = jax.tree.map(lambda a: lax.all_gather(a, axis), part)  121 us
    psum x1, waiting for transfers between devices, body(): grad_share = lax.psum(grad_share, 'dp')  116 us
    unnamed x5, waiting for transfers between devices  101 us
    all_gather x1, blocking collectives, entering(): gathered = jax.tree.map(lambda a: lax.all_gather(a, axis), part)  33.9 us
    add x31, other arithmetic, combine_pair(): later_one[0][:, :, None, None] * earlier[1] + later_one[1]  32.9 us
  transfers between devices with their start and end apart: 4, of which 4 were waited for; matrix products, arithmetic and copies ran while one was open for 2% of the time, Pallas kernels for 0%

commit v1 on v0

v1 whole, which is shorter than its diff:
```python
import jax
import jax.numpy as jnp
from jax import lax
from jax.experimental import pallas as pl
from jax.experimental.pallas import tpu as pltpu
from jax.sharding import Mesh, PartitionSpec as P

f32 = jnp.float32
bf16 = jnp.bfloat16

LD = 128
CHIP = 2 * LD
HEADS = 8
HEAD = 64
STATE = 128
HALF = HEADS * HEAD // 2
ZN = 16
DP = 16
ROWS = HALF // ZN
PAY = 2 * ROWS + 8


def mm(a, b):
    return jnp.dot(a, b, preferred_element_type=f32)


def mm_tn(a, b):
    return lax.dot_general(a, b, (((0,), (0,)), ((), ())), preferred_element_type=f32)


def mm_nt(a, b):
    return lax.dot_general(a, b, (((1,), (1,)), ((), ())), preferred_element_type=f32)


def causal(shape):
    return lax.broadcasted_iota(jnp.int32, shape, 0) >= lax.broadcasted_iota(jnp.int32, shape, 1)


def local_kernel(unit, c_ref, x_ref, g_ref, codes_ref, pack_ref, wx_ref, wbc_ref,
                 pay_ref, u_ref, ue_ref, v_ref, en_ref, ep_ref, te_ref, proj_ref, xc_ref,
                 gs_ref, cs_ref):
    c = c_ref[0]
    own = pl.multiple_of(c * LD, LD)
    oth = pl.multiple_of((1 - c) * LD, LD)
    d = x_ref.shape[1]
    xc_ref[pl.ds(own, LD), :] = x_ref[...]
    xc_ref[pl.ds(oth, LD), :] = pack_ref[:, :d].astype(bf16)
    gs_ref[pl.ds(own, LD), :] = g_ref[...].astype(f32)
    gs_ref[pl.ds(oth, LD), :] = pack_ref[:, d:d + HALF]
    cs_ref[pl.ds(own, LD), :] = codes_ref[...].astype(f32)
    cs_ref[pl.ds(oth, LD), :] = pack_ref[:, d + HALF:d + HALF + HEADS]
    codes = cs_ref[...]
    hi = jnp.floor(codes * (1.0 / 32.0))
    lo = codes - 32.0 * hi
    row = lax.broadcasted_iota(jnp.int32, (HEADS, HALF), 0)
    col = lax.broadcasted_iota(jnp.int32, (HEADS, HALF), 1)
    spread = jnp.where(row == col // HEAD + c * (HEADS // 2), 1.0, 0.0).astype(bf16)
    hi = mm(hi.astype(bf16), spread).astype(bf16)
    lo = mm(lo.astype(bf16), spread).astype(bf16)
    tri = jnp.where(causal((CHIP, CHIP)), 1.0, 0.0).astype(bf16)
    running = unit * (32.0 * mm(tri, hi) + mm(tri, lo))
    last = running[CHIP - 1:CHIP, :]
    en = jnp.exp(-running)
    ep = jnp.exp(running)
    te = jnp.exp(running - last)
    en_ref[...] = en
    ep_ref[...] = ep
    te_ref[...] = te
    xv = xc_ref[...]
    mixer = mm(xv, wx_ref[...]).astype(bf16).astype(f32)
    proj = mm(xv, wbc_ref[...]).astype(bf16)
    proj_ref[...] = proj
    v = (en * gs_ref[...]).astype(bf16)
    ue = (te * mixer).astype(bf16)
    u_ref[...] = (ep * mixer).astype(bf16)
    ue_ref[...] = ue
    v_ref[...] = v
    state = mm_tn(ue, proj[:, :STATE])
    adjoint = mm_tn(v, proj[:, STATE:])
    pay_ref[:, 0:ROWS, :] = state.reshape(ZN, ROWS, STATE)
    pay_ref[:, ROWS:2 * ROWS, :] = adjoint.reshape(ZN, ROWS, STATE)
    per = ZN // (HEADS // 2)
    for h in range(HEADS // 2):
        total = jnp.broadcast_to(last[:, h * HEAD:h * HEAD + 1], (8, STATE))
        for k in range(per):
            pay_ref[h * per + k, 2 * ROWS:, :] = total


def inner_kernel(u_ref, v_ref, proj_ref, yl_ref, gm_ref, gp_ref):
    mask = causal((CHIP, CHIP))
    inject = proj_ref[:, :STATE]
    readout = proj_ref[:, STATE:]
    u = u_ref[...]
    v = v_ref[...]
    scores = jnp.where(mask, mm_nt(readout, inject), 0.0).astype(bf16)
    pairs = jnp.where(mask, mm_nt(v, u), 0.0).astype(bf16)
    yl_ref[...] = mm(scores, u)
    gm_ref[...] = mm_tn(scores, v)
    gp_ref[:, :STATE] = mm_tn(pairs, readout)
    gp_ref[:, STATE:] = mm(pairs, inject)


def scan_kernel(in_ref, out_ref):
    decay = [jnp.exp(-in_ref[k, 2 * ROWS:2 * ROWS + 1, :]) for k in range(ZN)]
    carry = jnp.zeros((ROWS, STATE), f32)
    for k in range(ZN):
        out_ref[k, 0:ROWS, :] = carry
        if k + 1 < ZN:
            carry = decay[k] * carry + in_ref[k, 0:ROWS, :]
    carry = jnp.zeros((ROWS, STATE), f32)
    for k in reversed(range(ZN)):
        out_ref[k, ROWS:, :] = carry
        if k:
            carry = decay[k] * carry + in_ref[k, ROWS:2 * ROWS, :]


def outer_kernel(scale, c_ref, in_ref, u_ref, v_ref, en_ref, ep_ref, te_ref, proj_ref,
                 yl_ref, gml_ref, gp_ref, gm_ref, pk_ref, ps_ref, yk_ref, ys_ref, y_ref):
    c = c_ref[0]
    carry = in_ref[:, 0:ROWS, :].reshape(HALF, STATE).astype(bf16)
    adjoint = in_ref[:, ROWS:, :].reshape(HALF, STATE).astype(bf16)
    inject = proj_ref[:, :STATE]
    readout = proj_ref[:, STATE:]
    gi = scale * (gp_ref[:, :STATE] + mm(u_ref[...], adjoint))
    gr = scale * (gp_ref[:, STATE:] + mm(v_ref[...], carry))
    pk_ref[...] = jnp.where(c == 0, gi, gr)
    ps_ref[...] = jnp.where(c == 0, gr, gi)
    grad = ep_ref[...] * gml_ref[...] + te_ref[...] * mm_nt(inject, adjoint)
    gm_ref[...] = (scale * grad).astype(bf16)
    y_ref[...] = en_ref[...] * (yl_ref[...] + mm_nt(readout, carry))
    yk_ref[...] = y_ref[pl.ds(pl.multiple_of(c * LD, LD), LD), :]
    ys_ref[...] = y_ref[pl.ds(pl.multiple_of((1 - c) * LD, LD), LD), :]


def weight_kernel(xt_ref, gm_ref, pk_ref, pr_ref, out_ref):
    xt = xt_ref[...]
    out_ref[:, :HALF] = mm(xt, gm_ref[...])
    out_ref[:, HALF:] = mm(xt, (pk_ref[...] + pr_ref[...]).astype(bf16))


def join_kernel(c_ref, yk_ref, yr_ref, out_ref):
    c = c_ref[0]
    yk = yk_ref[...].astype(bf16)
    yr = yr_ref[...].astype(bf16)

    @pl.when(c == 0)
    def _():
        out_ref[:, :HALF] = yk
        out_ref[:, HALF:] = yr

    @pl.when(c != 0)
    def _():
        out_ref[:, :HALF] = yr
        out_ref[:, HALF:] = yk


def whole(shape):
    return pl.BlockSpec(shape, lambda i, c: (0,) * len(shape))


def call(kernel, outs, ins, scratch=(), c=None, specs=None):
    params = pltpu.CompilerParams(vmem_limit_bytes=48 * 1024 * 1024)
    shapes = [jax.ShapeDtypeStruct(s, d) for s, d in outs]
    if c is None:
        return pl.pallas_call(kernel, out_shape=shapes, compiler_params=params)(*ins)
    specs = specs or [whole(a.shape) for a in ins]
    return pl.pallas_call(
        kernel,
        out_shape=shapes,
        grid_spec=pltpu.PrefetchScalarGridSpec(
            num_scalar_prefetch=1, grid=(1,), in_specs=specs,
            out_specs=[whole(s) for s, _ in outs], scratch_shapes=list(scratch)),
        compiler_params=params,
    )(c, *ins)


def body(records, x_weight, bc_weight, decay_codes, out_grad):
    x = records[0]
    g = out_grad[0]
    codes = decay_codes[0]
    d = x.shape[1]
    frames = LD * 2 * ZN
    unit = 1.0 / (32.0 * frames)
    out_scale = float((STATE * frames) ** -0.5)
    grad_scale = float((DP * frames) ** -0.5)
    core = lax.axis_index("c")
    c = core.astype(jnp.int32).reshape(1)
    swap = [(0, 1), (1, 0)]

    g_send = jnp.where(core == 0, g[:, HALF:], g[:, :HALF]).astype(f32)
    pad = jnp.zeros((LD, 128 - HEADS), f32)
    pack = jnp.concatenate([x.astype(f32), g_send, codes.astype(f32), pad], axis=1)
    pack = lax.ppermute(pack, "c", swap)

    ins = (x, g, codes, pack, x_weight, bc_weight)
    specs = [whole(x.shape), pl.BlockSpec((LD, HALF), lambda i, c: (0, c[0])), whole(codes.shape),
             whole(pack.shape), pl.BlockSpec((d, HALF), lambda i, c: (0, c[0])), whole(bc_weight.shape)]
    sq = (CHIP, HALF)
    pay, u, ue, v, en, ep, te, proj, xc = call(
        lambda *refs: local_kernel(unit, *refs),
        [((ZN, PAY, STATE), f32), (sq, bf16), (sq, bf16), (sq, bf16), (sq, f32), (sq, f32), (sq, f32),
         ((CHIP, 2 * STATE), bf16), ((CHIP, d), bf16)],
        ins, [pltpu.VMEM(sq, f32), pltpu.VMEM((CHIP, HEADS), f32)], c, specs)

    pay = lax.all_to_all(pay, "z", 0, 0, tiled=True)
    yl, gml, gpl = call(inner_kernel, [(sq, f32), (sq, f32), ((CHIP, 2 * STATE), f32)], (u, v, proj))
    xt = xc.T.reshape(ZN, 2, DP, 2, CHIP).transpose(2, 0, 1, 3, 4).reshape(d, CHIP)
    (pay,) = call(scan_kernel, [((ZN, 2 * ROWS, STATE), f32)], (pay,))
    pay = lax.all_to_all(pay, "z", 0, 0, tiled=True)

    gm, pk, ps, yk, ys = call(
        lambda *refs: outer_kernel(out_scale, *refs),
        [(sq, bf16), ((CHIP, STATE), f32), ((CHIP, STATE), f32), ((LD, HALF), f32), ((LD, HALF), f32)],
        (pay, ue, v, en, ep, te, proj, yl, gml, gpl), [pltpu.VMEM(sq, f32)], c)
    pr = lax.ppermute(ps, "c", swap)
    yr = lax.ppermute(ys, "c", swap)
    width = HALF + STATE
    (grad,) = call(weight_kernel, [((d, width), f32)], (xt, gm, pk, pr))
    (y,) = call(join_kernel, [((LD, 2 * HALF), bf16)], (yk, yr), (), c)

    part = lax.all_to_all(grad.reshape(DP, d // DP, width), "dp", 0, 0, tiled=True)
    part = jnp.sum(part, axis=0).reshape(ZN, d // DP // ZN, width)
    part = lax.all_to_all(part, "z", 0, 0, tiled=True)
    part = (jnp.sum(part, axis=0) * grad_scale).reshape(1, 2, 2, width)
    part = jnp.broadcast_to(part, (DP, 2, 2, width)).reshape(2 * DP, 2, width)
    part = lax.all_to_all(part, ("dp", "c"), 0, 0, tiled=True)
    part = part.reshape(DP, 2, 2, width).transpose(0, 2, 1, 3).reshape(2 * DP, 2, width)
    x_grad = part[:, :, :HALF].reshape(2 * DP, 2 * HALF)
    bc_grad = part[:, :, HALF:].reshape(2 * DP, 2 * STATE)
    return y[None], x_grad, bc_grad


def solution(mesh):
    mesh = Mesh(mesh.devices.reshape(DP, ZN, 2), ("dp", "z", "c"))
    frames = P("dp", ("z", "c"), None)
    rows = P(("z", "c"), None)
    return jax.shard_map(
        body,
        mesh=mesh,
        in_specs=(frames, P(), P(), frames, frames),
        out_specs=(frames, rows, rows),
        check_vma=False,
    )
```

time: 446 us -> 140 us (0.31)
  the two profiles are of different devices: /device:TPU:32 before, /device:TPU:1 now
where the time goes in v1:
time: 140 us; the launch traced here: 139 us
  blocking collectives  52.9 us (38%)
  starting transfers between devices  45.8 us (33%)
  waiting for transfers between devices  27.8 us (20%)
  local copies, waits for them, and re-layouts  6.41 us (5%)
  Pallas kernels  3.72 us (3%)
  other arithmetic  2.01 us (1%)
    all_to_all x1, blocking collectives, body(): lax.all_to_all(grad.reshape(DP, d // DP, width), 'dp', 0, 0, tiled=True)  28 us
    all_to_all x1, blocking collectives, body(): pay = lax.all_to_all(pay, 'z', 0, 0, tiled=True)  24.8 us
    all_to_all x1, waiting for transfers between devices, body(): pay = lax.all_to_all(pay, 'z', 0, 0, tiled=True)  11.8 us
    all_to_all x1, starting transfers between devices, body(): pay = lax.all_to_all(pay, 'z', 0, 0, tiled=True)  11.6 us
    ppermute x1, starting transfers between devices, body(): pack = lax.ppermute(pack, 'c', swap)  8.78 us
    ppermute x1, starting transfers between devices, body(): pr = lax.ppermute(ps, 'c', swap)  7.91 us
    all_to_all x1, waiting for transfers between devices, body(): part = lax.all_to_all(part, 'z', 0, 0, tiled=True)  7.46 us
    all_to_all x1, starting transfers between devices, body(): part = lax.all_to_all(part, ('dp', 'c'), 0, 0, tiled=True)  7.4 us
  transfers between devices with their start and end apart: 6, of which 4 were waited for; matrix products, arithmetic and copies ran while one was open for 1% of the time, Pallas kernels for 1%

profile of v1, /device:TPU:1, one launch (start us, length us, event | category | flops | bytes accessed | tf_op | source)
XLA Modules:
  0.0 139.4 jit_solution(2408311647329302666)
XLA Ops:
  0.6 0.0 copy-start
  0.6 0.0 copy-start.2
  0.7 0.0 copy-start.3
  0.7 0.0 copy-start.1
  0.7 0.9 copy.21
  1.6 1.0 bitcast_convert_fusion.1
  2.6 0.9 fusion
  3.5 0.1 concatenate.3
  3.6 8.8 %collective-permute-start = (f32[128,1408]{1,0:T(8,128)S(1)}, f32[128,1408]{1,0:T(8,128)S(1)}, u32[]{:S(2)}, u32[]{:S(2)}) collective-permute-start(f32[128,1408]{1,0:T(8,128)S(1)} %concatenate.3), channel_id=1, source_target_pairs={{0,1},{1,0},{2,3},{3,2},{4,5},{5,4},{6,7},{7,6},{8,9},{9,8},{10,11... | collective-permute-start | bytes 2162696 | tf_op jit(solution)/shard_map/ppermute | solution.py:193
  12.4 1.8 %collective-permute-done.refs_4_ = f32[128,1408]{1,0:T(8,128)S(1)} collective-permute-done((f32[128,1408]{1,0:T(8,128)S(1)}, f32[128,1408]{1,0:T(8,128)S(1)}, u32[]{:S(2)}, u32[]{:S(2)}) %collective-permute-start) | collective-permute-done | bytes 720928 | tf_op jit(solution)/shard_map/ppermute | solution.py:193
  14.2 0.0 copy-done
  14.2 0.0 copy-done.2
  14.2 0.0 copy-done.3
  14.2 0.0 copy-done.1
  14.2 1.0 shard_map.76
  15.2 0.0 copy-start.4
  15.3 0.7 copy-done.4
  16.0 24.8 %all_to_all.25.in_ref = f32[16,40,128]{2,1,0:T(8,128)S(1)} all-to-all(f32[16,40,128]{2,1,0:T(8,128)S(1)} %get-tuple-element.20), channel_id=1, replica_groups=mesh['dp'=16,'z'=16,'c'=2] {'z'}, dimensions={0} | all-to-all | bytes 655360 | tf_op jit(solution)/shard_map/all_to_all | solution.py:205
  40.8 0.0 copy-done.6
  40.8 0.8 shard_map.77
  41.5 11.6 %all-to-all-start.1 = ((f32[16,32,128]{2,1,0:T(8,128)}), f32[16,32,128]{2,1,0:T(8,128)S(1)}, u32[]{:S(2)}, u32[]{:S(2)}) async-start(f32[16,32,128]{2,1,0:T(8,128)} %shard_map.77), calls=%async_computation.1 | async-start | bytes 524288 | tf_op jit(solution)/shard_map/all_to_all | solution.py:209
  53.2 0.0 copy-start.7
  53.2 0.9 copy-done.7
  54.1 0.5 shard_map.78
  54.6 11.8 %all-to-all-done.1.refs_1_ = f32[16,32,128]{2,1,0:T(8,128)S(1)} async-done(((f32[16,32,128]{2,1,0:T(8,128)}), f32[16,32,128]{2,1,0:T(8,128)S(1)}, u32[]{:S(2)}, u32[]{:S(2)}) %all-to-all-start.1) | async-done | bytes 262176 | tf_op jit(solution)/shard_map/all_to_all | solution.py:209
  66.4 0.0 copy-done.5
  66.4 0.3 shard_map.79
  66.7 7.9 %collective-permute-start.2 = (f32[256,128]{1,0:T(8,128)S(1)}, f32[256,128]{1,0:T(8,128)S(1)}, u32[]{:S(2)}, u32[]{:S(2)}) collective-permute-start(f32[256,128]{1,0:T(8,128)S(1)} %get-tuple-element.36), channel_id=1, source_target_pairs={{0,1},{1,0},{2,3},{3,2},{4,5},{5,4},{6,7},{7,6},{8,9},{9,8},{10,11... | collective-permute-start | bytes 393224 | tf_op jit(solution)/shard_map/ppermute | solution.py:215
  74.6 0.2 copy.22
  74.8 0.2 reshape.45
  75.0 0.5 copy.23
  75.5 0.2 reshape.46.xt_ref
  75.7 0.0 collective-permute-done.2.pr_ref
  75.7 0.4 shard_map.81
  76.2 28.0 %all_to_all.26 = f32[16,64,384]{2,1,0:T(8,128)S(1)} all-to-all(f32[16,64,384]{2,1,0:T(8,128)S(1)} %bitcast.21), channel_id=1, replica_groups=mesh['dp'=16,'z'=16,'c'=2] {'dp'}, dimensions={0} | all-to-all | bytes 3145728 | tf_op jit(solution)/shard_map/all_to_all | solution.py:221
  104.2 0.1 reduce_sum.18
  104.3 0.7 reshape.48
  105.0 5.6 %all-to-all-start.3 = ((f32[16,4,384]{2,1,0:T(4,128)}), f32[16,4,384]{2,1,0:T(4,128)S(1)}, u32[]{:S(2)}, u32[]{:S(2)}) async-start(f32[16,4,384]{2,1,0:T(4,128)} %reshape.48), calls=%async_computation.3 | async-start | bytes 196608 | tf_op jit(solution)/shard_map/all_to_all | solution.py:223
  110.6 4.4 %collective-permute-start.1 = (f32[128,256]{1,0:T(8,128)S(1)}, f32[128,256]{1,0:T(8,128)S(1)}, u32[]{:S(2)}, u32[]{:S(2)}) collective-permute-start(f32[128,256]{1,0:T(8,128)S(1)} %get-tuple-element.32), channel_id=1, source_target_pairs={{0,1},{1,0},{2,3},{3,2},{4,5},{5,4},{6,7},{7,6},{8,9},{9,8},{10,11... | collective-permute-start | bytes 393224 | tf_op jit(solution)/shard_map/ppermute | solution.py:216
  115.0 7.5 %all-to-all-done.3 = f32[16,4,384]{2,1,0:T(4,128)S(1)} async-done(((f32[16,4,384]{2,1,0:T(4,128)}), f32[16,4,384]{2,1,0:T(4,128)S(1)}, u32[]{:S(2)}, u32[]{:S(2)}) %all-to-all-start.3) | async-done | bytes 98336 | tf_op jit(solution)/shard_map/all_to_all | solution.py:223
  122.5 0.7 broadcast_in_dim.13
  123.2 7.4 %all-to-all-start.4 = ((f32[32,2,384]{2,1,0:T(2,128)}), f32[32,2,384]{2,1,0:T(2,128)S(1)}, u32[]{:S(2)}, u32[]{:S(2)}) async-start(f32[32,2,384]{2,1,0:T(2,128)} %bitcast.8), calls=%async_computation.4 | async-start | bytes 196608 | tf_op jit(solution)/shard_map/all_to_all | solution.py:226
  130.6 0.0 collective-permute-done.1.yr_ref
  130.6 0.7 shard_map.80
  131.3 6.8 %all-to-all-done.4 = f32[32,2,384]{2,1,0:T(2,128)S(1)} async-done(((f32[32,2,384]{2,1,0:T(2,128)}), f32[32,2,384]{2,1,0:T(2,128)S(1)}, u32[]{:S(2)}, u32[]{:S(2)}) %all-to-all-start.4) | async-done | bytes 98336 | tf_op jit(solution)/shard_map/all_to_all | solution.py:226
  138.0 0.1 copy.25
  138.1 0.6 copy.27
  138.8 0.6 copy.30
  (9 shorter events, 0.1 us)
Async XLA Ops:
  0.6 13.6 %copy-start = (bf16[1,128,1024]{2,1,0:T(8,128)(2,1)S(1)}, bf16[1,128,1024]{2,1,0:T(8,128)(2,1)}, u32[]{:S(2)}) copy-start(bf16[1,128,1024]{2,1,0:T(8,128)(2,1)} %param.5) | copy-start | bytes 786436
  0.6 13.6 %copy-start.2 = (bf16[1,128,512]{2,1,0:T(8,128)(2,1)S(1)}, bf16[1,128,512]{2,1,0:T(8,128)(2,1)}, u32[]{:S(2)}) copy-start(bf16[1,128,512]{2,1,0:T(8,128)(2,1)} %param.9) | copy-start | bytes 393220
  0.7 13.6 %copy-start.3 = (bf16[1024,256]{1,0:T(8,128)(2,1)S(1)}, bf16[1024,256]{1,0:T(8,128)(2,1)}, u32[]{:S(2)}) copy-start(bf16[1024,256]{1,0:T(8,128)(2,1)} %refs_6_.1) | copy-start | bytes 1572868
  0.7 13.6 %copy-start.1 = (bf16[1024,512]{1,0:T(8,128)(2,1)S(1)}, bf16[1024,512]{1,0:T(8,128)(2,1)}, u32[]{:S(2)}) copy-start(bf16[1024,512]{1,0:T(8,128)(2,1)} %refs_5_.1) | copy-start | bytes 3145732
  3.6 10.6 %collective-permute-start = (f32[128,1408]{1,0:T(8,128)S(1)}, f32[128,1408]{1,0:T(8,128)S(1)}, u32[]{:S(2)}, u32[]{:S(2)}) collective-permute-start(f32[128,1408]{1,0:T(8,128)S(1)} %concatenate.3), channel_id=1, source_target_pairs={{0,1},{1,0},{2,3},{3,2},{4,5},{5,4},{6,7},{7,6},{8,9},{9,8},{10,11... | collective-permute-start | bytes 2162696 | tf_op jit(solution)/shard_map/ppermute | solution.py:193
  15.2 0.7 copy-start.4
  15.9 24.8 %copy-start.6 = (bf16[256,256]{1,0:T(8,128)(2,1)}, bf16[256,256]{1,0:T(8,128)(2,1)S(1)}, u32[]{:S(2)}) copy-start(bf16[256,256]{1,0:T(8,128)(2,1)S(1)} %get-tuple-element.27.u_ref) | copy-start | bytes 393220
  15.9 50.4 %copy-start.5 = (f32[256,256]{1,0:T(8,128)S(1)}, f32[256,256]{1,0:T(8,128)}, u32[]{:S(2)}) copy-start(f32[256,256]{1,0:T(8,128)} %copy-done.4) | copy-start | bytes 786436
  41.5 24.9 %all-to-all-start.1 = ((f32[16,32,128]{2,1,0:T(8,128)}), f32[16,32,128]{2,1,0:T(8,128)S(1)}, u32[]{:S(2)}, u32[]{:S(2)}) async-start(f32[16,32,128]{2,1,0:T(8,128)} %shard_map.77), calls=%async_computation.1 | async-start | bytes 524288 | tf_op jit(solution)/shard_map/all_to_all | solution.py:209
  53.2 0.9 copy-start.7
  66.7 9.0 %collective-permute-start.2 = (f32[256,128]{1,0:T(8,128)S(1)}, f32[256,128]{1,0:T(8,128)S(1)}, u32[]{:S(2)}, u32[]{:S(2)}) collective-permute-start(f32[256,128]{1,0:T(8,128)S(1)} %get-tuple-element.36), channel_id=1, source_target_pairs={{0,1},{1,0},{2,3},{3,2},{4,5},{5,4},{6,7},{7,6},{8,9},{9,8},{10,11... | collective-permute-start | bytes 393224 | tf_op jit(solution)/shard_map/ppermute | solution.py:215
  105.0 17.5 %all-to-all-start.3 = ((f32[16,4,384]{2,1,0:T(4,128)}), f32[16,4,384]{2,1,0:T(4,128)S(1)}, u32[]{:S(2)}, u32[]{:S(2)}) async-start(f32[16,4,384]{2,1,0:T(4,128)} %reshape.48), calls=%async_computation.3 | async-start | bytes 196608 | tf_op jit(solution)/shard_map/all_to_all | solution.py:223
  110.6 20.0 %collective-permute-start.1 = (f32[128,256]{1,0:T(8,128)S(1)}, f32[128,256]{1,0:T(8,128)S(1)}, u32[]{:S(2)}, u32[]{:S(2)}) collective-permute-start(f32[128,256]{1,0:T(8,128)S(1)} %get-tuple-element.32), channel_id=1, source_target_pairs={{0,1},{1,0},{2,3},{3,2},{4,5},{5,4},{6,7},{7,6},{8,9},{9,8},{10,11... | collective-permute-start | bytes 393224 | tf_op jit(solution)/shard_map/ppermute | solution.py:216
  123.2 14.9 %all-to-all-start.4 = ((f32[32,2,384]{2,1,0:T(2,128)}), f32[32,2,384]{2,1,0:T(2,128)S(1)}, u32[]{:S(2)}, u32[]{:S(2)}) async-start(f32[32,2,384]{2,1,0:T(2,128)} %bitcast.8), calls=%async_computation.4 | async-start | bytes 196608 | tf_op jit(solution)/shard_map/all_to_all | solution.py:226

commit v2 on v1

v2 whole, which is shorter than its diff:
```python
import jax
import jax.numpy as jnp
from jax import lax
from jax.experimental import pallas as pl
from jax.experimental.pallas import tpu as pltpu
from jax.sharding import Mesh, PartitionSpec as P

f32 = jnp.float32
bf16 = jnp.bfloat16

LD = 128
CHIP = 2 * LD
HEADS = 8
HEAD = 64
STATE = 128
HALF = HEADS * HEAD // 2
ZN = 16
DP = 16
ROWS = HALF // ZN
PAY = 2 * ROWS + 8


def mm(a, b):
    return jnp.dot(a, b, preferred_element_type=f32)


def mm_tn(a, b):
    return lax.dot_general(a, b, (((0,), (0,)), ((), ())), preferred_element_type=f32)


def mm_nt(a, b):
    return lax.dot_general(a, b, (((1,), (1,)), ((), ())), preferred_element_type=f32)


def causal(shape):
    return lax.broadcasted_iota(jnp.int32, shape, 0) >= lax.broadcasted_iota(jnp.int32, shape, 1)


def pack_kernel(x_ref, g_ref, codes_ref, out_ref):
    d = x_ref.shape[1]
    out_ref[:, :d] = x_ref[...].astype(f32)
    out_ref[:, d:d + HALF] = g_ref[...].astype(f32)
    out_ref[:, d + HALF:] = jnp.zeros((LD, LD), f32)
    out_ref[0:HEADS, d + HALF:] = codes_ref[...].astype(f32)


def own_kernel(x_ref, g_ref, codes_ref, wx_ref, wbc_ref,
               mix_ref, proj_ref, g_out_ref, codes_out_ref, x_out_ref, wx_out_ref, wbc_out_ref):
    x = x_ref[...]
    wx = wx_ref[...]
    wbc = wbc_ref[...]
    mix_ref[...] = mm(x, wx).astype(bf16)
    proj_ref[...] = mm(x, wbc).astype(bf16)
    g_out_ref[...] = g_ref[...]
    codes_out_ref[...] = codes_ref[...].astype(f32)
    x_out_ref[...] = x
    wx_out_ref[...] = wx
    wbc_out_ref[...] = wbc


def local_kernel(unit, c_ref, mix_ref, pj_ref, g_ref, codes_ref, x_ref, wx_ref, wbc_ref, pack_ref,
                 pay_ref, ue_ref, v_ref, en_ref, te_ref, proj_ref, xc_ref, yl_ref, gm_ref, gp_ref,
                 gs_ref, cs_ref, ms_ref):
    c = c_ref[0]
    own = pl.multiple_of(c * LD, LD)
    oth = pl.multiple_of((1 - c) * LD, LD)
    d = x_ref.shape[1]
    xo = pack_ref[:, :d].astype(bf16)
    xc_ref[pl.ds(own, LD), :] = x_ref[...]
    xc_ref[pl.ds(oth, LD), :] = xo
    gs_ref[pl.ds(own, LD), :] = g_ref[...].astype(f32)
    gs_ref[pl.ds(oth, LD), :] = pack_ref[:, d:d + HALF]
    cs_ref[:, pl.ds(own, LD)] = codes_ref[...]
    cs_ref[:, pl.ds(oth, LD)] = pack_ref[0:HEADS, d + HALF:]
    ms_ref[pl.ds(own, LD), :] = mix_ref[...]
    ms_ref[pl.ds(oth, LD), :] = mm(xo, wx_ref[...]).astype(bf16)
    proj_ref[pl.ds(own, LD), :] = pj_ref[...]
    proj_ref[pl.ds(oth, LD), :] = mm(xo, wbc_ref[...]).astype(bf16)
    codes = cs_ref[...]
    hi = jnp.floor(codes * (1.0 / 32.0))
    lo = codes - 32.0 * hi
    row = lax.broadcasted_iota(jnp.int32, (HEADS, HALF), 0)
    col = lax.broadcasted_iota(jnp.int32, (HEADS, HALF), 1)
    spread = jnp.where(row == col // HEAD + c * (HEADS // 2), 1.0, 0.0).astype(bf16)
    hi = mm_tn(hi.astype(bf16), spread).astype(bf16)
    lo = mm_tn(lo.astype(bf16), spread).astype(bf16)
    mask = causal((CHIP, CHIP))
    tri = jnp.where(mask, 1.0, 0.0).astype(bf16)
    running = unit * (32.0 * mm(tri, hi) + mm(tri, lo))
    last = running[CHIP - 1:CHIP, :]
    en = jnp.exp(-running)
    ep = jnp.exp(running)
    te = jnp.exp(running - last)
    en_ref[...] = en
    te_ref[...] = te
    mixer = ms_ref[...].astype(f32)
    inject = proj_ref[:, :STATE]
    readout = proj_ref[:, STATE:]
    v = (en * gs_ref[...]).astype(bf16)
    ue = (te * mixer).astype(bf16)
    u = (ep * mixer).astype(bf16)
    ue_ref[...] = ue
    v_ref[...] = v
    state = mm_tn(ue, inject)
    adjoint = mm_tn(v, readout)
    pay_ref[:, 0:ROWS, :] = state.reshape(ZN, ROWS, STATE)
    pay_ref[:, ROWS:2 * ROWS, :] = adjoint.reshape(ZN, ROWS, STATE)
    per = ZN // (HEADS // 2)
    for h in range(HEADS // 2):
        total = jnp.broadcast_to(last[:, h * HEAD:h * HEAD + 1], (8, STATE))
        for k in range(per):
            pay_ref[h * per + k, 2 * ROWS:, :] = total
    scores = jnp.where(mask, mm_nt(readout, inject), 0.0).astype(bf16)
    pairs = jnp.where(mask, mm_nt(v, u), 0.0).astype(bf16)
    yl_ref[...] = en * mm(scores, u)
    gm_ref[...] = ep * mm_tn(scores, v)
    gp_ref[:, :STATE] = mm_tn(pairs, readout)
    gp_ref[:, STATE:] = mm(pairs, inject)


def scan_kernel(in_ref, out_ref):
    decay = [jnp.exp(-in_ref[k, 2 * ROWS:2 * ROWS + 1, :]) for k in range(ZN)]
    carry = jnp.zeros((ROWS, STATE), f32)
    for k in range(ZN):
        out_ref[k, 0:ROWS, :] = carry
        if k + 1 < ZN:
            carry = decay[k] * carry + in_ref[k, 0:ROWS, :]
    carry = jnp.zeros((ROWS, STATE), f32)
    for k in reversed(range(ZN)):
        out_ref[k, ROWS:, :] = carry
        if k:
            carry = decay[k] * carry + in_ref[k, ROWS:2 * ROWS, :]


def outer_kernel(scale, c_ref, in_ref, u_ref, v_ref, en_ref, te_ref, proj_ref,
                 yl_ref, gml_ref, gp_ref, gm_ref, pk_ref, ps_ref, yk_ref, ys_ref, y_ref):
    c = c_ref[0]
    carry = in_ref[:, 0:ROWS, :].reshape(HALF, STATE).astype(bf16)
    adjoint = in_ref[:, ROWS:, :].reshape(HALF, STATE).astype(bf16)
    inject = proj_ref[:, :STATE]
    readout = proj_ref[:, STATE:]
    gi = scale * (gp_ref[:, :STATE] + mm(u_ref[...], adjoint))
    gr = scale * (gp_ref[:, STATE:] + mm(v_ref[...], carry))
    pk_ref[...] = jnp.where(c == 0, gi, gr)
    ps_ref[...] = jnp.where(c == 0, gr, gi)
    grad = gml_ref[...] + te_ref[...] * mm_nt(inject, adjoint)
    gm_ref[...] = (scale * grad).astype(bf16)
    y_ref[...] = yl_ref[...] + en_ref[...] * mm_nt(readout, carry)
    yk_ref[...] = y_ref[pl.ds(pl.multiple_of(c * LD, LD), LD), :]
    ys_ref[...] = y_ref[pl.ds(pl.multiple_of((1 - c) * LD, LD), LD), :]


def fold_kernel(in_ref, out_ref):
    total = jnp.sum(in_ref[...], axis=0)
    step = out_ref.shape[1]
    for k in range(ZN):
        out_ref[k] = total[k * step:(k + 1) * step, :]


def spread_kernel(scale, in_ref, out_ref):
    total = scale * jnp.sum(in_ref[...], axis=0)
    for k in range(2 * DP):
        half = k % 2
        out_ref[k] = total[2 * half:2 * half + 2, :]


def place_kernel(in_ref, x_ref, bc_ref):
    for k in range(DP):
        for half in range(2):
            piece = in_ref[2 * k + half]
            x_ref[2 * k:2 * k + 2, half * HALF:(half + 1) * HALF] = piece[:, :HALF]
            bc_ref[2 * k:2 * k + 2, half * STATE:(half + 1) * STATE] = piece[:, HALF:]


def weight_kernel(xt_ref, gm_ref, pk_ref, pr_ref, out_ref):
    xt = xt_ref[...]
    out_ref[:, :HALF] = mm(xt, gm_ref[...])
    out_ref[:, HALF:] = mm(xt, (pk_ref[...] + pr_ref[...]).astype(bf16))


def join_kernel(c_ref, yk_ref, yr_ref, out_ref):
    c = c_ref[0]
    yk = yk_ref[...].astype(bf16)
    yr = yr_ref[...].astype(bf16)

    @pl.when(c == 0)
    def _():
        out_ref[:, :HALF] = yk
        out_ref[:, HALF:] = yr

    @pl.when(c != 0)
    def _():
        out_ref[:, :HALF] = yr
        out_ref[:, HALF:] = yk


def whole(shape):
    return pl.BlockSpec(shape, lambda i, c: (0,) * len(shape))


def call(kernel, outs, ins, scratch=(), c=None, specs=None):
    params = pltpu.CompilerParams(vmem_limit_bytes=16 * 1024 * 1024)
    shapes = [jax.ShapeDtypeStruct(s, d) for s, d in outs]
    if c is None:
        return pl.pallas_call(kernel, out_shape=shapes, compiler_params=params)(*ins)
    specs = specs or [whole(a.shape) for a in ins]
    return pl.pallas_call(
        kernel,
        out_shape=shapes,
        grid_spec=pltpu.PrefetchScalarGridSpec(
            num_scalar_prefetch=1, grid=(1,), in_specs=specs,
            out_specs=[whole(s) for s, _ in outs], scratch_shapes=list(scratch)),
        compiler_params=params,
    )(c, *ins)


def body(records, x_weight, bc_weight, decay_codes, out_grad):
    x = records[0]
    g = out_grad[0]
    codes = decay_codes[0]
    d = x.shape[1]
    frames = LD * 2 * ZN
    unit = 1.0 / (32.0 * frames)
    out_scale = float((STATE * frames) ** -0.5)
    grad_scale = float((DP * frames) ** -0.5)
    core = lax.axis_index("c")
    c = core.astype(jnp.int32).reshape(1)
    swap = [(0, 1), (1, 0)]

    codes = codes.T
    here = pl.BlockSpec((LD, HALF), lambda i, c: (0, c[0]))
    there = pl.BlockSpec((LD, HALF), lambda i, c: (0, 1 - c[0]))
    x, g, codes, wx, wbc = (
        pltpu.with_memory_space_constraint(a, pltpu.MemorySpace.HBM)
        for a in (x, g, codes, x_weight, bc_weight))
    (pack,) = call(
        lambda c_ref, *refs: pack_kernel(*refs), [((LD, d + HALF + LD), f32)], (x, g, codes), (), c,
        [whole(x.shape), there, whole(codes.shape)])
    pack = lax.ppermute(pack, "c", swap)
    half = (LD, HALF)
    owned = call(
        lambda c_ref, *refs: own_kernel(*refs),
        [(half, bf16), ((LD, 2 * STATE), bf16), (half, bf16), ((HEADS, LD), f32), ((LD, d), bf16),
         ((d, HALF), bf16), ((d, 2 * STATE), bf16)],
        (x, g, codes, wx, wbc), (), c,
        [whole(x.shape), here, whole(codes.shape), pl.BlockSpec((d, HALF), lambda i, c: (0, c[0])),
         whole(wbc.shape)])

    sq = (CHIP, HALF)
    pay, ue, v, en, te, proj, xc, yl, gml, gpl = call(
        lambda *refs: local_kernel(unit, *refs),
        [((ZN, PAY, STATE), f32), (sq, bf16), (sq, bf16), (sq, f32), (sq, f32), ((CHIP, 2 * STATE), bf16),
         ((CHIP, d), bf16), (sq, f32), (sq, f32), ((CHIP, 2 * STATE), f32)],
        (*owned, pack), [pltpu.VMEM(sq, f32), pltpu.VMEM((HEADS, CHIP), f32), pltpu.VMEM(sq, bf16)], c)

    pay = lax.all_to_all(pay, "z", 0, 0, tiled=True)
    (pay,) = call(scan_kernel, [((ZN, 2 * ROWS, STATE), f32)], (pay,))
    pay = lax.all_to_all(pay, "z", 0, 0, tiled=True)

    gm, pk, ps, yk, ys = call(
        lambda *refs: outer_kernel(out_scale, *refs),
        [(sq, bf16), ((CHIP, STATE), f32), ((CHIP, STATE), f32), ((LD, HALF), f32), ((LD, HALF), f32)],
        (pay, ue, v, en, te, proj, yl, gml, gpl), [pltpu.VMEM(sq, f32)], c)
    pr = lax.ppermute(ps, "c", swap)
    yr = lax.ppermute(ys, "c", swap)
    xt = xc.T.reshape(ZN, 2, DP, 2, CHIP).transpose(2, 0, 1, 3, 4).reshape(d, CHIP)
    width = HALF + STATE
    (grad,) = call(weight_kernel, [((d, width), f32)], (xt, gm, pk, pr))
    (y,) = call(join_kernel, [((LD, 2 * HALF), bf16)], (yk, yr), (), c)

    part = lax.all_to_all(grad.reshape(DP, d // DP, width), "dp", 0, 0, tiled=True)
    (part,) = call(fold_kernel, [((ZN, d // DP // ZN, width), f32)], (part,))
    part = lax.all_to_all(part, "z", 0, 0, tiled=True)
    (part,) = call(lambda *refs: spread_kernel(grad_scale, *refs), [((2 * DP, 2, width), f32)], (part,))
    part = lax.all_to_all(part, ("dp", "c"), 0, 0, tiled=True)
    x_grad, bc_grad = call(place_kernel, [((2 * DP, 2 * HALF), f32), ((2 * DP, 2 * STATE), f32)], (part,))
    return y[None], x_grad, bc_grad


def solution(mesh):
    mesh = Mesh(mesh.devices.reshape(DP, ZN, 2), ("dp", "z", "c"))
    frames = P("dp", ("z", "c"), None)
    rows = P(("z", "c"), None)
    return jax.shard_map(
        body,
        mesh=mesh,
        in_specs=(frames, P(), P(), frames, frames),
        out_specs=(frames, rows, rows),
        check_vma=False,
    )
```

time: 140 us -> 136 us (0.971)
  blocking collectives: 52.9 us -> 77.4 us
  waiting for transfers between devices: 27.8 us -> 14.3 us
  starting transfers between devices: 45.8 us -> 34.1 us
  local copies, waits for them, and re-layouts: 6.41 us -> 1.08 us
  Pallas kernels: 3.72 us -> 7.59 us
  other arithmetic: 2.01 us -> 0 us
    all_to_all x1 -> x2, blocking collectives: 24.8 us -> 49.4 us  [body(): pay = lax.all_to_all(pay, 'z', 0, 0, tiled=True)]
    all_to_all x1 -> x0, waiting for transfers between devices: 11.8 us -> none  [body(): pay = lax.all_to_all(pay, 'z', 0, 0, tiled=True)]
    all_to_all x1 -> x0, starting transfers between devices: 11.6 us -> none  [body(): pay = lax.all_to_all(pay, 'z', 0, 0, tiled=True)]
    unnamed x19 -> x0, local copies, waits for them, and re-layouts: 3.8 us -> none
    pallas_call x3 -> x5, Pallas kernels: 2.01 us -> 5.03 us  [call(): pl.pallas_call(kernel, out_shape=shapes, grid_spec=pltpu.PrefetchScalarGr...]
    convert_element_type x3 -> x0, other arithmetic: 1.89 us -> none  [the longest x1 0.99 us: body(): x.astype(f32)]
    ppermute x1, waiting for transfers between devices: 1.8 us -> 0.07 us  [body(): pack = lax.ppermute(pack, 'c', swap)]
  transfers between devices with their start and end apart: 6 -> 5, of which waited for: 4 -> 3; matrix products, arithmetic and copies ran while one was open for 1% -> 1% of each run, Pallas kernels for 1% -> 2%
where the time goes in v2:
time: 136 us; the launch traced here: 135 us
  blocking collectives  77.4 us (57%)
  starting transfers between devices  34.1 us (25%)
  waiting for transfers between devices  14.3 us (11%)
  Pallas kernels  7.59 us (6%)
    all_to_all x2, blocking collectives, body(): pay = lax.all_to_all(pay, 'z', 0, 0, tiled=True)  49.4 us
    all_to_all x1, blocking collectives, body(): lax.all_to_all(grad.reshape(DP, d // DP, width), 'dp', 0, 0, tiled=True)  28 us
    ppermute x1, starting transfers between devices, body(): pack = lax.ppermute(pack, 'c', swap)  8.79 us
    ppermute x1, starting transfers between devices, body(): pr = lax.ppermute(ps, 'c', swap)  7.87 us
    all_to_all x1, waiting for transfers between devices, body(): part = lax.all_to_all(part, 'z', 0, 0, tiled=True)  7.46 us
    all_to_all x1, starting transfers between devices, body(): part = lax.all_to_all(part, ('dp', 'c'), 0, 0, tiled=True)  7.4 us
    all_to_all x1, waiting for transfers between devices, body(): part = lax.all_to_all(part, ('dp', 'c'), 0, 0, tiled=True)  6.76 us
    all_to_all x1, starting transfers between devices, body(): part = lax.all_to_all(part, 'z', 0, 0, tiled=True)  5.63 us
  transfers between devices with their start and end apart: 5, of which 3 were waited for; matrix products, arithmetic and copies ran while one was open for 1% of the time, Pallas kernels for 2%

profile of v2, /device:TPU:1, one launch (start us, length us, event | category | flops | bytes accessed | tf_op | source)
XLA Modules:
  0.0 135.2 jit_solution(12805265742502417715)
XLA Ops:
  0.6 1.0 shard_map.77
  1.7 8.8 %collective-permute-start = (f32[128,1408]{1,0:T(8,128)S(1)}, f32[128,1408]{1,0:T(8,128)S(1)}, u32[]{:S(2)}, u32[]{:S(2)}) collective-permute-start(f32[128,1408]{1,0:T(8,128)S(1)} %shard_map.77), channel_id=1, source_target_pairs={{0,1},{1,0},{2,3},{3,2},{4,5},{5,4},{6,7},{7,6},{8,9},{9,8},{10,11... | collective-permute-start | bytes 2162696 | tf_op jit(solution)/shard_map/ppermute | solution.py:239
  10.5 1.7 %shard_map.76 = (bf16[128,256]{1,0:T(8,128)(2,1)S(1)}, bf16[128,256]{1,0:T(8,128)(2,1)S(1)}, bf16[128,256]{1,0:T(8,128)(2,1)S(1)}, f32[8,128]{1,0:T(8,128)S(1)},...) custom-call(s32[1]{0:T(128)} %bitcast.c_ref.refs_0_, ...), custom_call_target="tpu_custom_call" | custom-call | tf_op jit(solution)/shard_map/pallas_call | solution.py:207
  12.2 0.1 collective-permute-done.refs_8_
  12.3 1.3 shard_map.78
  13.6 24.8 %all_to_all.25.in_ref = f32[16,40,128]{2,1,0:T(8,128)S(1)} all-to-all(f32[16,40,128]{2,1,0:T(8,128)S(1)} %get-tuple-element.34), channel_id=1, replica_groups=mesh['dp'=16,'z'=16,'c'=2] {'z'}, dimensions={0} | all-to-all | bytes 655360 | tf_op jit(solution)/shard_map/all_to_all | solution.py:256
  38.3 0.1 shard_map.79
  38.4 24.6 %all_to_all.26.refs_1_ = f32[16,32,128]{2,1,0:T(8,128)S(1)} all-to-all(f32[16,32,128]{2,1,0:T(8,128)S(1)} %shard_map.79), channel_id=1, replica_groups=mesh['dp'=16,'z'=16,'c'=2] {'z'}, dimensions={0} | all-to-all | bytes 524288 | tf_op jit(solution)/shard_map/all_to_all | solution.py:258
  63.0 0.3 shard_map.80
  63.3 7.9 %collective-permute-start.2 = (f32[256,128]{1,0:T(8,128)S(1)}, f32[256,128]{1,0:T(8,128)S(1)}, u32[]{:S(2)}, u32[]{:S(2)}) collective-permute-start(f32[256,128]{1,0:T(8,128)S(1)} %get-tuple-element.48), channel_id=1, source_target_pairs={{0,1},{1,0},{2,3},{3,2},{4,5},{5,4},{6,7},{7,6},{8,9},{9,8},{10,11... | collective-permute-start | bytes 393224 | tf_op jit(solution)/shard_map/ppermute | solution.py:264
  71.2 0.2 copy.9
  71.4 0.2 reshape.19
  71.6 0.5 copy.10
  72.1 0.2 reshape.20.xt_ref
  72.3 0.0 collective-permute-done.2.pr_ref
  72.3 0.4 shard_map.82
  72.8 28.0 %all_to_all.27.in_ref = f32[16,64,384]{2,1,0:T(8,128)S(1)} all-to-all(f32[16,64,384]{2,1,0:T(8,128)S(1)} %bitcast.10), channel_id=1, replica_groups=mesh['dp'=16,'z'=16,'c'=2] {'dp'}, dimensions={0} | all-to-all | bytes 3145728 | tf_op jit(solution)/shard_map/all_to_all | solution.py:271
  100.8 0.7 shard_map.83
  101.5 5.6 %all-to-all-start.3 = ((f32[16,4,384]{2,1,0:T(4,128)}), f32[16,4,384]{2,1,0:T(4,128)S(1)}, u32[]{:S(2)}, u32[]{:S(2)}) async-start(f32[16,4,384]{2,1,0:T(4,128)} %shard_map.83), calls=%async_computation.3 | async-start | bytes 196608 | tf_op jit(solution)/shard_map/all_to_all | solution.py:273
  107.1 4.4 %collective-permute-start.1 = (f32[128,256]{1,0:T(8,128)S(1)}, f32[128,256]{1,0:T(8,128)S(1)}, u32[]{:S(2)}, u32[]{:S(2)}) collective-permute-start(f32[128,256]{1,0:T(8,128)S(1)} %get-tuple-element.44), channel_id=1, source_target_pairs={{0,1},{1,0},{2,3},{3,2},{4,5},{5,4},{6,7},{7,6},{8,9},{9,8},{10,11... | collective-permute-start | bytes 393224 | tf_op jit(solution)/shard_map/ppermute | solution.py:265
  111.5 7.5 %all-to-all-done.3.refs_0_ = f32[16,4,384]{2,1,0:T(4,128)S(1)} async-done(((f32[16,4,384]{2,1,0:T(4,128)}), f32[16,4,384]{2,1,0:T(4,128)S(1)}, u32[]{:S(2)}, u32[]{:S(2)}) %all-to-all-start.3) | async-done | bytes 98336 | tf_op jit(solution)/shard_map/all_to_all | solution.py:273
  119.0 0.7 shard_map.84
  119.7 7.4 %all-to-all-start.4 = ((f32[32,2,384]{2,1,0:T(2,128)}), f32[32,2,384]{2,1,0:T(2,128)S(1)}, u32[]{:S(2)}, u32[]{:S(2)}) async-start(f32[32,2,384]{2,1,0:T(2,128)} %shard_map.84), calls=%async_computation.4 | async-start | bytes 196608 | tf_op jit(solution)/shard_map/all_to_all | solution.py:275
  127.1 0.0 collective-permute-done.1.yr_ref
  127.1 0.7 shard_map.81
  127.8 6.8 %all-to-all-done.4.in_ref = f32[32,2,384]{2,1,0:T(2,128)S(1)} async-done(((f32[32,2,384]{2,1,0:T(2,128)}), f32[32,2,384]{2,1,0:T(2,128)S(1)}, u32[]{:S(2)}, u32[]{:S(2)}) %all-to-all-start.4) | async-done | bytes 98336 | tf_op jit(solution)/shard_map/all_to_all | solution.py:275
  134.5 0.7 shard_map.85
Async XLA Ops:
  1.7 10.6 %collective-permute-start = (f32[128,1408]{1,0:T(8,128)S(1)}, f32[128,1408]{1,0:T(8,128)S(1)}, u32[]{:S(2)}, u32[]{:S(2)}) collective-permute-start(f32[128,1408]{1,0:T(8,128)S(1)} %shard_map.77), channel_id=1, source_target_pairs={{0,1},{1,0},{2,3},{3,2},{4,5},{5,4},{6,7},{7,6},{8,9},{9,8},{10,11... | collective-permute-start | bytes 2162696 | tf_op jit(solution)/shard_map/ppermute | solution.py:239
  63.3 9.0 %collective-permute-start.2 = (f32[256,128]{1,0:T(8,128)S(1)}, f32[256,128]{1,0:T(8,128)S(1)}, u32[]{:S(2)}, u32[]{:S(2)}) collective-permute-start(f32[256,128]{1,0:T(8,128)S(1)} %get-tuple-element.48), channel_id=1, source_target_pairs={{0,1},{1,0},{2,3},{3,2},{4,5},{5,4},{6,7},{7,6},{8,9},{9,8},{10,11... | collective-permute-start | bytes 393224 | tf_op jit(solution)/shard_map/ppermute | solution.py:264
  101.5 17.5 %all-to-all-start.3 = ((f32[16,4,384]{2,1,0:T(4,128)}), f32[16,4,384]{2,1,0:T(4,128)S(1)}, u32[]{:S(2)}, u32[]{:S(2)}) async-start(f32[16,4,384]{2,1,0:T(4,128)} %shard_map.83), calls=%async_computation.3 | async-start | bytes 196608 | tf_op jit(solution)/shard_map/all_to_all | solution.py:273
  107.1 19.9 %collective-permute-start.1 = (f32[128,256]{1,0:T(8,128)S(1)}, f32[128,256]{1,0:T(8,128)S(1)}, u32[]{:S(2)}, u32[]{:S(2)}) collective-permute-start(f32[128,256]{1,0:T(8,128)S(1)} %get-tuple-element.44), channel_id=1, source_target_pairs={{0,1},{1,0},{2,3},{3,2},{4,5},{5,4},{6,7},{7,6},{8,9},{9,8},{10,11... | collective-permute-start | bytes 393224 | tf_op jit(solution)/shard_map/ppermute | solution.py:265
  119.7 14.9 %all-to-all-start.4 = ((f32[32,2,384]{2,1,0:T(2,128)}), f32[32,2,384]{2,1,0:T(2,128)S(1)}, u32[]{:S(2)}, u32[]{:S(2)}) async-start(f32[32,2,384]{2,1,0:T(2,128)} %shard_map.84), calls=%async_computation.4 | async-start | bytes 196608 | tf_op jit(solution)/shard_map/all_to_all | solution.py:275

commit v3 on v2

--- a/solution.py
+++ b/solution.py
@@ -16,8 +16,8 @@
 HALF = HEADS * HEAD // 2
 ZN = 16
 DP = 16
-ROWS = HALF // ZN
-PAY = 2 * ROWS + 8
+GROUP = 4
+GROUPS = ZN // GROUP
 
 
 def mm(a, b):
@@ -103,13 +103,10 @@
     v_ref[...] = v
     state = mm_tn(ue, inject)
     adjoint = mm_tn(v, readout)
-    pay_ref[:, 0:ROWS, :] = state.reshape(ZN, ROWS, STATE)
-    pay_ref[:, ROWS:2 * ROWS, :] = adjoint.reshape(ZN, ROWS, STATE)
-    per = ZN // (HEADS // 2)
-    for h in range(HEADS // 2):
-        total = jnp.broadcast_to(last[:, h * HEAD:h * HEAD + 1], (8, STATE))
-        for k in range(per):
-            pay_ref[h * per + k, 2 * ROWS:, :] = total
+    for h in range(GROUP):
+        pay_ref[h, 0:HEAD, :] = state[h * HEAD:(h + 1) * HEAD, :]
+        pay_ref[h, HEAD:2 * HEAD, :] = adjoint[h * HEAD:(h + 1) * HEAD, :]
+        pay_ref[h, 2 * HEAD:, :] = jnp.broadcast_to(last[:, h * HEAD:h * HEAD + 1], (8, STATE))
     scores = jnp.where(mask, mm_nt(readout, inject), 0.0).astype(bf16)
     pairs = jnp.where(mask, mm_nt(v, u), 0.0).astype(bf16)
     yl_ref[...] = en * mm(scores, u)
@@ -118,36 +115,60 @@
     gp_ref[:, STATE:] = mm(pairs, inject)
 
 
-def scan_kernel(in_ref, out_ref):
-    decay = [jnp.exp(-in_ref[k, 2 * ROWS:2 * ROWS + 1, :]) for k in range(ZN)]
-    carry = jnp.zeros((ROWS, STATE), f32)
-    for k in range(ZN):
-        out_ref[k, 0:ROWS, :] = carry
-        if k + 1 < ZN:
-            carry = decay[k] * carry + in_ref[k, 0:ROWS, :]
-    carry = jnp.zeros((ROWS, STATE), f32)
-    for k in reversed(range(ZN)):
-        out_ref[k, ROWS:, :] = carry
+def total_kernel(c_ref, in_ref, out_ref):
+    group = c_ref[0]
+    logs = [in_ref[k, 2 * HEAD:, :] for k in range(GROUP)]
+    decay = [jnp.exp(-a[0:1, :]) for a in logs]
+    state = in_ref[0, 0:HEAD, :]
+    for k in range(1, GROUP):
+        state = decay[k] * state + in_ref[k, 0:HEAD, :]
+    adjoint = in_ref[GROUP - 1, HEAD:2 * HEAD, :]
+    for k in reversed(range(GROUP - 1)):
+        adjoint = decay[k] * adjoint + in_ref[k, HEAD:2 * HEAD, :]
+    total = logs[0] + logs[1] + logs[2] + logs[3]
+    for k in range(GROUPS):
+        out_ref[k, 0:HEAD, :] = jnp.where(k > group, state, adjoint)
+        out_ref[k, HEAD:, :] = total
+
+
+def prefix_kernel(c_ref, in_ref, far_ref, out_ref):
+    group = c_ref[0]
+    far = [jnp.exp(-far_ref[k, HEAD:HEAD + 1, :]) for k in range(GROUPS)]
+    decay = [jnp.exp(-in_ref[k, 2 * HEAD:2 * HEAD + 1, :]) for k in range(GROUP)]
+    carry = jnp.zeros((HEAD, STATE), f32)
+    for k in range(GROUPS - 1):
+        carry = jnp.where(k < group, far[k] * carry + far_ref[k, 0:HEAD, :], carry)
+    for k in range(GROUP):
+        out_ref[k, 0:HEAD, :] = carry
+        if k + 1 < GROUP:
+            carry = decay[k] * carry + in_ref[k, 0:HEAD, :]
+    carry = jnp.zeros((HEAD, STATE), f32)
+    for k in reversed(range(1, GROUPS)):
+        carry = jnp.where(k > group, far[k] * carry + far_ref[k, 0:HEAD, :], carry)
+    for k in reversed(range(GROUP)):
+        out_ref[k, HEAD:, :] = carry
         if k:
-            carry = decay[k] * carry + in_ref[k, ROWS:2 * ROWS, :]
+            carry = decay[k] * carry + in_ref[k, HEAD:2 * HEAD, :]
 
 
 def outer_kernel(scale, c_ref, in_ref, u_ref, v_ref, en_ref, te_ref, proj_ref,
-                 yl_ref, gml_ref, gp_ref, gm_ref, pk_ref, ps_ref, yk_ref, ys_ref, y_ref):
+                 yl_ref, gml_ref, gp_ref, gm_ref, pk_ref, yk_ref, send_ref, y_ref):
     c = c_ref[0]
-    carry = in_ref[:, 0:ROWS, :].reshape(HALF, STATE).astype(bf16)
-    adjoint = in_ref[:, ROWS:, :].reshape(HALF, STATE).astype(bf16)
+    carry = in_ref[:, 0:HEAD, :].reshape(HALF, STATE).astype(bf16)
+    adjoint = in_ref[:, HEAD:, :].reshape(HALF, STATE).astype(bf16)
     inject = proj_ref[:, :STATE]
     readout = proj_ref[:, STATE:]
     gi = scale * (gp_ref[:, :STATE] + mm(u_ref[...], adjoint))
     gr = scale * (gp_ref[:, STATE:] + mm(v_ref[...], carry))
     pk_ref[...] = jnp.where(c == 0, gi, gr)
-    ps_ref[...] = jnp.where(c == 0, gr, gi)
+    send_ref[0:CHIP, :] = jnp.where(c == 0, gr, gi)
     grad = gml_ref[...] + te_ref[...] * mm_nt(inject, adjoint)
     gm_ref[...] = (scale * grad).astype(bf16)
     y_ref[...] = yl_ref[...] + en_ref[...] * mm_nt(readout, carry)
     yk_ref[...] = y_ref[pl.ds(pl.multiple_of(c * LD, LD), LD), :]
-    ys_ref[...] = y_ref[pl.ds(pl.multiple_of((1 - c) * LD, LD), LD), :]
+    there = y_ref[pl.ds(pl.multiple_of((1 - c) * LD, LD), LD), :]
+    send_ref[CHIP:CHIP + LD, :] = there[:, :LD]
+    send_ref[CHIP + LD:, :] = there[:, LD:]
 
 
 def fold_kernel(in_ref, out_ref):
@@ -172,26 +193,16 @@
             bc_ref[2 * k:2 * k + 2, half * STATE:(half + 1) * STATE] = piece[:, HALF:]
 
 
-def weight_kernel(xt_ref, gm_ref, pk_ref, pr_ref, out_ref):
+def weight_kernel(c_ref, xt_ref, gm_ref, pk_ref, yk_ref, recv_ref, out_ref, y_ref):
     xt = xt_ref[...]
     out_ref[:, :HALF] = mm(xt, gm_ref[...])
-    out_ref[:, HALF:] = mm(xt, (pk_ref[...] + pr_ref[...]).astype(bf16))
-
-
-def join_kernel(c_ref, yk_ref, yr_ref, out_ref):
+    out_ref[:, HALF:] = mm(xt, (pk_ref[...] + recv_ref[0:CHIP, :]).astype(bf16))
     c = c_ref[0]
-    yk = yk_ref[...].astype(bf16)
-    yr = yr_ref[...].astype(bf16)
-
-    @pl.when(c == 0)
-    def _():
-        out_ref[:, :HALF] = yk
-        out_ref[:, HALF:] = yr
-
-    @pl.when(c != 0)
-    def _():
-        out_ref[:, :HALF] = yr
-        out_ref[:, HALF:] = yk
+    own = pl.multiple_of(c * HALF, LD)
+    oth = pl.multiple_of((1 - c) * HALF, LD)
+    y_ref[:, pl.ds(own, HALF)] = yk_ref[...].astype(bf16)
+    y_ref[:, pl.ds(oth, LD)] = recv_ref[CHIP:CHIP + LD, :].astype(bf16)
+    y_ref[:, pl.ds(pl.multiple_of(oth + LD, LD), LD)] = recv_ref[CHIP + LD:, :].astype(bf16)
 
 
 def whole(shape):
@@ -225,6 +236,7 @@
     grad_scale = float((DP * frames) ** -0.5)
     core = lax.axis_index("c")
     c = core.astype(jnp.int32).reshape(1)
+    group = lax.axis_index("zh").astype(jnp.int32).reshape(1)
     swap = [(0, 1), (1, 0)]
 
     codes = codes.T
@@ -249,28 +261,28 @@
     sq = (CHIP, HALF)
     pay, ue, v, en, te, proj, xc, yl, gml, gpl = call(
         lambda *refs: local_kernel(unit, *refs),
-        [((ZN, PAY, STATE), f32), (sq, bf16), (sq, bf16), (sq, f32), (sq, f32), ((CHIP, 2 * STATE), bf16),
+        [((GROUP, 2 * HEAD + 8, STATE), f32), (sq, bf16), (sq, bf16), (sq, f32), (sq, f32), ((CHIP, 2 * STATE), bf16),
          ((CHIP, d), bf16), (sq, f32), (sq, f32), ((CHIP, 2 * STATE), f32)],
         (*owned, pack), [pltpu.VMEM(sq, f32), pltpu.VMEM((HEADS, CHIP), f32), pltpu.VMEM(sq, bf16)], c)
 
-    pay = lax.all_to_all(pay, "z", 0, 0, tiled=True)
-    (pay,) = call(scan_kernel, [((ZN, 2 * ROWS, STATE), f32)], (pay,))
-    pay = lax.all_to_all(pay, "z", 0, 0, tiled=True)
-
-    gm, pk, ps, yk, ys = call(
+    pay = lax.all_to_all(pay, "zl", 0, 0, tiled=True)
+    (far,) = call(total_kernel, [((GROUPS, HEAD + 8, STATE), f32)], (pay,), (), group)
+    far = lax.all_to_all(far, "zh", 0, 0, tiled=True)
+    (pay,) = call(prefix_kernel, [((GROUP, 2 * HEAD, STATE), f32)], (pay, far), (), group)
+    pay = lax.all_to_all(pay, "zl", 0, 0, tiled=True)
+
+    gm, pk, yk, send = call(
         lambda *refs: outer_kernel(out_scale, *refs),
-        [(sq, bf16), ((CHIP, STATE), f32), ((CHIP, STATE), f32), ((LD, HALF), f32), ((LD, HALF), f32)],
+        [(sq, bf16), ((CHIP, STATE), f32), ((LD, HALF), f32), ((2 * CHIP, LD), f32)],
         (pay, ue, v, en, te, proj, yl, gml, gpl), [pltpu.VMEM(sq, f32)], c)
-    pr = lax.ppermute(ps, "c", swap)
-    yr = lax.ppermute(ys, "c", swap)
+    recv = lax.ppermute(send, "c", swap)
     xt = xc.T.reshape(ZN, 2, DP, 2, CHIP).transpose(2, 0, 1, 3, 4).reshape(d, CHIP)
     width = HALF + STATE
-    (grad,) = call(weight_kernel, [((d, width), f32)], (xt, gm, pk, pr))
-    (y,) = call(join_kernel, [((LD, 2 * HALF), bf16)], (yk, yr), (), c)
+    grad, y = call(weight_kernel, [((d, width), f32), ((LD, 2 * HALF), bf16)], (xt, gm, pk, yk, recv), (), c)
 
     part = lax.all_to_all(grad.reshape(DP, d // DP, width), "dp", 0, 0, tiled=True)
     (part,) = call(fold_kernel, [((ZN, d // DP // ZN, width), f32)], (part,))
-    part = lax.all_to_all(part, "z", 0, 0, tiled=True)
+    part = lax.all_to_all(part, ("zh", "zl"), 0, 0, tiled=True)
     (part,) = call(lambda *refs: spread_kernel(grad_scale, *refs), [((2 * DP, 2, width), f32)], (part,))
     part = lax.all_to_all(part, ("dp", "c"), 0, 0, tiled=True)
     x_grad, bc_grad = call(place_kernel, [((2 * DP, 2 * HALF), f32), ((2 * DP, 2 * STATE), f32)], (part,))
@@ -278,9 +290,9 @@
 
 
 def solution(mesh):
-    mesh = Mesh(mesh.devices.reshape(DP, ZN, 2), ("dp", "z", "c"))
-    frames = P("dp", ("z", "c"), None)
-    rows = P(("z", "c"), None)
+    mesh = Mesh(mesh.devices.reshape(DP, GROUPS, GROUP, 2), ("dp", "zh", "zl", "c"))
+    frames = P("dp", ("zh", "zl", "c"), None)
+    rows = P(("zh", "zl", "c"), None)
     return jax.shard_map(
         body,
         mesh=mesh,

time: 136 us -> 126 us (0.926)
  starting transfers between devices: 34.1 us -> 18.7 us
  blocking collectives: 77.4 us -> 90.5 us
  waiting for transfers between devices: 14.3 us -> 7.84 us
    all_to_all x2 -> x4, blocking collectives: 49.4 us -> 62.3 us  [the longest x1 23.3 us: body(): far = lax.all_to_all(far, 'zh', 0, 0, tiled=True)]
    all_to_all x2 -> x1, starting transfers between devices: 13 us -> 3.45 us  [body(): pay = lax.all_to_all(pay, 'zl', 0, 0, tiled=True)]
    all_to_all x2 -> x1, waiting for transfers between devices: 14.2 us -> 7.73 us  [body(): pay = lax.all_to_all(pay, 'zl', 0, 0, tiled=True)]
    ppermute x2 -> x1, starting transfers between devices: 12.3 us -> 6.42 us  [body(): recv = lax.ppermute(send, 'c', swap)]
    pallas_call x5 -> x3, Pallas kernels: 2.56 us -> 0.79 us  [call(): pl.pallas_call(kernel, out_shape=shapes, compiler_params=params)(*ins)]
    pallas_call x5 -> x7, Pallas kernels: 5.03 us -> 6.03 us  [call(): pl.pallas_call(kernel, out_shape=shapes, grid_spec=pltpu.PrefetchScalarGr...]
  transfers between devices with their start and end apart: 5 -> 3, of which waited for: 3 -> 2; matrix products, arithmetic and copies ran while one was open for 1% -> 1% of each run, Pallas kernels for 2% -> 1%
where the time goes in v3:
time: 126 us
  blocking collectives  90.5 us (72%)
  starting transfers between devices  18.7 us (15%)
  waiting for transfers between devices  7.84 us (6%)
  Pallas kernels  6.82 us (5%)
    all_to_all x1, blocking collectives, body(): lax.all_to_all(grad.reshape(DP, d // DP, width), 'dp', 0, 0, tiled=True)  28.1 us
    all_to_all x1, blocking collectives, body(): far = lax.all_to_all(far, 'zh', 0, 0, tiled=True)  23.3 us
    all_to_all x1, blocking collectives, body(): part = lax.all_to_all(part, ('zh', 'zl'), 0, 0, tiled=True)  16 us
    all_to_all x1, blocking collectives, body(): part = lax.all_to_all(part, ('dp', 'c'), 0, 0, tiled=True)  14.4 us
    ppermute x1, starting transfers between devices, body(): pack = lax.ppermute(pack, 'c', swap)  8.79 us
    all_to_all x1, blocking collectives, body(): pay = lax.all_to_all(pay, 'zl', 0, 0, tiled=True)  8.61 us
    all_to_all x1, waiting for transfers between devices, body(): pay = lax.all_to_all(pay, 'zl', 0, 0, tiled=True)  7.73 us
    ppermute x1, starting transfers between devices, body(): recv = lax.ppermute(send, 'c', swap)  6.42 us
  transfers between devices with their start and end apart: 3, of which 2 were waited for; matrix products, arithmetic and copies ran while one was open for 1% of the time, Pallas kernels for 1%

profile of v3, /device:TPU:1, one launch (start us, length us, event | category | flops | bytes accessed | tf_op | source)
XLA Modules:
  0.0 125.6 jit_solution(17232441957214020269)
XLA Ops:
  0.6 1.0 shard_map.77
  1.7 8.8 %collective-permute-start = (f32[128,1408]{1,0:T(8,128)S(1)}, f32[128,1408]{1,0:T(8,128)S(1)}, u32[]{:S(2)}, u32[]{:S(2)}) collective-permute-start(f32[128,1408]{1,0:T(8,128)S(1)} %shard_map.77), channel_id=1, source_target_pairs={{0,1},{1,0},{2,3},{3,2},{4,5},{5,4},{6,7},{7,6},{8,9},{9,8},{10,11... | collective-permute-start | bytes 2162696 | tf_op jit(solution)/shard_map/ppermute | solution.py:251
  10.5 1.7 %shard_map.76 = (bf16[128,256]{1,0:T(8,128)(2,1)S(1)}, bf16[128,256]{1,0:T(8,128)(2,1)S(1)}, bf16[128,256]{1,0:T(8,128)(2,1)S(1)}, f32[8,128]{1,0:T(8,128)S(1)},...) custom-call(s32[1]{0:T(128)} %bitcast.c_ref.refs_0_, ...), custom_call_target="tpu_custom_call" | custom-call | tf_op jit(solution)/shard_map/pallas_call | solution.py:218
  12.2 0.1 collective-permute-done.refs_8_
  12.3 1.9 %shard_map.78 = (f32[4,136,128]{2,1,0:T(8,128)}, bf16[256,256]{1,0:T(8,128)(2,1)S(1)}, bf16[256,256]{1,0:T(8,128)(2,1)S(1)}, f32[256,256]{1,0:T(8,128)S(1)}, f32...) custom-call(s32[1]{0:T(128)} %bitcast.c_ref.refs_0_, ...), custom_call_target="tpu_custom_call" | custom-call | tf_op jit(solution)/shard_map/pallas_call | solution.py:218
  14.1 3.4 %all-to-all-start = ((f32[4,136,128]{2,1,0:T(8,128)}), f32[4,136,128]{2,1,0:T(8,128)S(1)}, u32[]{:S(2)}, u32[]{:S(2)}) async-start(f32[4,136,128]{2,1,0:T(8,128)} %get-tuple-element.36), calls=%async_computation | async-start | bytes 557056 | tf_op jit(solution)/shard_map/all_to_all | solution.py:268
  17.6 7.7 %all-to-all-done.in_ref = f32[4,136,128]{2,1,0:T(8,128)S(1)} async-done(((f32[4,136,128]{2,1,0:T(8,128)}), f32[4,136,128]{2,1,0:T(8,128)S(1)}, u32[]{:S(2)}, u32[]{:S(2)}) %all-to-all-start) | async-done | bytes 278560 | tf_op jit(solution)/shard_map/all_to_all | solution.py:268
  25.4 23.3 %all_to_all.30.far_ref = f32[4,72,128]{2,1,0:T(8,128)S(1)} all-to-all(f32[4,72,128]{2,1,0:T(8,128)S(1)} %shard_map.79), channel_id=1, replica_groups=mesh['dp'=16,'zh'=4,'zl'=4,'c'=2] {'zh'}, dimensions={0} | all-to-all | bytes 294912 | tf_op jit(solution)/shard_map/all_to_all | solution.py:270
  48.7 0.1 shard_map.80
  48.7 8.6 %all_to_all.31.refs_1_ = f32[4,128,128]{2,1,0:T(8,128)S(1)} all-to-all(f32[4,128,128]{2,1,0:T(8,128)S(1)} %shard_map.80), channel_id=1, replica_groups=mesh['dp'=16,'zh'=4,'zl'=4,'c'=2] {'zl'}, dimensions={0} | all-to-all | bytes 524288 | tf_op jit(solution)/shard_map/all_to_all | solution.py:272
  57.3 0.3 shard_map.81
  57.6 6.4 %collective-permute-start.1 = (f32[512,128]{1,0:T(8,128)S(1)}, f32[512,128]{1,0:T(8,128)S(1)}, u32[]{:S(2)}, u32[]{:S(2)}) collective-permute-start(f32[512,128]{1,0:T(8,128)S(1)} %get-tuple-element.48), channel_id=1, source_target_pairs={{0,1},{1,0},{2,3},{3,2},{4,5},{5,4},{6,7},{7,6},{8,9},{9,8},{10,11... | collective-permute-start | bytes 786440 | tf_op jit(solution)/shard_map/ppermute | solution.py:278
  64.1 0.2 copy.9
  64.3 0.2 reshape.22
  64.5 0.5 copy.10
  65.0 0.2 reshape.23.xt_ref
  65.2 0.0 collective-permute-done.1.recv_ref
  65.2 1.0 shard_map.82
  66.2 28.1 %all_to_all.32.in_ref = f32[16,64,384]{2,1,0:T(8,128)S(1)} all-to-all(f32[16,64,384]{2,1,0:T(8,128)S(1)} %bitcast.11), channel_id=1, replica_groups=mesh['dp'=16,'zh'=4,'zl'=4,'c'=2] {'dp'}, dimensions={0} | all-to-all | bytes 3145728 | tf_op jit(solution)/shard_map/all_to_all | solution.py:283
  94.4 0.1 shard_map.83
  94.4 16.0 %all_to_all.33.refs_0_ = f32[16,4,384]{2,1,0:T(4,128)S(1)} all-to-all(f32[16,4,384]{2,1,0:T(4,128)S(1)} %shard_map.83), channel_id=1, replica_groups=mesh['dp'=16,'zh'=4,'zl'=4,'c'=2] {'zh','zl'}, dimensions={0} | all-to-all | bytes 196608 | tf_op jit(solution)/shard_map/all_to_all | solution.py:285
  110.5 14.4 %all_to_all.34.in_ref = f32[32,2,384]{2,1,0:T(2,128)S(1)} all-to-all(f32[32,2,384]{2,1,0:T(2,128)S(1)} %shard_map.84), channel_id=1, replica_groups=mesh['dp'=16,'zh'=4,'zl'=4,'c'=2] {'dp','c'}, dimensions={0} | all-to-all | bytes 196608 | tf_op jit(solution)/shard_map/all_to_all | solution.py:287
  124.9 0.7 shard_map.85
  (2 shorter events, 0.1 us)
Async XLA Ops:
  1.7 10.6 %collective-permute-start = (f32[128,1408]{1,0:T(8,128)S(1)}, f32[128,1408]{1,0:T(8,128)S(1)}, u32[]{:S(2)}, u32[]{:S(2)}) collective-permute-start(f32[128,1408]{1,0:T(8,128)S(1)} %shard_map.77), channel_id=1, source_target_pairs={{0,1},{1,0},{2,3},{3,2},{4,5},{5,4},{6,7},{7,6},{8,9},{9,8},{10,11... | collective-permute-start | bytes 2162696 | tf_op jit(solution)/shard_map/ppermute | solution.py:251
  14.1 11.2 %all-to-all-start = ((f32[4,136,128]{2,1,0:T(8,128)}), f32[4,136,128]{2,1,0:T(8,128)S(1)}, u32[]{:S(2)}, u32[]{:S(2)}) async-start(f32[4,136,128]{2,1,0:T(8,128)} %get-tuple-element.36), calls=%async_computation | async-start | bytes 557056 | tf_op jit(solution)/shard_map/all_to_all | solution.py:268
  57.6 7.6 %collective-permute-start.1 = (f32[512,128]{1,0:T(8,128)S(1)}, f32[512,128]{1,0:T(8,128)S(1)}, u32[]{:S(2)}, u32[]{:S(2)}) collective-permute-start(f32[512,128]{1,0:T(8,128)S(1)} %get-tuple-element.48), channel_id=1, source_target_pairs={{0,1},{1,0},{2,3},{3,2},{4,5},{5,4},{6,7},{7,6},{8,9},{9,8},{10,11... | collective-permute-start | bytes 786440 | tf_op jit(solution)/shard_map/ppermute | solution.py:278

commit v4 on v3

v4 whole, which is shorter than its diff:
```python
import jax
import jax.numpy as jnp
from jax import lax
from jax.experimental import pallas as pl
from jax.experimental.pallas import tpu as pltpu
from jax.sharding import Mesh, PartitionSpec as P

f32 = jnp.float32
bf16 = jnp.bfloat16

LD = 128
CHIP = 2 * LD
HEADS = 8
HEAD = 64
STATE = 128
HALF = HEADS * HEAD // 2
ZN = 16
DP = 16
GROUP = 4
GROUPS = ZN // GROUP


def mm(a, b):
    return jnp.dot(a, b, preferred_element_type=f32)


def mm_tn(a, b):
    return lax.dot_general(a, b, (((0,), (0,)), ((), ())), preferred_element_type=f32)


def mm_nt(a, b):
    return lax.dot_general(a, b, (((1,), (1,)), ((), ())), preferred_element_type=f32)


def causal(shape):
    return lax.broadcasted_iota(jnp.int32, shape, 0) >= lax.broadcasted_iota(jnp.int32, shape, 1)


def pack_kernel(c_ref, group_ref, x_ref, g_ref, codes_ref, out_ref):
    d = x_ref.shape[1]
    out_ref[:, :d] = x_ref[...].astype(f32)
    out_ref[:, d:d + HALF] = g_ref[...].astype(f32)
    out_ref[:, d + HALF:] = jnp.zeros((LD, LD), f32)
    out_ref[0:HEADS, d + HALF:] = codes_ref[...].astype(f32)


def own_kernel(c_ref, group_ref, x_ref, g_ref, codes_ref, wx_ref, wbc_ref,
               mix_ref, proj_ref, g_out_ref, codes_out_ref, x_out_ref, wx_out_ref, wbc_out_ref):
    x = x_ref[...]
    wx = wx_ref[...]
    wbc = wbc_ref[...]
    mix_ref[...] = mm(x, wx).astype(bf16)
    proj_ref[...] = mm(x, wbc).astype(bf16)
    g_out_ref[...] = g_ref[...]
    codes_out_ref[...] = codes_ref[...].astype(f32)
    x_out_ref[...] = x
    wx_out_ref[...] = wx
    wbc_out_ref[...] = wbc


def local_kernel(unit, c_ref, group_ref, mix_ref, pj_ref, g_ref, codes_ref, x_ref, wx_ref, wbc_ref, pack_ref,
                 pay_ref, ue_ref, v_ref, en_ref, te_ref, proj_ref, xc_ref, yl_ref, gm_ref, gp_ref,
                 gs_ref, cs_ref, ms_ref):
    c = c_ref[0]
    own = pl.multiple_of(c * LD, LD)
    oth = pl.multiple_of((1 - c) * LD, LD)
    d = x_ref.shape[1]
    xo = pack_ref[:, :d].astype(bf16)
    xc_ref[pl.ds(own, LD), :] = x_ref[...]
    xc_ref[pl.ds(oth, LD), :] = xo
    gs_ref[pl.ds(own, LD), :] = g_ref[...].astype(f32)
    gs_ref[pl.ds(oth, LD), :] = pack_ref[:, d:d + HALF]
    cs_ref[:, pl.ds(own, LD)] = codes_ref[...]
    cs_ref[:, pl.ds(oth, LD)] = pack_ref[0:HEADS, d + HALF:]
    ms_ref[pl.ds(own, LD), :] = mix_ref[...]
    ms_ref[pl.ds(oth, LD), :] = mm(xo, wx_ref[...]).astype(bf16)
    proj_ref[pl.ds(own, LD), :] = pj_ref[...]
    proj_ref[pl.ds(oth, LD), :] = mm(xo, wbc_ref[...]).astype(bf16)
    codes = cs_ref[...]
    hi = jnp.floor(codes * (1.0 / 32.0))
    lo = codes - 32.0 * hi
    row = lax.broadcasted_iota(jnp.int32, (HEADS, HALF), 0)
    col = lax.broadcasted_iota(jnp.int32, (HEADS, HALF), 1)
    spread = jnp.where(row == col // HEAD + c * (HEADS // 2), 1.0, 0.0).astype(bf16)
    hi = mm_tn(hi.astype(bf16), spread).astype(bf16)
    lo = mm_tn(lo.astype(bf16), spread).astype(bf16)
    mask = causal((CHIP, CHIP))
    tri = jnp.where(mask, 1.0, 0.0).astype(bf16)
    running = unit * (32.0 * mm(tri, hi) + mm(tri, lo))
    last = running[CHIP - 1:CHIP, :]
    en = jnp.exp(-running)
    ep = jnp.exp(running)
    te = jnp.exp(running - last)
    en_ref[...] = en
    te_ref[...] = te
    mixer = ms_ref[...].astype(f32)
    inject = proj_ref[:, :STATE]
    readout = proj_ref[:, STATE:]
    v = (en * gs_ref[...]).astype(bf16)
    ue = (te * mixer).astype(bf16)
    u = (ep * mixer).astype(bf16)
    ue_ref[...] = ue
    v_ref[...] = v
    state = mm_tn(ue, inject)
    adjoint = mm_tn(v, readout)
    for h in range(GROUP):
        at = (group_ref[0] + h) & (GROUP - 1)
        pay_ref[at, 0:HEAD, :] = state[h * HEAD:(h + 1) * HEAD, :]
        pay_ref[at, HEAD:2 * HEAD, :] = adjoint[h * HEAD:(h + 1) * HEAD, :]
        pay_ref[at, 2 * HEAD:, :] = jnp.broadcast_to(last[:, h * HEAD:h * HEAD + 1], (8, STATE))
    scores = jnp.where(mask, mm_nt(readout, inject), 0.0).astype(bf16)
    pairs = jnp.where(mask, mm_nt(v, u), 0.0).astype(bf16)
    yl_ref[...] = en * mm(scores, u)
    gm_ref[...] = ep * mm_tn(scores, v)
    gp_ref[:, :STATE] = mm_tn(pairs, readout)
    gp_ref[:, STATE:] = mm(pairs, inject)


def total_kernel(c_ref, group_ref, in_ref, out_ref):
    group = group_ref[0]
    logs = [in_ref[k, 2 * HEAD:, :] for k in range(GROUP)]
    decay = [jnp.exp(-a[0:1, :]) for a in logs]
    state = in_ref[0, 0:HEAD, :]
    for k in range(1, GROUP):
        state = decay[k] * state + in_ref[k, 0:HEAD, :]
    adjoint = in_ref[GROUP - 1, HEAD:2 * HEAD, :]
    for k in reversed(range(GROUP - 1)):
        adjoint = decay[k] * adjoint + in_ref[k, HEAD:2 * HEAD, :]
    total = logs[0] + logs[1] + logs[2] + logs[3]
    for k in range(GROUPS):
        out_ref[k, 0:HEAD, :] = jnp.where(k > group, state, adjoint)
        out_ref[k, HEAD:, :] = total


def prefix_kernel(c_ref, group_ref, in_ref, far_ref, out_ref):
    group = group_ref[0]
    far = [jnp.exp(-far_ref[k, HEAD:HEAD + 1, :]) for k in range(GROUPS)]
    decay = [jnp.exp(-in_ref[k, 2 * HEAD:2 * HEAD + 1, :]) for k in range(GROUP)]
    carry = jnp.zeros((HEAD, STATE), f32)
    for k in range(GROUPS - 1):
        carry = jnp.where(k < group, far[k] * carry + far_ref[k, 0:HEAD, :], carry)
    for k in range(GROUP):
        out_ref[k, 0:HEAD, :] = carry
        if k + 1 < GROUP:
            carry = decay[k] * carry + in_ref[k, 0:HEAD, :]
    carry = jnp.zeros((HEAD, STATE), f32)
    for k in reversed(range(1, GROUPS)):
        carry = jnp.where(k > group, far[k] * carry + far_ref[k, 0:HEAD, :], carry)
    for k in reversed(range(GROUP)):
        out_ref[k, HEAD:, :] = carry
        if k:
            carry = decay[k] * carry + in_ref[k, HEAD:2 * HEAD, :]


def outer_kernel(scale, c_ref, group_ref, in_ref, u_ref, v_ref, en_ref, te_ref, proj_ref,
                 yl_ref, gml_ref, gp_ref, gm_ref, pk_ref, yk_ref, send_ref, y_ref):
    c = c_ref[0]
    pieces = [in_ref[(group_ref[0] + h) & (GROUP - 1)] for h in range(GROUP)]
    carry = jnp.concatenate([a[:HEAD] for a in pieces], axis=0).astype(bf16)
    adjoint = jnp.concatenate([a[HEAD:] for a in pieces], axis=0).astype(bf16)
    inject = proj_ref[:, :STATE]
    readout = proj_ref[:, STATE:]
    gi = scale * (gp_ref[:, :STATE] + mm(u_ref[...], adjoint))
    gr = scale * (gp_ref[:, STATE:] + mm(v_ref[...], carry))
    pk_ref[...] = jnp.where(c == 0, gi, gr)
    send_ref[0:CHIP, :] = jnp.where(c == 0, gr, gi)
    grad = gml_ref[...] + te_ref[...] * mm_nt(inject, adjoint)
    gm_ref[...] = (scale * grad).astype(bf16)
    y_ref[...] = yl_ref[...] + en_ref[...] * mm_nt(readout, carry)
    yk_ref[...] = y_ref[pl.ds(pl.multiple_of(c * LD, LD), LD), :]
    there = y_ref[pl.ds(pl.multiple_of((1 - c) * LD, LD), LD), :]
    send_ref[CHIP:CHIP + LD, :] = there[:, :LD]
    send_ref[CHIP + LD:, :] = there[:, LD:]


def weight_kernel(c_ref, group_ref, xt_ref, gm_ref, pk_ref, recv_ref, out_ref):
    xt = xt_ref[...]
    out_ref[:, :HALF] = mm(xt, gm_ref[...])
    out_ref[:, HALF:] = mm(xt, (pk_ref[...] + recv_ref[...]).astype(bf16))


def fold_kernel(c_ref, group_ref, in_ref, out_ref):
    total = jnp.sum(in_ref[...], axis=0)
    step = out_ref.shape[1]
    for k in range(ZN):
        out_ref[k] = total[k * step:(k + 1) * step, :]


def spread_kernel(scale, c_ref, group_ref, in_ref, out_ref):
    total = scale * jnp.sum(in_ref[...], axis=0)
    for k in range(2 * DP):
        half = k % 2
        out_ref[k] = total[2 * half:2 * half + 2, :]


def place_kernel(c_ref, group_ref, in_ref, yk_ref, recv_ref, x_ref, bc_ref, y_ref):
    for k in range(DP):
        for half in range(2):
            piece = in_ref[2 * k + half]
            x_ref[2 * k:2 * k + 2, half * HALF:(half + 1) * HALF] = piece[:, :HALF]
            bc_ref[2 * k:2 * k + 2, half * STATE:(half + 1) * STATE] = piece[:, HALF:]
    c = c_ref[0]
    own = pl.multiple_of(c * HALF, LD)
    oth = pl.multiple_of((1 - c) * HALF, LD)
    y_ref[:, pl.ds(own, HALF)] = yk_ref[...].astype(bf16)
    y_ref[:, pl.ds(oth, LD)] = recv_ref[0:LD, :].astype(bf16)
    y_ref[:, pl.ds(pl.multiple_of(oth + LD, LD), LD)] = recv_ref[LD:, :].astype(bf16)


def whole(shape):
    return pl.BlockSpec(shape, lambda i, c, g: (0,) * len(shape))


def call(kernel, place, outs, ins, scratch=(), specs=None):
    return pl.pallas_call(
        kernel,
        out_shape=[jax.ShapeDtypeStruct(s, d) for s, d in outs],
        grid_spec=pltpu.PrefetchScalarGridSpec(
            num_scalar_prefetch=2, grid=(1,), in_specs=specs or [whole(a.shape) for a in ins],
            out_specs=[whole(s) for s, _ in outs], scratch_shapes=list(scratch)),
        compiler_params=pltpu.CompilerParams(vmem_limit_bytes=16 * 1024 * 1024),
    )(*place, *ins)


def body(records, x_weight, bc_weight, decay_codes, out_grad):
    x = records[0]
    g = out_grad[0]
    codes = decay_codes[0].T
    d = x.shape[1]
    frames = LD * 2 * ZN
    unit = 1.0 / (32.0 * frames)
    out_scale = float((STATE * frames) ** -0.5)
    grad_scale = float((DP * frames) ** -0.5)
    place = lax.optimization_barrier((
        lax.axis_index("c").astype(jnp.int32).reshape(1),
        lax.div(lax.axis_index("z"), GROUP).astype(jnp.int32).reshape(1)))
    swap = [(0, 1), (1, 0)]
    near = [[GROUP * a + b for b in range(GROUP)] for a in range(GROUPS)]
    across = [[GROUP * a + (a + b) % GROUP for a in range(GROUPS)] for b in range(GROUP)]

    here = pl.BlockSpec((LD, HALF), lambda i, c, g: (0, c[0]))
    there = pl.BlockSpec((LD, HALF), lambda i, c, g: (0, 1 - c[0]))
    x, g, codes, wx, wbc = (
        pltpu.with_memory_space_constraint(a, pltpu.MemorySpace.HBM)
        for a in (x, g, codes, x_weight, bc_weight))
    (pack,) = call(
        pack_kernel, place, [((LD, d + HALF + LD), f32)], (x, g, codes), (),
        [whole(x.shape), there, whole(codes.shape)])
    pack = lax.ppermute(pack, "c", swap)
    half = (LD, HALF)
    owned = call(
        own_kernel, place,
        [(half, bf16), ((LD, 2 * STATE), bf16), (half, bf16), ((HEADS, LD), f32), ((LD, d), bf16),
         ((d, HALF), bf16), ((d, 2 * STATE), bf16)],
        (x, g, codes, wx, wbc), (),
        [whole(x.shape), here, whole(codes.shape), pl.BlockSpec((d, HALF), lambda i, c, g: (0, c[0])),
         whole(wbc.shape)])

    sq = (CHIP, HALF)
    pay, ue, v, en, te, proj, xc, yl, gml, gpl = call(
        lambda *refs: local_kernel(unit, *refs), place,
        [((GROUP, 2 * HEAD + 8, STATE), f32), (sq, bf16), (sq, bf16), (sq, f32), (sq, f32),
         ((CHIP, 2 * STATE), bf16), ((CHIP, d), bf16), (sq, f32), (sq, f32), ((CHIP, 2 * STATE), f32)],
        (*owned, pack), [pltpu.VMEM(sq, f32), pltpu.VMEM((HEADS, CHIP), f32), pltpu.VMEM(sq, bf16)])

    pay = lax.all_to_all(pay, "z", 0, 0, tiled=True, axis_index_groups=near)
    (far,) = call(total_kernel, place, [((GROUPS, HEAD + 8, STATE), f32)], (pay,))
    far = lax.all_to_all(far, "z", 0, 0, tiled=True, axis_index_groups=across)
    (pay,) = call(prefix_kernel, place, [((GROUP, 2 * HEAD, STATE), f32)], (pay, far))
    pay = lax.all_to_all(pay, "z", 0, 0, tiled=True, axis_index_groups=near)

    gm, pk, yk, send = call(
        lambda *refs: outer_kernel(out_scale, *refs), place,
        [(sq, bf16), ((CHIP, STATE), f32), ((LD, HALF), f32), ((2 * CHIP, LD), f32)],
        (pay, ue, v, en, te, proj, yl, gml, gpl), [pltpu.VMEM(sq, f32)])
    recv = lax.ppermute(send, "c", swap)
    xt = xc.T.reshape(ZN, 2, DP, 2, CHIP).transpose(2, 0, 1, 3, 4).reshape(d, CHIP)
    width = HALF + STATE
    top = pl.BlockSpec((CHIP, LD), lambda i, c, g: (0, 0))
    low = pl.BlockSpec((CHIP, LD), lambda i, c, g: (1, 0))
    (grad,) = call(
        weight_kernel, place, [((d, width), f32)], (xt, gm, pk, recv), (),
        [whole(xt.shape), whole(gm.shape), whole(pk.shape), top])

    part = lax.all_to_all(grad.reshape(DP, d // DP, width), "dp", 0, 0, tiled=True)
    (part,) = call(fold_kernel, place, [((ZN, d // DP // ZN, width), f32)], (part,))
    part = lax.all_to_all(part, "z", 0, 0, tiled=True)
    (part,) = call(lambda *refs: spread_kernel(grad_scale, *refs), place, [((2 * DP, 2, width), f32)], (part,))
    part = lax.all_to_all(part, ("dp", "c"), 0, 0, tiled=True)
    x_grad, bc_grad, y = call(
        place_kernel, place,
        [((2 * DP, 2 * HALF), f32), ((2 * DP, 2 * STATE), f32), ((LD, 2 * HALF), bf16)], (part, yk, recv), (),
        [whole(part.shape), whole(yk.shape), low])
    return y[None], x_grad, bc_grad


def solution(mesh):
    mesh = Mesh(mesh.devices.reshape(DP, ZN, 2), ("dp", "z", "c"))
    frames = P("dp", ("z", "c"), None)
    rows = P(("z", "c"), None)
    return jax.shard_map(
        body,
        mesh=mesh,
        in_specs=(frames, P(), P(), frames, frames),
        out_specs=(frames, rows, rows),
        check_vma=False,
    )
```

time: 126 us -> 122 us (0.968)
  blocking collectives: 90.5 us -> 99.8 us
  waiting for transfers between devices: 7.84 us -> 0.11 us
  starting transfers between devices: 18.7 us -> 14.5 us
    all_to_all x3 -> x4, blocking collectives: 47.9 us -> 57.2 us  [the longest x2 23.3 us: body(): pay = lax.all_to_all(pay, 'z', 0, 0, tiled=True, axis_index_groups=near)]
    all_to_all x1 -> x0, waiting for transfers between devices: 7.73 us -> none  [body(): pay = lax.all_to_all(pay, 'zl', 0, 0, tiled=True)]
    all_to_all x1 -> x0, starting transfers between devices: 3.45 us -> none  [body(): pay = lax.all_to_all(pay, 'zl', 0, 0, tiled=True)]
  transfers between devices with their start and end apart: 3 -> 2, of which waited for: 2 -> 1; matrix products, arithmetic and copies ran while one was open for 1% -> 1% of each run, Pallas kernels for 1% -> 1%
where the time goes in v4:
time: 122 us
  blocking collectives  99.8 us (82%)
  starting transfers between devices  14.5 us (12%)
  Pallas kernels  5.7 us (5%)
    all_to_all x1, blocking collectives, body(): lax.all_to_all(grad.reshape(DP, d // DP, width), 'dp', 0, 0, tiled=True)  28.1 us
    all_to_all x2, blocking collectives, body(): pay = lax.all_to_all(pay, 'z', 0, 0, tiled=True, axis_index_groups=near)  23.3 us
    all_to_all x1, blocking collectives, body(): far = lax.all_to_all(far, 'z', 0, 0, tiled=True, axis_index_groups=across)  19.4 us
    all_to_all x1, blocking collectives, body(): part = lax.all_to_all(part, 'z', 0, 0, tiled=True)  14.6 us
    all_to_all x1, blocking collectives, body(): part = lax.all_to_all(part, ('dp', 'c'), 0, 0, tiled=True)  14.4 us
    ppermute x1, starting transfers between devices, body(): pack = lax.ppermute(pack, 'c', swap)  8.79 us
    pallas_call x10, Pallas kernels, call(): pl.pallas_call(kernel, out_shape=[jax.ShapeDtypeStruct(s, d) for s, d in...  5.7 us
    ppermute x1, starting transfers between devices, body(): recv = lax.ppermute(send, 'c', swap)  5.67 us
  transfers between devices with their start and end apart: 2, of which 1 were waited for; matrix products, arithmetic and copies ran while one was open for 1% of the time, Pallas kernels for 1%

profile of v4, /device:TPU:1, one launch (start us, length us, event | category | flops | bytes accessed | tf_op | source)
XLA Modules:
  0.0 121.8 jit_solution(13211246660232320758)
XLA Ops:
  0.6 1.0 shard_map.77
  1.7 8.8 %collective-permute-start = (f32[128,1408]{1,0:T(8,128)S(1)}, f32[128,1408]{1,0:T(8,128)S(1)}, u32[]{:S(2)}, u32[]{:S(2)}) collective-permute-start(f32[128,1408]{1,0:T(8,128)S(1)} %shard_map.77), channel_id=1, source_target_pairs={{0,1},{1,0},{2,3},{3,2},{4,5},{5,4},{6,7},{7,6},{8,9},{9,8},{10,11... | collective-permute-start | bytes 2162696 | tf_op jit(solution)/shard_map/ppermute | solution.py:249
  10.5 1.7 %shard_map.76 = (bf16[128,256]{1,0:T(8,128)(2,1)S(1)}, bf16[128,256]{1,0:T(8,128)(2,1)S(1)}, bf16[128,256]{1,0:T(8,128)(2,1)S(1)}, f32[8,128]{1,0:T(8,128)S(1)},...) custom-call(s32[1]{0:T(128)} %bitcast.c_ref.refs_0_, ...), custom_call_target="tpu_custom_call" | custom-call | tf_op jit(solution)/shard_map/pallas_call | solution.py:215
  12.2 0.1 collective-permute-done.refs_9_
  12.3 1.3 %shard_map.78 = (f32[4,136,128]{2,1,0:T(8,128)S(1)}, bf16[256,256]{1,0:T(8,128)(2,1)S(1)}, bf16[256,256]{1,0:T(8,128)(2,1)S(1)}, f32[256,256]{1,0:T(8,128)S(1)},...) custom-call(s32[1]{0:T(128)} %bitcast.c_ref.refs_0_, ...), custom_call_target="tpu_custom_call" | custom-call | tf_op jit(solution)/shard_map/pallas_call | solution.py:215
  13.6 10.9 %all_to_all.30.in_ref = f32[4,136,128]{2,1,0:T(8,128)S(1)} all-to-all(f32[4,136,128]{2,1,0:T(8,128)S(1)} %get-tuple-element.39), channel_id=1, replica_groups={{0,2,4,6},{8,10,12,14},{16,18,20,22},{24,26,28,30},{1,3,5,7},{9,11,13,1..., dimensions={0} | all-to-all | bytes 557056 | tf_op jit(solution)/shard_map/all_to_all | solution.py:266
  24.5 19.4 %all_to_all.31.far_ref = f32[4,72,128]{2,1,0:T(8,128)S(1)} all-to-all(f32[4,72,128]{2,1,0:T(8,128)S(1)} %shard_map.79), channel_id=1, replica_groups={{0,10,20,30},{2,12,22,24},{4,14,16,26},{6,8,18,28},{1,11,21,31},{3,13,2..., dimensions={0} | all-to-all | bytes 294912 | tf_op jit(solution)/shard_map/all_to_all | solution.py:268
  43.9 12.4 %all_to_all.32.refs_2_ = f32[4,128,128]{2,1,0:T(8,128)S(1)} all-to-all(f32[4,128,128]{2,1,0:T(8,128)S(1)} %shard_map.80), channel_id=1, replica_groups={{0,2,4,6},{8,10,12,14},{16,18,20,22},{24,26,28,30},{1,3,5,7},{9,11,13,1..., dimensions={0} | all-to-all | bytes 524288 | tf_op jit(solution)/shard_map/all_to_all | solution.py:270
  56.3 0.3 shard_map.81
  56.6 5.7 %collective-permute-start.1 = (f32[512,128]{1,0:T(8,128)S(1)}, f32[512,128]{1,0:T(8,128)S(1)}, u32[]{:S(2)}, u32[]{:S(2)}) collective-permute-start(f32[512,128]{1,0:T(8,128)S(1)} %get-tuple-element.50), channel_id=1, source_target_pairs={{0,1},{1,0},{2,3},{3,2},{4,5},{5,4},{6,7},{7,6},{8,9},{9,8},{10,11... | collective-permute-start | bytes 786440 | tf_op jit(solution)/shard_map/ppermute | solution.py:276
  62.3 0.2 copy.9
  62.5 0.2 reshape.23
  62.7 0.5 copy.10
  63.2 0.2 reshape.24.xt_ref
  63.4 0.0 collective-permute-done.1.recv_ref
  63.4 0.4 shard_map.82
  63.8 28.1 %all_to_all.33.in_ref = f32[16,64,384]{2,1,0:T(8,128)S(1)} all-to-all(f32[16,64,384]{2,1,0:T(8,128)S(1)} %bitcast.11), channel_id=1, replica_groups=mesh['dp'=16,'z'=16,'c'=2] {'dp'}, dimensions={0} | all-to-all | bytes 3145728 | tf_op jit(solution)/shard_map/all_to_all | solution.py:285
  92.0 0.1 shard_map.83
  92.1 14.6 %all_to_all.34.refs_2_ = f32[16,4,384]{2,1,0:T(4,128)S(1)} all-to-all(f32[16,4,384]{2,1,0:T(4,128)S(1)} %shard_map.83), channel_id=1, replica_groups=mesh['dp'=16,'z'=16,'c'=2] {'z'}, dimensions={0} | all-to-all | bytes 196608 | tf_op jit(solution)/shard_map/all_to_all | solution.py:287
  106.7 14.4 %all_to_all.35.in_ref = f32[32,2,384]{2,1,0:T(2,128)S(1)} all-to-all(f32[32,2,384]{2,1,0:T(2,128)S(1)} %shard_map.84), channel_id=1, replica_groups=mesh['dp'=16,'z'=16,'c'=2] {'dp','c'}, dimensions={0} | all-to-all | bytes 196608 | tf_op jit(solution)/shard_map/all_to_all | solution.py:289
  121.1 0.7 shard_map.85
  (3 shorter events, 0.1 us)
Async XLA Ops:
  1.7 10.6 %collective-permute-start = (f32[128,1408]{1,0:T(8,128)S(1)}, f32[128,1408]{1,0:T(8,128)S(1)}, u32[]{:S(2)}, u32[]{:S(2)}) collective-permute-start(f32[128,1408]{1,0:T(8,128)S(1)} %shard_map.77), channel_id=1, source_target_pairs={{0,1},{1,0},{2,3},{3,2},{4,5},{5,4},{6,7},{7,6},{8,9},{9,8},{10,11... | collective-permute-start | bytes 2162696 | tf_op jit(solution)/shard_map/ppermute | solution.py:249
  56.6 6.8 %collective-permute-start.1 = (f32[512,128]{1,0:T(8,128)S(1)}, f32[512,128]{1,0:T(8,128)S(1)}, u32[]{:S(2)}, u32[]{:S(2)}) collective-permute-start(f32[512,128]{1,0:T(8,128)S(1)} %get-tuple-element.50), channel_id=1, source_target_pairs={{0,1},{1,0},{2,3},{3,2},{4,5},{5,4},{6,7},{7,6},{8,9},{9,8},{10,11... | collective-permute-start | bytes 786440 | tf_op jit(solution)/shard_map/ppermute | solution.py:276

commit v5 on v4

--- a/solution.py
+++ b/solution.py
@@ -36,29 +36,44 @@
     return lax.broadcasted_iota(jnp.int32, shape, 0) >= lax.broadcasted_iota(jnp.int32, shape, 1)
 
 
-def pack_kernel(c_ref, group_ref, x_ref, g_ref, codes_ref, out_ref):
+def pack_kernel(c_ref, group_ref, x_hbm, g_hbm, codes_hbm, out_ref, x_ref, g_ref, codes_ref,
+                there_ref, int_ref, sems):
+    c = c_ref[0]
     d = x_ref.shape[1]
+    own = pl.multiple_of(c * HALF, HALF)
+    oth = pl.multiple_of((1 - c) * HALF, HALF)
+    copies = [
+        pltpu.make_async_copy(x_hbm, x_ref, sems.at[0]),
+        pltpu.make_async_copy(g_hbm.at[:, pl.ds(oth, HALF)], there_ref, sems.at[1]),
+        pltpu.make_async_copy(codes_hbm, int_ref, sems.at[2]),
+        pltpu.make_async_copy(g_hbm.at[:, pl.ds(own, HALF)], g_ref, sems.at[3]),
+    ]
+    for copy in copies:
+        copy.start()
+    for copy in copies:
+        copy.wait()
+    codes = int_ref[...].astype(f32)
+    codes_ref[...] = codes
     out_ref[:, :d] = x_ref[...].astype(f32)
-    out_ref[:, d:d + HALF] = g_ref[...].astype(f32)
-    out_ref[:, d + HALF:] = jnp.zeros((LD, LD), f32)
-    out_ref[0:HEADS, d + HALF:] = codes_ref[...].astype(f32)
-
-
-def own_kernel(c_ref, group_ref, x_ref, g_ref, codes_ref, wx_ref, wbc_ref,
-               mix_ref, proj_ref, g_out_ref, codes_out_ref, x_out_ref, wx_out_ref, wbc_out_ref):
+    out_ref[:, d:d + HALF] = there_ref[...].astype(f32)
+    out_ref[HEADS:, d + HALF:] = jnp.zeros((LD - HEADS, LD), f32)
+    out_ref[0:HEADS, d + HALF:] = codes
+
+
+def own_kernel(c_ref, group_ref, x_ref, wx_hbm, wbc_hbm, mix_ref, proj_ref, wx_ref, wbc_ref, sems):
+    own = pl.multiple_of(c_ref[0] * HALF, HALF)
+    first = pltpu.make_async_copy(wx_hbm.at[:, pl.ds(own, HALF)], wx_ref, sems.at[0])
+    second = pltpu.make_async_copy(wbc_hbm, wbc_ref, sems.at[1])
+    first.start()
+    second.start()
     x = x_ref[...]
-    wx = wx_ref[...]
-    wbc = wbc_ref[...]
-    mix_ref[...] = mm(x, wx).astype(bf16)
-    proj_ref[...] = mm(x, wbc).astype(bf16)
-    g_out_ref[...] = g_ref[...]
-    codes_out_ref[...] = codes_ref[...].astype(f32)
-    x_out_ref[...] = x
-    wx_out_ref[...] = wx
-    wbc_out_ref[...] = wbc
-
-
-def local_kernel(unit, c_ref, group_ref, mix_ref, pj_ref, g_ref, codes_ref, x_ref, wx_ref, wbc_ref, pack_ref,
+    first.wait()
+    mix_ref[...] = mm(x, wx_ref[...]).astype(bf16)
+    second.wait()
+    proj_ref[...] = mm(x, wbc_ref[...]).astype(bf16)
+
+
+def local_kernel(unit, c_ref, group_ref, mix_ref, pj_ref, wx_ref, wbc_ref, x_ref, g_ref, codes_ref, pack_ref,
                  pay_ref, ue_ref, v_ref, en_ref, te_ref, proj_ref, xc_ref, yl_ref, gm_ref, gp_ref,
                  gs_ref, cs_ref, ms_ref):
     c = c_ref[0]
@@ -176,7 +191,7 @@
 def weight_kernel(c_ref, group_ref, xt_ref, gm_ref, pk_ref, recv_ref, out_ref):
     xt = xt_ref[...]
     out_ref[:, :HALF] = mm(xt, gm_ref[...])
-    out_ref[:, HALF:] = mm(xt, (pk_ref[...] + recv_ref[...]).astype(bf16))
+    out_ref[:, HALF:] = mm(xt, (pk_ref[...] + recv_ref[0:CHIP, :]).astype(bf16))
 
 
 def fold_kernel(c_ref, group_ref, in_ref, out_ref):
@@ -193,31 +208,41 @@
         out_ref[k] = total[2 * half:2 * half + 2, :]
 
 
-def place_kernel(c_ref, group_ref, in_ref, yk_ref, recv_ref, x_ref, bc_ref, y_ref):
+def place_kernel(c_ref, group_ref, in_ref, yk_ref, recv_ref, x_hbm, bc_hbm, y_hbm,
+                 x_ref, bc_ref, y_ref, sems):
+    c = c_ref[0]
+    own = pl.multiple_of(c * HALF, LD)
+    oth = pl.multiple_of((1 - c) * HALF, LD)
+    y_ref[:, pl.ds(own, HALF)] = yk_ref[...].astype(bf16)
+    y_ref[:, pl.ds(oth, LD)] = recv_ref[CHIP:CHIP + LD, :].astype(bf16)
+    y_ref[:, pl.ds(pl.multiple_of(oth + LD, LD), LD)] = recv_ref[CHIP + LD:, :].astype(bf16)
+    copies = [pltpu.make_async_copy(y_ref, y_hbm, sems.at[0])]
+    copies[0].start()
     for k in range(DP):
         for half in range(2):
             piece = in_ref[2 * k + half]
             x_ref[2 * k:2 * k + 2, half * HALF:(half + 1) * HALF] = piece[:, :HALF]
             bc_ref[2 * k:2 * k + 2, half * STATE:(half + 1) * STATE] = piece[:, HALF:]
-    c = c_ref[0]
-    own = pl.multiple_of(c * HALF, LD)
-    oth = pl.multiple_of((1 - c) * HALF, LD)
-    y_ref[:, pl.ds(own, HALF)] = yk_ref[...].astype(bf16)
-    y_ref[:, pl.ds(oth, LD)] = recv_ref[0:LD, :].astype(bf16)
-    y_ref[:, pl.ds(pl.multiple_of(oth + LD, LD), LD)] = recv_ref[LD:, :].astype(bf16)
-
-
-def whole(shape):
-    return pl.BlockSpec(shape, lambda i, c, g: (0,) * len(shape))
-
-
-def call(kernel, place, outs, ins, scratch=(), specs=None):
+    copies.append(pltpu.make_async_copy(x_ref, x_hbm, sems.at[1]))
+    copies.append(pltpu.make_async_copy(bc_ref, bc_hbm, sems.at[2]))
+    for copy in copies[1:]:
+        copy.start()
+    for copy in copies:
+        copy.wait()
+
+
+vmem = pl.BlockSpec(memory_space=pltpu.VMEM)
+smem = pl.BlockSpec(memory_space=pltpu.SMEM)
+anywhere = pl.BlockSpec(memory_space=pl.ANY)
+
+
+def call(kernel, place, outs, ins, scratch=(), in_hbm=(), out_hbm=False):
     return pl.pallas_call(
         kernel,
         out_shape=[jax.ShapeDtypeStruct(s, d) for s, d in outs],
-        grid_spec=pltpu.PrefetchScalarGridSpec(
-            num_scalar_prefetch=2, grid=(1,), in_specs=specs or [whole(a.shape) for a in ins],
-            out_specs=[whole(s) for s, _ in outs], scratch_shapes=list(scratch)),
+        in_specs=[smem, smem] + [anywhere if k in in_hbm else vmem for k in range(len(ins))],
+        out_specs=[anywhere if out_hbm else vmem for _ in outs],
+        scratch_shapes=list(scratch),
         compiler_params=pltpu.CompilerParams(vmem_limit_bytes=16 * 1024 * 1024),
     )(*place, *ins)
 
@@ -238,30 +263,27 @@
     near = [[GROUP * a + b for b in range(GROUP)] for a in range(GROUPS)]
     across = [[GROUP * a + (a + b) % GROUP for a in range(GROUPS)] for b in range(GROUP)]
 
-    here = pl.BlockSpec((LD, HALF), lambda i, c, g: (0, c[0]))
-    there = pl.BlockSpec((LD, HALF), lambda i, c, g: (0, 1 - c[0]))
     x, g, codes, wx, wbc = (
         pltpu.with_memory_space_constraint(a, pltpu.MemorySpace.HBM)
         for a in (x, g, codes, x_weight, bc_weight))
-    (pack,) = call(
-        pack_kernel, place, [((LD, d + HALF + LD), f32)], (x, g, codes), (),
-        [whole(x.shape), there, whole(codes.shape)])
+    half = (LD, HALF)
+    pack, xv, gv, cv = call(
+        pack_kernel, place,
+        [((LD, d + HALF + LD), f32), ((LD, d), bf16), (half, bf16), ((HEADS, LD), f32)], (x, g, codes),
+        [pltpu.VMEM(half, bf16), pltpu.VMEM((HEADS, LD), jnp.int32), pltpu.SemaphoreType.DMA((4,))],
+        (0, 1, 2))
     pack = lax.ppermute(pack, "c", swap)
-    half = (LD, HALF)
     owned = call(
         own_kernel, place,
-        [(half, bf16), ((LD, 2 * STATE), bf16), (half, bf16), ((HEADS, LD), f32), ((LD, d), bf16),
-         ((d, HALF), bf16), ((d, 2 * STATE), bf16)],
-        (x, g, codes, wx, wbc), (),
-        [whole(x.shape), here, whole(codes.shape), pl.BlockSpec((d, HALF), lambda i, c, g: (0, c[0])),
-         whole(wbc.shape)])
+        [(half, bf16), ((LD, 2 * STATE), bf16), ((d, HALF), bf16), ((d, 2 * STATE), bf16)],
+        (xv, wx, wbc), [pltpu.SemaphoreType.DMA((2,))], (1, 2))
 
     sq = (CHIP, HALF)
     pay, ue, v, en, te, proj, xc, yl, gml, gpl = call(
         lambda *refs: local_kernel(unit, *refs), place,
         [((GROUP, 2 * HEAD + 8, STATE), f32), (sq, bf16), (sq, bf16), (sq, f32), (sq, f32),
          ((CHIP, 2 * STATE), bf16), ((CHIP, d), bf16), (sq, f32), (sq, f32), ((CHIP, 2 * STATE), f32)],
-        (*owned, pack), [pltpu.VMEM(sq, f32), pltpu.VMEM((HEADS, CHIP), f32), pltpu.VMEM(sq, bf16)])
+        (*owned, xv, gv, cv, pack), [pltpu.VMEM(sq, f32), pltpu.VMEM((HEADS, CHIP), f32), pltpu.VMEM(sq, bf16)])
 
     pay = lax.all_to_all(pay, "z", 0, 0, tiled=True, axis_index_groups=near)
     (far,) = call(total_kernel, place, [((GROUPS, HEAD + 8, STATE), f32)], (pay,))
@@ -276,21 +298,17 @@
     recv = lax.ppermute(send, "c", swap)
     xt = xc.T.reshape(ZN, 2, DP, 2, CHIP).transpose(2, 0, 1, 3, 4).reshape(d, CHIP)
     width = HALF + STATE
-    top = pl.BlockSpec((CHIP, LD), lambda i, c, g: (0, 0))
-    low = pl.BlockSpec((CHIP, LD), lambda i, c, g: (1, 0))
-    (grad,) = call(
-        weight_kernel, place, [((d, width), f32)], (xt, gm, pk, recv), (),
-        [whole(xt.shape), whole(gm.shape), whole(pk.shape), top])
+    (grad,) = call(weight_kernel, place, [((d, width), f32)], (xt, gm, pk, recv))
 
     part = lax.all_to_all(grad.reshape(DP, d // DP, width), "dp", 0, 0, tiled=True)
     (part,) = call(fold_kernel, place, [((ZN, d // DP // ZN, width), f32)], (part,))
     part = lax.all_to_all(part, "z", 0, 0, tiled=True)
     (part,) = call(lambda *refs: spread_kernel(grad_scale, *refs), place, [((2 * DP, 2, width), f32)], (part,))
     part = lax.all_to_all(part, ("dp", "c"), 0, 0, tiled=True)
+    outs = [((2 * DP, 2 * HALF), f32), ((2 * DP, 2 * STATE), f32), ((LD, 2 * HALF), bf16)]
     x_grad, bc_grad, y = call(
-        place_kernel, place,
-        [((2 * DP, 2 * HALF), f32), ((2 * DP, 2 * STATE), f32), ((LD, 2 * HALF), bf16)], (part, yk, recv), (),
-        [whole(part.shape), whole(yk.shape), low])
+        place_kernel, place, outs, (part, yk, recv),
+        [pltpu.VMEM(s, t) for s, t in outs] + [pltpu.SemaphoreType.DMA((3,))], (), True)
     return y[None], x_grad, bc_grad
 
 

time: 122 us -> 122 us (level)
  no operation moved by 1% of the time
where the time goes in v5:
time: 122 us
  blocking collectives  99.7 us (82%)
  starting transfers between devices  14.5 us (12%)
  Pallas kernels  5.64 us (5%)
    all_to_all x1, blocking collectives, body(): lax.all_to_all(grad.reshape(DP, d // DP, width), 'dp', 0, 0, tiled=True)  28.2 us
    all_to_all x2, blocking collectives, body(): pay = lax.all_to_all(pay, 'z', 0, 0, tiled=True, axis_index_groups=near)  23.3 us
    all_to_all x1, blocking collectives, body(): far = lax.all_to_all(far, 'z', 0, 0, tiled=True, axis_index_groups=across)  19.3 us
    all_to_all x1, blocking collectives, body(): part = lax.all_to_all(part, 'z', 0, 0, tiled=True)  14.6 us
    all_to_all x1, blocking collectives, body(): part = lax.all_to_all(part, ('dp', 'c'), 0, 0, tiled=True)  14.4 us
    ppermute x1, starting transfers between devices, body(): pack = lax.ppermute(pack, 'c', swap)  8.79 us
    ppermute x1, starting transfers between devices, body(): recv = lax.ppermute(send, 'c', swap)  5.67 us
    pallas_call x10, Pallas kernels, call(): pl.pallas_call(kernel, out_shape=[jax.ShapeDtypeStruct(s, d) for s, d in...  5.64 us
  transfers between devices with their start and end apart: 2, of which 1 were waited for; matrix products, arithmetic and copies ran while one was open for 1% of the time, Pallas kernels for 1%

profile of v5, /device:TPU:1, one launch (start us, length us, event | category | flops | bytes accessed | tf_op | source)
XLA Modules:
  0.0 121.8 jit_solution(16542145264257284666)
XLA Ops:
  0.6 1.1 shard_map.76
  1.7 8.8 %collective-permute-start = (f32[128,1408]{1,0:T(8,128)S(1)}, f32[128,1408]{1,0:T(8,128)S(1)}, u32[]{:S(2)}, u32[]{:S(2)}) collective-permute-start(f32[128,1408]{1,0:T(8,128)S(1)} %get-tuple-element.39), channel_id=1, source_target_pairs={{0,1},{1,0},{2,3},{3,2},{4,5},{5,4},{6,7},{7,6},{8,9},{9,8},{10,11... | collective-permute-start | bytes 2162696 | tf_op jit(solution)/shard_map/ppermute | solution.py:275
  10.5 1.6 %shard_map.77 = (bf16[128,256]{1,0:T(8,128)(2,1)S(1)}, bf16[128,256]{1,0:T(8,128)(2,1)S(1)}, bf16[1024,256]{1,0:T(8,128)(2,1)S(1)}, bf16[1024,256]{1,0:T(8,128)(2,1)S(1)}) custom-call(s32[1]{0:T(128)} %bitcast.c_ref.refs_0_, s32[1]{0:T(128)} %bitcast.1.group_ref.refs_1_, bf16[128,1024]{1,0:T(8,128)(2,1)S(1)} %get-tuple-element.32.x_ref.refs_6_, ...), custom_call_target="tpu_custom_call" | custom-call | tf_op jit(solution)/shard_map/pallas_call | solution.py:240
  12.1 0.2 collective-permute-done.refs_9_
  12.3 1.3 %shard_map.78 = (f32[4,136,128]{2,1,0:T(8,128)S(1)}, bf16[256,256]{1,0:T(8,128)(2,1)S(1)}, bf16[256,256]{1,0:T(8,128)(2,1)S(1)}, f32[256,256]{1,0:T(8,128)S(1)},...) custom-call(s32[1]{0:T(128)} %bitcast.c_ref.refs_0_, ...), custom_call_target="tpu_custom_call" | custom-call | tf_op jit(solution)/shard_map/pallas_call | solution.py:240
  13.6 10.9 %all_to_all.30.in_ref = f32[4,136,128]{2,1,0:T(8,128)S(1)} all-to-all(f32[4,136,128]{2,1,0:T(8,128)S(1)} %get-tuple-element.41), channel_id=1, replica_groups={{0,2,4,6},{8,10,12,14},{16,18,20,22},{24,26,28,30},{1,3,5,7},{9,11,13,1..., dimensions={0} | all-to-all | bytes 557056 | tf_op jit(solution)/shard_map/all_to_all | solution.py:288
  24.5 19.3 %all_to_all.31.far_ref = f32[4,72,128]{2,1,0:T(8,128)S(1)} all-to-all(f32[4,72,128]{2,1,0:T(8,128)S(1)} %shard_map.79), channel_id=1, replica_groups={{0,10,20,30},{2,12,22,24},{4,14,16,26},{6,8,18,28},{1,11,21,31},{3,13,2..., dimensions={0} | all-to-all | bytes 294912 | tf_op jit(solution)/shard_map/all_to_all | solution.py:290
  43.9 12.4 %all_to_all.32.refs_2_ = f32[4,128,128]{2,1,0:T(8,128)S(1)} all-to-all(f32[4,128,128]{2,1,0:T(8,128)S(1)} %shard_map.80), channel_id=1, replica_groups={{0,2,4,6},{8,10,12,14},{16,18,20,22},{24,26,28,30},{1,3,5,7},{9,11,13,1..., dimensions={0} | all-to-all | bytes 524288 | tf_op jit(solution)/shard_map/all_to_all | solution.py:292
  56.3 0.3 shard_map.81
  56.6 5.7 %collective-permute-start.1 = (f32[512,128]{1,0:T(8,128)S(1)}, f32[512,128]{1,0:T(8,128)S(1)}, u32[]{:S(2)}, u32[]{:S(2)}) collective-permute-start(f32[512,128]{1,0:T(8,128)S(1)} %get-tuple-element.52), channel_id=1, source_target_pairs={{0,1},{1,0},{2,3},{3,2},{4,5},{5,4},{6,7},{7,6},{8,9},{9,8},{10,11... | collective-permute-start | bytes 786440 | tf_op jit(solution)/shard_map/ppermute | solution.py:298
  62.3 0.2 copy.9
  62.5 0.2 reshape.23
  62.7 0.5 copy.10
  63.2 0.2 reshape.24.xt_ref
  63.4 0.0 collective-permute-done.1.recv_ref
  63.4 0.4 shard_map.82
  63.9 28.2 %all_to_all.33.in_ref = f32[16,64,384]{2,1,0:T(8,128)S(1)} all-to-all(f32[16,64,384]{2,1,0:T(8,128)S(1)} %bitcast.11), channel_id=1, replica_groups=mesh['dp'=16,'z'=16,'c'=2] {'dp'}, dimensions={0} | all-to-all | bytes 3145728 | tf_op jit(solution)/shard_map/all_to_all | solution.py:303
  92.0 0.1 shard_map.83
  92.1 14.6 %all_to_all.34.refs_2_ = f32[16,4,384]{2,1,0:T(4,128)S(1)} all-to-all(f32[16,4,384]{2,1,0:T(4,128)S(1)} %shard_map.83), channel_id=1, replica_groups=mesh['dp'=16,'z'=16,'c'=2] {'z'}, dimensions={0} | all-to-all | bytes 196608 | tf_op jit(solution)/shard_map/all_to_all | solution.py:305
  106.7 14.4 %all_to_all.35.in_ref = f32[32,2,384]{2,1,0:T(2,128)S(1)} all-to-all(f32[32,2,384]{2,1,0:T(2,128)S(1)} %shard_map.84), channel_id=1, replica_groups=mesh['dp'=16,'z'=16,'c'=2] {'dp','c'}, dimensions={0} | all-to-all | bytes 196608 | tf_op jit(solution)/shard_map/all_to_all | solution.py:307
  121.1 0.7 shard_map.85
  (3 shorter events, 0.1 us)
Async XLA Ops:
  1.7 10.6 %collective-permute-start = (f32[128,1408]{1,0:T(8,128)S(1)}, f32[128,1408]{1,0:T(8,128)S(1)}, u32[]{:S(2)}, u32[]{:S(2)}) collective-permute-start(f32[128,1408]{1,0:T(8,128)S(1)} %get-tuple-element.39), channel_id=1, source_target_pairs={{0,1},{1,0},{2,3},{3,2},{4,5},{5,4},{6,7},{7,6},{8,9},{9,8},{10,11... | collective-permute-start | bytes 2162696 | tf_op jit(solution)/shard_map/ppermute | solution.py:275
  56.6 6.8 %collective-permute-start.1 = (f32[512,128]{1,0:T(8,128)S(1)}, f32[512,128]{1,0:T(8,128)S(1)}, u32[]{:S(2)}, u32[]{:S(2)}) collective-permute-start(f32[512,128]{1,0:T(8,128)S(1)} %get-tuple-element.52), channel_id=1, source_target_pairs={{0,1},{1,0},{2,3},{3,2},{4,5},{5,4},{6,7},{7,6},{8,9},{9,8},{10,11... | collective-permute-start | bytes 786440 | tf_op jit(solution)/shard_map/ppermute | solution.py:298

commit v6 on v4

--- a/solution.py
+++ b/solution.py
@@ -180,25 +180,30 @@
 
 
 def fold_kernel(c_ref, group_ref, in_ref, out_ref):
-    total = jnp.sum(in_ref[...], axis=0)
+    width = in_ref.shape[2]
     step = out_ref.shape[1]
-    for k in range(ZN):
-        out_ref[k] = total[k * step:(k + 1) * step, :]
+    for half in range(2):
+        total = in_ref[half]
+        for k in range(1, DP):
+            total = total + in_ref[2 * k + half]
+        for k in range(ZN):
+            out_ref[k, :, half * width:(half + 1) * width] = total[k * step:(k + 1) * step, :]
 
 
 def spread_kernel(scale, c_ref, group_ref, in_ref, out_ref):
     total = scale * jnp.sum(in_ref[...], axis=0)
-    for k in range(2 * DP):
-        half = k % 2
-        out_ref[k] = total[2 * half:2 * half + 2, :]
+    for k in range(DP):
+        out_ref[k] = total
 
 
 def place_kernel(c_ref, group_ref, in_ref, yk_ref, recv_ref, x_ref, bc_ref, y_ref):
+    width = HALF + STATE
     for k in range(DP):
+        piece = in_ref[k]
         for half in range(2):
-            piece = in_ref[2 * k + half]
-            x_ref[2 * k:2 * k + 2, half * HALF:(half + 1) * HALF] = piece[:, :HALF]
-            bc_ref[2 * k:2 * k + 2, half * STATE:(half + 1) * STATE] = piece[:, HALF:]
+            at = half * width
+            x_ref[2 * k:2 * k + 2, half * HALF:(half + 1) * HALF] = piece[:, at:at + HALF]
+            bc_ref[2 * k:2 * k + 2, half * STATE:(half + 1) * STATE] = piece[:, at + HALF:at + width]
     c = c_ref[0]
     own = pl.multiple_of(c * HALF, LD)
     oth = pl.multiple_of((1 - c) * HALF, LD)
@@ -274,7 +279,7 @@
         [(sq, bf16), ((CHIP, STATE), f32), ((LD, HALF), f32), ((2 * CHIP, LD), f32)],
         (pay, ue, v, en, te, proj, yl, gml, gpl), [pltpu.VMEM(sq, f32)])
     recv = lax.ppermute(send, "c", swap)
-    xt = xc.T.reshape(ZN, 2, DP, 2, CHIP).transpose(2, 0, 1, 3, 4).reshape(d, CHIP)
+    xt = xc.T.reshape(ZN, 2, DP, 2, CHIP).transpose(2, 1, 0, 3, 4).reshape(d, CHIP)
     width = HALF + STATE
     top = pl.BlockSpec((CHIP, LD), lambda i, c, g: (0, 0))
     low = pl.BlockSpec((CHIP, LD), lambda i, c, g: (1, 0))
@@ -282,11 +287,12 @@
         weight_kernel, place, [((d, width), f32)], (xt, gm, pk, recv), (),
         [whole(xt.shape), whole(gm.shape), whole(pk.shape), top])
 
-    part = lax.all_to_all(grad.reshape(DP, d // DP, width), "dp", 0, 0, tiled=True)
-    (part,) = call(fold_kernel, place, [((ZN, d // DP // ZN, width), f32)], (part,))
+    rows = d // DP // 2
+    part = lax.all_to_all(grad.reshape(2 * DP, rows, width), ("dp", "c"), 0, 0, tiled=True)
+    (part,) = call(fold_kernel, place, [((ZN, rows // ZN, 2 * width), f32)], (part,))
     part = lax.all_to_all(part, "z", 0, 0, tiled=True)
-    (part,) = call(lambda *refs: spread_kernel(grad_scale, *refs), place, [((2 * DP, 2, width), f32)], (part,))
-    part = lax.all_to_all(part, ("dp", "c"), 0, 0, tiled=True)
+    (part,) = call(lambda *refs: spread_kernel(grad_scale, *refs), place, [((DP, rows // ZN, 2 * width), f32)], (part,))
+    part = lax.all_to_all(part, "dp", 0, 0, tiled=True)
     x_grad, bc_grad, y = call(
         place_kernel, place,
         [((2 * DP, 2 * HALF), f32), ((2 * DP, 2 * STATE), f32), ((LD, 2 * HALF), bf16)], (part, yk, recv), (),

time: 122 us -> 121 us (level)
  the two profiles are of different devices: /device:TPU:1 before, /device:TPU:32 now
where the time goes in v6:
time: 121 us
  blocking collectives  109 us (90%)
  Pallas kernels  5.72 us (5%)
  starting transfers between devices  3.84 us (3%)
    all_to_all x1, blocking collectives, body(): lax.all_to_all(grad.reshape(2 * DP, rows, width), ('dp', 'c'), 0, 0, tile...  29.5 us
    all_to_all x2, blocking collectives, body(): pay = lax.all_to_all(pay, 'z', 0, 0, tiled=True, axis_index_groups=near)  26.5 us
    all_to_all x1, blocking collectives, body(): far = lax.all_to_all(far, 'z', 0, 0, tiled=True, axis_index_groups=across)  23.2 us
    all_to_all x1, blocking collectives, body(): part = lax.all_to_all(part, 'z', 0, 0, tiled=True)  18.6 us
    all_to_all x1, blocking collectives, body(): part = lax.all_to_all(part, 'dp', 0, 0, tiled=True)  10.9 us
    pallas_call x10, Pallas kernels, call(): pl.pallas_call(kernel, out_shape=[jax.ShapeDtypeStruct(s, d) for s, d in...  5.72 us
  transfers between devices with their start and end apart: 2, of which 2 were waited for; matrix products, arithmetic and copies ran while one was open for 1% of the time, Pallas kernels for 1%

profile of v6, /device:TPU:32, one launch (start us, length us, event | category | flops | bytes accessed | tf_op | source)
XLA Modules:
  0.0 120.8 jit_solution(10746496710130560279)
XLA Ops:
  0.6 1.0 shard_map.77
  1.7 1.9 %collective-permute-start = (f32[128,1408]{1,0:T(8,128)S(1)}, f32[128,1408]{1,0:T(8,128)S(1)}, u32[]{:S(2)}, u32[]{:S(2)}) collective-permute-start(f32[128,1408]{1,0:T(8,128)S(1)} %shard_map.77), channel_id=1, source_target_pairs={{0,1},{1,0},{2,3},{3,2},{4,5},{5,4},{6,7},{7,6},{8,9},{9,8},{10,11... | collective-permute-start | bytes 2162696 | tf_op jit(solution)/shard_map/ppermute | solution.py:254
  3.6 1.7 %shard_map.76 = (bf16[128,256]{1,0:T(8,128)(2,1)S(1)}, bf16[128,256]{1,0:T(8,128)(2,1)S(1)}, bf16[128,256]{1,0:T(8,128)(2,1)S(1)}, f32[8,128]{1,0:T(8,128)S(1)},...) custom-call(s32[1]{0:T(128)} %bitcast.c_ref.refs_0_, ...), custom_call_target="tpu_custom_call" | custom-call | tf_op jit(solution)/shard_map/pallas_call | solution.py:220
  5.3 0.4 collective-permute-done.refs_9_
  5.8 1.3 %shard_map.78 = (f32[4,136,128]{2,1,0:T(8,128)S(1)}, bf16[256,256]{1,0:T(8,128)(2,1)S(1)}, bf16[256,256]{1,0:T(8,128)(2,1)S(1)}, f32[256,256]{1,0:T(8,128)S(1)},...) custom-call(s32[1]{0:T(128)} %bitcast.c_ref.refs_0_, ...), custom_call_target="tpu_custom_call" | custom-call | tf_op jit(solution)/shard_map/pallas_call | solution.py:220
  7.1 16.1 %all_to_all.30.in_ref = f32[4,136,128]{2,1,0:T(8,128)S(1)} all-to-all(f32[4,136,128]{2,1,0:T(8,128)S(1)} %get-tuple-element.39), channel_id=1, replica_groups={{0,2,4,6},{8,10,12,14},{16,18,20,22},{24,26,28,30},{1,3,5,7},{9,11,13,1..., dimensions={0} | all-to-all | bytes 557056 | tf_op jit(solution)/shard_map/all_to_all | solution.py:271
  23.2 23.2 %all_to_all.31.far_ref = f32[4,72,128]{2,1,0:T(8,128)S(1)} all-to-all(f32[4,72,128]{2,1,0:T(8,128)S(1)} %shard_map.79), channel_id=1, replica_groups={{0,10,20,30},{2,12,22,24},{4,14,16,26},{6,8,18,28},{1,11,21,31},{3,13,2..., dimensions={0} | all-to-all | bytes 294912 | tf_op jit(solution)/shard_map/all_to_all | solution.py:273
  46.5 10.3 %all_to_all.32.refs_2_ = f32[4,128,128]{2,1,0:T(8,128)S(1)} all-to-all(f32[4,128,128]{2,1,0:T(8,128)S(1)} %shard_map.80), channel_id=1, replica_groups={{0,2,4,6},{8,10,12,14},{16,18,20,22},{24,26,28,30},{1,3,5,7},{9,11,13,1..., dimensions={0} | all-to-all | bytes 524288 | tf_op jit(solution)/shard_map/all_to_all | solution.py:275
  56.8 0.3 shard_map.81
  57.1 1.9 %collective-permute-start.1 = (f32[512,128]{1,0:T(8,128)S(1)}, f32[512,128]{1,0:T(8,128)S(1)}, u32[]{:S(2)}, u32[]{:S(2)}) collective-permute-start(f32[512,128]{1,0:T(8,128)S(1)} %get-tuple-element.50), channel_id=1, source_target_pairs={{0,1},{1,0},{2,3},{3,2},{4,5},{5,4},{6,7},{7,6},{8,9},{9,8},{10,11... | collective-permute-start | bytes 786440 | tf_op jit(solution)/shard_map/ppermute | solution.py:281
  59.1 0.2 copy.9
  59.3 0.2 reshape.23
  59.5 0.5 copy.10
  60.0 0.2 reshape.24.xt_ref
  60.2 0.3 collective-permute-done.1.recv_ref
  60.6 0.4 shard_map.82
  61.0 29.5 %all_to_all.33.in_ref = f32[32,32,384]{2,1,0:T(8,128)S(1)} all-to-all(f32[32,32,384]{2,1,0:T(8,128)S(1)} %bitcast.11), channel_id=1, replica_groups=mesh['dp'=16,'z'=16,'c'=2] {'dp','c'}, dimensions={0} | all-to-all | bytes 3145728 | tf_op jit(solution)/shard_map/all_to_all | solution.py:291
  90.5 0.1 shard_map.83
  90.6 18.6 %all_to_all.34.refs_2_ = f32[16,2,768]{2,1,0:T(2,128)S(1)} all-to-all(f32[16,2,768]{2,1,0:T(2,128)S(1)} %shard_map.83), channel_id=1, replica_groups=mesh['dp'=16,'z'=16,'c'=2] {'z'}, dimensions={0} | all-to-all | bytes 196608 | tf_op jit(solution)/shard_map/all_to_all | solution.py:293
  109.2 0.1 shard_map.84
  109.2 10.9 %all_to_all.35.in_ref = f32[16,2,768]{2,1,0:T(2,128)S(1)} all-to-all(f32[16,2,768]{2,1,0:T(2,128)S(1)} %shard_map.84), channel_id=1, replica_groups=mesh['dp'=16,'z'=16,'c'=2] {'dp'}, dimensions={0} | all-to-all | bytes 196608 | tf_op jit(solution)/shard_map/all_to_all | solution.py:295
  120.1 0.7 shard_map.85
  (2 shorter events, 0.1 us)
Async XLA Ops:
  1.7 4.1 %collective-permute-start = (f32[128,1408]{1,0:T(8,128)S(1)}, f32[128,1408]{1,0:T(8,128)S(1)}, u32[]{:S(2)}, u32[]{:S(2)}) collective-permute-start(f32[128,1408]{1,0:T(8,128)S(1)} %shard_map.77), channel_id=1, source_target_pairs={{0,1},{1,0},{2,3},{3,2},{4,5},{5,4},{6,7},{7,6},{8,9},{9,8},{10,11... | collective-permute-start | bytes 2162696 | tf_op jit(solution)/shard_map/ppermute | solution.py:254
  57.1 3.4 %collective-permute-start.1 = (f32[512,128]{1,0:T(8,128)S(1)}, f32[512,128]{1,0:T(8,128)S(1)}, u32[]{:S(2)}, u32[]{:S(2)}) collective-permute-start(f32[512,128]{1,0:T(8,128)S(1)} %get-tuple-element.50), channel_id=1, source_target_pairs={{0,1},{1,0},{2,3},{3,2},{4,5},{5,4},{6,7},{7,6},{8,9},{9,8},{10,11... | collective-permute-start | bytes 786440 | tf_op jit(solution)/shard_map/ppermute | solution.py:281

commit v7 on v6

--- a/solution.py
+++ b/solution.py
@@ -180,20 +180,21 @@
 
 
 def fold_kernel(c_ref, group_ref, in_ref, out_ref):
+    total = jnp.sum(in_ref[...], axis=0)
+    step = out_ref.shape[1]
+    for k in range(2 * ZN):
+        out_ref[k] = total[k * step:(k + 1) * step, :]
+
+
+def spread_kernel(scale, c_ref, group_ref, in_ref, out_ref):
     width = in_ref.shape[2]
-    step = out_ref.shape[1]
     for half in range(2):
         total = in_ref[half]
-        for k in range(1, DP):
+        for k in range(1, ZN):
             total = total + in_ref[2 * k + half]
-        for k in range(ZN):
-            out_ref[k, :, half * width:(half + 1) * width] = total[k * step:(k + 1) * step, :]
-
-
-def spread_kernel(scale, c_ref, group_ref, in_ref, out_ref):
-    total = scale * jnp.sum(in_ref[...], axis=0)
-    for k in range(DP):
-        out_ref[k] = total
+        total = scale * total
+        for k in range(DP):
+            out_ref[k, :, half * width:(half + 1) * width] = total
 
 
 def place_kernel(c_ref, group_ref, in_ref, yk_ref, recv_ref, x_ref, bc_ref, y_ref):
@@ -279,7 +280,7 @@
         [(sq, bf16), ((CHIP, STATE), f32), ((LD, HALF), f32), ((2 * CHIP, LD), f32)],
         (pay, ue, v, en, te, proj, yl, gml, gpl), [pltpu.VMEM(sq, f32)])
     recv = lax.ppermute(send, "c", swap)
-    xt = xc.T.reshape(ZN, 2, DP, 2, CHIP).transpose(2, 1, 0, 3, 4).reshape(d, CHIP)
+    xt = xc.T.reshape(ZN, 2, DP, 2, CHIP).transpose(2, 0, 1, 3, 4).reshape(d, CHIP)
     width = HALF + STATE
     top = pl.BlockSpec((CHIP, LD), lambda i, c, g: (0, 0))
     low = pl.BlockSpec((CHIP, LD), lambda i, c, g: (1, 0))
@@ -287,11 +288,12 @@
         weight_kernel, place, [((d, width), f32)], (xt, gm, pk, recv), (),
         [whole(xt.shape), whole(gm.shape), whole(pk.shape), top])
 
-    rows = d // DP // 2
-    part = lax.all_to_all(grad.reshape(2 * DP, rows, width), ("dp", "c"), 0, 0, tiled=True)
-    (part,) = call(fold_kernel, place, [((ZN, rows // ZN, 2 * width), f32)], (part,))
-    part = lax.all_to_all(part, "z", 0, 0, tiled=True)
-    (part,) = call(lambda *refs: spread_kernel(grad_scale, *refs), place, [((DP, rows // ZN, 2 * width), f32)], (part,))
+    rows = d // DP
+    step = rows // ZN // 2
+    part = lax.all_to_all(grad.reshape(DP, rows, width), "dp", 0, 0, tiled=True)
+    (part,) = call(fold_kernel, place, [((2 * ZN, step, width), f32)], (part,))
+    part = lax.all_to_all(part, ("z", "c"), 0, 0, tiled=True)
+    (part,) = call(lambda *refs: spread_kernel(grad_scale, *refs), place, [((DP, step, 2 * width), f32)], (part,))
     part = lax.all_to_all(part, "dp", 0, 0, tiled=True)
     x_grad, bc_grad, y = call(
         place_kernel, place,

time: 121 us -> 123 us (1.017)
  the two profiles are of different devices: /device:TPU:32 before, /device:TPU:2 now
where the time goes in v7:
time: 123 us
  blocking collectives  110 us (89%)
  Pallas kernels  5.7 us (5%)
  starting transfers between devices  3.84 us (3%)
    all_to_all x1, blocking collectives, body(): part = lax.all_to_all(grad.reshape(DP, rows, width), 'dp', 0, 0, tiled=True)  28 us
    all_to_all x2, blocking collectives, body(): pay = lax.all_to_all(pay, 'z', 0, 0, tiled=True, axis_index_groups=near)  27.7 us
    all_to_all x1, blocking collectives, body(): far = lax.all_to_all(far, 'z', 0, 0, tiled=True, axis_index_groups=across)  23.7 us
    all_to_all x1, blocking collectives, body(): part = lax.all_to_all(part, ('z', 'c'), 0, 0, tiled=True)  19.1 us
    all_to_all x1, blocking collectives, body(): part = lax.all_to_all(part, 'dp', 0, 0, tiled=True)  11.9 us
    pallas_call x10, Pallas kernels, call(): pl.pallas_call(kernel, out_shape=[jax.ShapeDtypeStruct(s, d) for s, d in...  5.7 us
  transfers between devices with their start and end apart: 2, of which 2 were waited for; matrix products, arithmetic and copies ran while one was open for 1% of the time, Pallas kernels for 1%

profile of v7, /device:TPU:2, one launch (start us, length us, event | category | flops | bytes accessed | tf_op | source)
XLA Modules:
  0.0 122.6 jit_solution(6302881219951166082)
XLA Ops:
  0.6 1.0 shard_map.77
  1.7 1.9 %collective-permute-start = (f32[128,1408]{1,0:T(8,128)S(1)}, f32[128,1408]{1,0:T(8,128)S(1)}, u32[]{:S(2)}, u32[]{:S(2)}) collective-permute-start(f32[128,1408]{1,0:T(8,128)S(1)} %shard_map.77), channel_id=1, source_target_pairs={{0,1},{1,0},{2,3},{3,2},{4,5},{5,4},{6,7},{7,6},{8,9},{9,8},{10,11... | collective-permute-start | bytes 2162696 | tf_op jit(solution)/shard_map/ppermute | solution.py:255
  3.6 1.7 %shard_map.76 = (bf16[128,256]{1,0:T(8,128)(2,1)S(1)}, bf16[128,256]{1,0:T(8,128)(2,1)S(1)}, bf16[128,256]{1,0:T(8,128)(2,1)S(1)}, f32[8,128]{1,0:T(8,128)S(1)},...) custom-call(s32[1]{0:T(128)} %bitcast.c_ref.refs_0_, ...), custom_call_target="tpu_custom_call" | custom-call | tf_op jit(solution)/shard_map/pallas_call | solution.py:221
  5.3 0.4 collective-permute-done.refs_9_
  5.8 1.3 %shard_map.78 = (f32[4,136,128]{2,1,0:T(8,128)S(1)}, bf16[256,256]{1,0:T(8,128)(2,1)S(1)}, bf16[256,256]{1,0:T(8,128)(2,1)S(1)}, f32[256,256]{1,0:T(8,128)S(1)},...) custom-call(s32[1]{0:T(128)} %bitcast.c_ref.refs_0_, ...), custom_call_target="tpu_custom_call" | custom-call | tf_op jit(solution)/shard_map/pallas_call | solution.py:221
  7.1 15.2 %all_to_all.30.in_ref = f32[4,136,128]{2,1,0:T(8,128)S(1)} all-to-all(f32[4,136,128]{2,1,0:T(8,128)S(1)} %get-tuple-element.39), channel_id=1, replica_groups={{0,2,4,6},{8,10,12,14},{16,18,20,22},{24,26,28,30},{1,3,5,7},{9,11,13,1..., dimensions={0} | all-to-all | bytes 557056 | tf_op jit(solution)/shard_map/all_to_all | solution.py:272
  22.3 23.7 %all_to_all.31.far_ref = f32[4,72,128]{2,1,0:T(8,128)S(1)} all-to-all(f32[4,72,128]{2,1,0:T(8,128)S(1)} %shard_map.79), channel_id=1, replica_groups={{0,10,20,30},{2,12,22,24},{4,14,16,26},{6,8,18,28},{1,11,21,31},{3,13,2..., dimensions={0} | all-to-all | bytes 294912 | tf_op jit(solution)/shard_map/all_to_all | solution.py:274
  46.1 12.4 %all_to_all.32.refs_2_ = f32[4,128,128]{2,1,0:T(8,128)S(1)} all-to-all(f32[4,128,128]{2,1,0:T(8,128)S(1)} %shard_map.80), channel_id=1, replica_groups={{0,2,4,6},{8,10,12,14},{16,18,20,22},{24,26,28,30},{1,3,5,7},{9,11,13,1..., dimensions={0} | all-to-all | bytes 524288 | tf_op jit(solution)/shard_map/all_to_all | solution.py:276
  58.5 0.3 shard_map.81
  58.8 1.9 %collective-permute-start.1 = (f32[512,128]{1,0:T(8,128)S(1)}, f32[512,128]{1,0:T(8,128)S(1)}, u32[]{:S(2)}, u32[]{:S(2)}) collective-permute-start(f32[512,128]{1,0:T(8,128)S(1)} %get-tuple-element.50), channel_id=1, source_target_pairs={{0,1},{1,0},{2,3},{3,2},{4,5},{5,4},{6,7},{7,6},{8,9},{9,8},{10,11... | collective-permute-start | bytes 786440 | tf_op jit(solution)/shard_map/ppermute | solution.py:282
  60.8 0.2 copy.9
  61.0 0.2 reshape.23
  61.2 0.5 copy.10
  61.7 0.2 reshape.24.xt_ref
  61.9 0.4 collective-permute-done.1.recv_ref
  62.3 0.4 shard_map.82
  62.7 28.0 %all_to_all.33.in_ref = f32[16,64,384]{2,1,0:T(8,128)S(1)} all-to-all(f32[16,64,384]{2,1,0:T(8,128)S(1)} %bitcast.11), channel_id=1, replica_groups=mesh['dp'=16,'z'=16,'c'=2] {'dp'}, dimensions={0} | all-to-all | bytes 3145728 | tf_op jit(solution)/shard_map/all_to_all | solution.py:293
  90.7 0.1 shard_map.83
  90.8 19.1 %all_to_all.34.refs_2_ = f32[32,2,384]{2,1,0:T(2,128)S(1)} all-to-all(f32[32,2,384]{2,1,0:T(2,128)S(1)} %shard_map.83), channel_id=1, replica_groups=mesh['dp'=16,'z'=16,'c'=2] {'z','c'}, dimensions={0} | all-to-all | bytes 196608 | tf_op jit(solution)/shard_map/all_to_all | solution.py:295
  110.0 11.9 %all_to_all.35.in_ref = f32[16,2,768]{2,1,0:T(2,128)S(1)} all-to-all(f32[16,2,768]{2,1,0:T(2,128)S(1)} %shard_map.84), channel_id=1, replica_groups=mesh['dp'=16,'z'=16,'c'=2] {'dp'}, dimensions={0} | all-to-all | bytes 196608 | tf_op jit(solution)/shard_map/all_to_all | solution.py:297
  121.8 0.7 shard_map.85
  (3 shorter events, 0.1 us)
Async XLA Ops:
  1.7 4.1 %collective-permute-start = (f32[128,1408]{1,0:T(8,128)S(1)}, f32[128,1408]{1,0:T(8,128)S(1)}, u32[]{:S(2)}, u32[]{:S(2)}) collective-permute-start(f32[128,1408]{1,0:T(8,128)S(1)} %shard_map.77), channel_id=1, source_target_pairs={{0,1},{1,0},{2,3},{3,2},{4,5},{5,4},{6,7},{7,6},{8,9},{9,8},{10,11... | collective-permute-start | bytes 2162696 | tf_op jit(solution)/shard_map/ppermute | solution.py:255
  58.8 3.4 %collective-permute-start.1 = (f32[512,128]{1,0:T(8,128)S(1)}, f32[512,128]{1,0:T(8,128)S(1)}, u32[]{:S(2)}, u32[]{:S(2)}) collective-permute-start(f32[512,128]{1,0:T(8,128)S(1)} %get-tuple-element.50), channel_id=1, source_target_pairs={{0,1},{1,0},{2,3},{3,2},{4,5},{5,4},{6,7},{7,6},{8,9},{9,8},{10,11... | collective-permute-start | bytes 786440 | tf_op jit(solution)/shard_map/ppermute | solution.py:282

commit v8 on v4

--- a/solution.py
+++ b/solution.py
@@ -162,21 +162,27 @@
     readout = proj_ref[:, STATE:]
     gi = scale * (gp_ref[:, :STATE] + mm(u_ref[...], adjoint))
     gr = scale * (gp_ref[:, STATE:] + mm(v_ref[...], carry))
-    pk_ref[...] = jnp.where(c == 0, gi, gr)
-    send_ref[0:CHIP, :] = jnp.where(c == 0, gr, gi)
-    grad = gml_ref[...] + te_ref[...] * mm_nt(inject, adjoint)
-    gm_ref[...] = (scale * grad).astype(bf16)
+    grad = scale * (gml_ref[...] + te_ref[...] * mm_nt(inject, adjoint))
+    gm_ref[...] = grad.astype(bf16)
+    pk_ref[:, :STATE] = gi
+    pk_ref[:, STATE:] = gr
+    send_ref[:, :HALF] = grad
+    send_ref[:, HALF:HALF + STATE] = gi
+    send_ref[:, HALF + STATE:2 * HALF] = gr
     y_ref[...] = yl_ref[...] + en_ref[...] * mm_nt(readout, carry)
     yk_ref[...] = y_ref[pl.ds(pl.multiple_of(c * LD, LD), LD), :]
     there = y_ref[pl.ds(pl.multiple_of((1 - c) * LD, LD), LD), :]
-    send_ref[CHIP:CHIP + LD, :] = there[:, :LD]
-    send_ref[CHIP + LD:, :] = there[:, LD:]
+    send_ref[0:LD, 2 * HALF:] = there[:, :LD]
+    send_ref[LD:, 2 * HALF:] = there[:, LD:]
 
 
 def weight_kernel(c_ref, group_ref, xt_ref, gm_ref, pk_ref, recv_ref, out_ref):
-    xt = xt_ref[...]
-    out_ref[:, :HALF] = mm(xt, gm_ref[...])
-    out_ref[:, HALF:] = mm(xt, (pk_ref[...] + recv_ref[...]).astype(bf16))
+    c = c_ref[0]
+    rows = out_ref.shape[0]
+    xt = xt_ref[pl.ds(pl.multiple_of(c * rows, rows), rows), :]
+    out_ref[:, pl.ds(pl.multiple_of(c * HALF, HALF), HALF)] = mm(xt, gm_ref[...])
+    out_ref[:, pl.ds(pl.multiple_of((1 - c) * HALF, HALF), HALF)] = mm(xt, recv_ref[:, :HALF].astype(bf16))
+    out_ref[:, 2 * HALF:] = mm(xt, (pk_ref[...] + recv_ref[:, HALF:2 * HALF]).astype(bf16))
 
 
 def fold_kernel(c_ref, group_ref, in_ref, out_ref):
@@ -188,17 +194,15 @@
 
 def spread_kernel(scale, c_ref, group_ref, in_ref, out_ref):
     total = scale * jnp.sum(in_ref[...], axis=0)
-    for k in range(2 * DP):
-        half = k % 2
-        out_ref[k] = total[2 * half:2 * half + 2, :]
+    for k in range(DP):
+        out_ref[k] = total
 
 
 def place_kernel(c_ref, group_ref, in_ref, yk_ref, recv_ref, x_ref, bc_ref, y_ref):
     for k in range(DP):
-        for half in range(2):
-            piece = in_ref[2 * k + half]
-            x_ref[2 * k:2 * k + 2, half * HALF:(half + 1) * HALF] = piece[:, :HALF]
-            bc_ref[2 * k:2 * k + 2, half * STATE:(half + 1) * STATE] = piece[:, HALF:]
+        piece = in_ref[k]
+        x_ref[2 * k:2 * k + 2, :] = piece[:, :2 * HALF]
+        bc_ref[2 * k:2 * k + 2, :] = piece[:, 2 * HALF:]
     c = c_ref[0]
     own = pl.multiple_of(c * HALF, LD)
     oth = pl.multiple_of((1 - c) * HALF, LD)
@@ -271,26 +275,23 @@
 
     gm, pk, yk, send = call(
         lambda *refs: outer_kernel(out_scale, *refs), place,
-        [(sq, bf16), ((CHIP, STATE), f32), ((LD, HALF), f32), ((2 * CHIP, LD), f32)],
+        [(sq, bf16), ((CHIP, 2 * STATE), f32), ((LD, HALF), f32), ((CHIP, 2 * HALF + LD), f32)],
         (pay, ue, v, en, te, proj, yl, gml, gpl), [pltpu.VMEM(sq, f32)])
     recv = lax.ppermute(send, "c", swap)
-    xt = xc.T.reshape(ZN, 2, DP, 2, CHIP).transpose(2, 0, 1, 3, 4).reshape(d, CHIP)
-    width = HALF + STATE
-    top = pl.BlockSpec((CHIP, LD), lambda i, c, g: (0, 0))
-    low = pl.BlockSpec((CHIP, LD), lambda i, c, g: (1, 0))
-    (grad,) = call(
-        weight_kernel, place, [((d, width), f32)], (xt, gm, pk, recv), (),
-        [whole(xt.shape), whole(gm.shape), whole(pk.shape), top])
-
-    part = lax.all_to_all(grad.reshape(DP, d // DP, width), "dp", 0, 0, tiled=True)
-    (part,) = call(fold_kernel, place, [((ZN, d // DP // ZN, width), f32)], (part,))
+    xt = xc.T.reshape(ZN, 2, DP, 2, CHIP).transpose(1, 2, 0, 3, 4).reshape(d, CHIP)
+    width = 2 * HALF + 2 * STATE
+    (grad,) = call(weight_kernel, place, [((d // 2, width), f32)], (xt, gm, pk, recv))
+
+    rows = d // 2 // DP
+    part = lax.all_to_all(grad.reshape(DP, rows, width), "dp", 0, 0, tiled=True)
+    (part,) = call(fold_kernel, place, [((ZN, rows // ZN, width), f32)], (part,))
     part = lax.all_to_all(part, "z", 0, 0, tiled=True)
-    (part,) = call(lambda *refs: spread_kernel(grad_scale, *refs), place, [((2 * DP, 2, width), f32)], (part,))
-    part = lax.all_to_all(part, ("dp", "c"), 0, 0, tiled=True)
+    (part,) = call(lambda *refs: spread_kernel(grad_scale, *refs), place, [((DP, rows // ZN, width), f32)], (part,))
+    part = lax.all_to_all(part, "dp", 0, 0, tiled=True)
     x_grad, bc_grad, y = call(
         place_kernel, place,
         [((2 * DP, 2 * HALF), f32), ((2 * DP, 2 * STATE), f32), ((LD, 2 * HALF), bf16)], (part, yk, recv), (),
-        [whole(part.shape), whole(yk.shape), low])
+        [whole(part.shape), whole(yk.shape), pl.BlockSpec((CHIP, LD), lambda i, c, g: (0, 2 * HALF // LD))])
     return y[None], x_grad, bc_grad
 
 

time: 122 us -> 121 us (level)
  the two profiles are of different devices: /device:TPU:1 before, /device:TPU:32 now
where the time goes in v8:
time: 121 us; the launch traced here: 120 us
  blocking collectives  108 us (89%)
  Pallas kernels  5.69 us (5%)
  starting transfers between devices  3.84 us (3%)
  waiting for transfers between devices  1.33 us (1%)
    all_to_all x1, blocking collectives, body(): part = lax.all_to_all(grad.reshape(DP, rows, width), 'dp', 0, 0, tiled=True)  29.9 us
    all_to_all x2, blocking collectives, body(): pay = lax.all_to_all(pay, 'z', 0, 0, tiled=True, axis_index_groups=near)  26.5 us
    all_to_all x1, blocking collectives, body(): far = lax.all_to_all(far, 'z', 0, 0, tiled=True, axis_index_groups=across)  23.2 us
    all_to_all x1, blocking collectives, body(): part = lax.all_to_all(part, 'z', 0, 0, tiled=True)  16.6 us
    all_to_all x1, blocking collectives, body(): part = lax.all_to_all(part, 'dp', 0, 0, tiled=True)  11.4 us
    pallas_call x10, Pallas kernels, call(): pl.pallas_call(kernel, out_shape=[jax.ShapeDtypeStruct(s, d) for s, d in...  5.69 us
  transfers between devices with their start and end apart: 2, of which 2 were waited for; matrix products, arithmetic and copies ran while one was open for 1% of the time, Pallas kernels for 1%

profile of v8, /device:TPU:32, one launch (start us, length us, event | category | flops | bytes accessed | tf_op | source)
XLA Modules:
  0.0 120.3 jit_solution(14264975655954321545)
XLA Ops:
  0.6 1.0 shard_map.77
  1.7 1.9 %collective-permute-start = (f32[128,1408]{1,0:T(8,128)S(1)}, f32[128,1408]{1,0:T(8,128)S(1)}, u32[]{:S(2)}, u32[]{:S(2)}) collective-permute-start(f32[128,1408]{1,0:T(8,128)S(1)} %shard_map.77), channel_id=1, source_target_pairs={{0,1},{1,0},{2,3},{3,2},{4,5},{5,4},{6,7},{7,6},{8,9},{9,8},{10,11... | collective-permute-start | bytes 2162696 | tf_op jit(solution)/shard_map/ppermute | solution.py:253
  3.6 1.7 %shard_map.76 = (bf16[128,256]{1,0:T(8,128)(2,1)S(1)}, bf16[128,256]{1,0:T(8,128)(2,1)S(1)}, bf16[128,256]{1,0:T(8,128)(2,1)S(1)}, f32[8,128]{1,0:T(8,128)S(1)},...) custom-call(s32[1]{0:T(128)} %bitcast.c_ref.refs_0_, ...), custom_call_target="tpu_custom_call" | custom-call | tf_op jit(solution)/shard_map/pallas_call | solution.py:219
  5.3 0.4 collective-permute-done.refs_9_
  5.8 1.3 %shard_map.78 = (f32[4,136,128]{2,1,0:T(8,128)S(1)}, bf16[256,256]{1,0:T(8,128)(2,1)S(1)}, bf16[256,256]{1,0:T(8,128)(2,1)S(1)}, f32[256,256]{1,0:T(8,128)S(1)},...) custom-call(s32[1]{0:T(128)} %bitcast.c_ref.refs_0_, ...), custom_call_target="tpu_custom_call" | custom-call | tf_op jit(solution)/shard_map/pallas_call | solution.py:219
  7.1 16.1 %all_to_all.30.in_ref = f32[4,136,128]{2,1,0:T(8,128)S(1)} all-to-all(f32[4,136,128]{2,1,0:T(8,128)S(1)} %get-tuple-element.39), channel_id=1, replica_groups={{0,2,4,6},{8,10,12,14},{16,18,20,22},{24,26,28,30},{1,3,5,7},{9,11,13,1..., dimensions={0} | all-to-all | bytes 557056 | tf_op jit(solution)/shard_map/all_to_all | solution.py:270
  23.2 23.2 %all_to_all.31.far_ref = f32[4,72,128]{2,1,0:T(8,128)S(1)} all-to-all(f32[4,72,128]{2,1,0:T(8,128)S(1)} %shard_map.79), channel_id=1, replica_groups={{0,10,20,30},{2,12,22,24},{4,14,16,26},{6,8,18,28},{1,11,21,31},{3,13,2..., dimensions={0} | all-to-all | bytes 294912 | tf_op jit(solution)/shard_map/all_to_all | solution.py:272
  46.5 10.3 %all_to_all.32.refs_2_ = f32[4,128,128]{2,1,0:T(8,128)S(1)} all-to-all(f32[4,128,128]{2,1,0:T(8,128)S(1)} %shard_map.80), channel_id=1, replica_groups={{0,2,4,6},{8,10,12,14},{16,18,20,22},{24,26,28,30},{1,3,5,7},{9,11,13,1..., dimensions={0} | all-to-all | bytes 524288 | tf_op jit(solution)/shard_map/all_to_all | solution.py:274
  56.8 0.3 shard_map.81
  57.1 1.9 %collective-permute-start.1 = (f32[256,640]{1,0:T(8,128)S(1)}, f32[256,640]{1,0:T(8,128)S(1)}, u32[]{:S(2)}, u32[]{:S(2)}) collective-permute-start(f32[256,640]{1,0:T(8,128)S(1)} %get-tuple-element.50), channel_id=1, source_target_pairs={{0,1},{1,0},{2,3},{3,2},{4,5},{5,4},{6,7},{7,6},{8,9},{9,8},{10,11... | collective-permute-start | bytes 1966088 | tf_op jit(solution)/shard_map/ppermute | solution.py:280
  59.1 0.2 copy.9
  59.3 0.2 reshape.23
  59.5 0.5 copy.10
  60.0 0.2 reshape.24.xt_ref
  60.2 0.9 collective-permute-done.1.recv_ref
  61.1 0.4 shard_map.82
  61.5 29.9 %all_to_all.33.in_ref = f32[16,32,768]{2,1,0:T(8,128)S(1)} all-to-all(f32[16,32,768]{2,1,0:T(8,128)S(1)} %bitcast.11), channel_id=1, replica_groups=mesh['dp'=16,'z'=16,'c'=2] {'dp'}, dimensions={0} | all-to-all | bytes 3145728 | tf_op jit(solution)/shard_map/all_to_all | solution.py:286
  91.4 0.1 shard_map.83
  91.5 16.6 %all_to_all.34.refs_2_ = f32[16,2,768]{2,1,0:T(2,128)S(1)} all-to-all(f32[16,2,768]{2,1,0:T(2,128)S(1)} %shard_map.83), channel_id=1, replica_groups=mesh['dp'=16,'z'=16,'c'=2] {'z'}, dimensions={0} | all-to-all | bytes 196608 | tf_op jit(solution)/shard_map/all_to_all | solution.py:288
  108.1 0.1 shard_map.84
  108.2 11.4 %all_to_all.35.in_ref = f32[16,2,768]{2,1,0:T(2,128)S(1)} all-to-all(f32[16,2,768]{2,1,0:T(2,128)S(1)} %shard_map.84), channel_id=1, replica_groups=mesh['dp'=16,'z'=16,'c'=2] {'dp'}, dimensions={0} | all-to-all | bytes 196608 | tf_op jit(solution)/shard_map/all_to_all | solution.py:290
  119.6 0.7 shard_map.85
  (2 shorter events, 0.1 us)
Async XLA Ops:
  1.7 4.1 %collective-permute-start = (f32[128,1408]{1,0:T(8,128)S(1)}, f32[128,1408]{1,0:T(8,128)S(1)}, u32[]{:S(2)}, u32[]{:S(2)}) collective-permute-start(f32[128,1408]{1,0:T(8,128)S(1)} %shard_map.77), channel_id=1, source_target_pairs={{0,1},{1,0},{2,3},{3,2},{4,5},{5,4},{6,7},{7,6},{8,9},{9,8},{10,11... | collective-permute-start | bytes 2162696 | tf_op jit(solution)/shard_map/ppermute | solution.py:253
  57.1 4.0 %collective-permute-start.1 = (f32[256,640]{1,0:T(8,128)S(1)}, f32[256,640]{1,0:T(8,128)S(1)}, u32[]{:S(2)}, u32[]{:S(2)}) collective-permute-start(f32[256,640]{1,0:T(8,128)S(1)} %get-tuple-element.50), channel_id=1, source_target_pairs={{0,1},{1,0},{2,3},{3,2},{4,5},{5,4},{6,7},{7,6},{8,9},{9,8},{10,11... | collective-permute-start | bytes 1966088 | tf_op jit(solution)/shard_map/ppermute | solution.py:280

commit v9 on v8

--- a/solution.py
+++ b/solution.py
@@ -17,6 +17,7 @@
 ZN = 16
 DP = 16
 GROUP = 4
+CUTS = 4
 GROUPS = ZN // GROUP
 
 
@@ -36,11 +37,24 @@
     return lax.broadcasted_iota(jnp.int32, shape, 0) >= lax.broadcasted_iota(jnp.int32, shape, 1)
 
 
-def pack_kernel(c_ref, group_ref, x_ref, g_ref, codes_ref, out_ref):
+def pack_kernel(c_ref, group_ref, x_hbm, g_hbm, codes_hbm, out_ref, x_ref, g_ref, codes_ref, sems):
     d = x_ref.shape[1]
-    out_ref[:, :d] = x_ref[...].astype(f32)
+    other = pl.multiple_of((1 - c_ref[0]) * HALF, HALF)
+    step = LD // CUTS
+    copies = [
+        pltpu.make_async_copy(x_hbm.at[k * step:(k + 1) * step], x_ref.at[k * step:(k + 1) * step], sems.at[k])
+        for k in range(CUTS)]
+    copies.append(pltpu.make_async_copy(g_hbm.at[:, pl.ds(other, HALF)], g_ref, sems.at[CUTS]))
+    copies.append(pltpu.make_async_copy(codes_hbm, codes_ref, sems.at[CUTS + 1]))
+    for copy in copies:
+        copy.start()
+    out_ref[HEADS:, d + HALF:] = jnp.zeros((LD - HEADS, LD), f32)
+    for k in range(CUTS):
+        copies[k].wait()
+        out_ref[k * step:(k + 1) * step, :d] = x_ref[k * step:(k + 1) * step, :].astype(f32)
+    copies[CUTS].wait()
     out_ref[:, d:d + HALF] = g_ref[...].astype(f32)
-    out_ref[:, d + HALF:] = jnp.zeros((LD, LD), f32)
+    copies[CUTS + 1].wait()
     out_ref[0:HEADS, d + HALF:] = codes_ref[...].astype(f32)
 
 
@@ -90,7 +104,7 @@
     last = running[CHIP - 1:CHIP, :]
     en = jnp.exp(-running)
     ep = jnp.exp(running)
-    te = jnp.exp(running - last)
+    te = ep * jnp.exp(-last)
     en_ref[...] = en
     te_ref[...] = te
     mixer = ms_ref[...].astype(f32)
@@ -176,11 +190,17 @@
     send_ref[LD:, 2 * HALF:] = there[:, LD:]
 
 
-def weight_kernel(c_ref, group_ref, xt_ref, gm_ref, pk_ref, recv_ref, out_ref):
+def near_kernel(c_ref, group_ref, xt_ref, gm_ref, out_ref):
+    rows = out_ref.shape[0]
+    xt = xt_ref[pl.ds(pl.multiple_of(c_ref[0] * rows, rows), rows), :]
+    out_ref[...] = mm(xt, gm_ref[...])
+
+
+def weight_kernel(c_ref, group_ref, xt_ref, near_ref, pk_ref, recv_ref, out_ref):
     c = c_ref[0]
     rows = out_ref.shape[0]
     xt = xt_ref[pl.ds(pl.multiple_of(c * rows, rows), rows), :]
-    out_ref[:, pl.ds(pl.multiple_of(c * HALF, HALF), HALF)] = mm(xt, gm_ref[...])
+    out_ref[:, pl.ds(pl.multiple_of(c * HALF, HALF), HALF)] = near_ref[...]
     out_ref[:, pl.ds(pl.multiple_of((1 - c) * HALF, HALF), HALF)] = mm(xt, recv_ref[:, :HALF].astype(bf16))
     out_ref[:, 2 * HALF:] = mm(xt, (pk_ref[...] + recv_ref[:, HALF:2 * HALF]).astype(bf16))
 
@@ -243,13 +263,15 @@
     across = [[GROUP * a + (a + b) % GROUP for a in range(GROUPS)] for b in range(GROUP)]
 
     here = pl.BlockSpec((LD, HALF), lambda i, c, g: (0, c[0]))
-    there = pl.BlockSpec((LD, HALF), lambda i, c, g: (0, 1 - c[0]))
     x, g, codes, wx, wbc = (
         pltpu.with_memory_space_constraint(a, pltpu.MemorySpace.HBM)
         for a in (x, g, codes, x_weight, bc_weight))
+    raw = pl.BlockSpec(memory_space=pl.ANY)
     (pack,) = call(
-        pack_kernel, place, [((LD, d + HALF + LD), f32)], (x, g, codes), (),
-        [whole(x.shape), there, whole(codes.shape)])
+        pack_kernel, place, [((LD, d + HALF + LD), f32)], (x, g, codes),
+        [pltpu.VMEM((LD, d), bf16), pltpu.VMEM((LD, HALF), bf16), pltpu.VMEM((HEADS, LD), jnp.int32),
+         pltpu.SemaphoreType.DMA((CUTS + 2,))],
+        [raw, raw, raw])
     pack = lax.ppermute(pack, "c", swap)
     half = (LD, HALF)
     owned = call(
@@ -280,7 +302,8 @@
     recv = lax.ppermute(send, "c", swap)
     xt = xc.T.reshape(ZN, 2, DP, 2, CHIP).transpose(1, 2, 0, 3, 4).reshape(d, CHIP)
     width = 2 * HALF + 2 * STATE
-    (grad,) = call(weight_kernel, place, [((d // 2, width), f32)], (xt, gm, pk, recv))
+    (near_part,) = call(near_kernel, place, [((d // 2, HALF), f32)], (xt, gm))
+    (grad,) = call(weight_kernel, place, [((d // 2, width), f32)], (xt, near_part, pk, recv))
 
     rows = d // 2 // DP
     part = lax.all_to_all(grad.reshape(DP, rows, width), "dp", 0, 0, tiled=True)

time: 121 us -> 121 us (level)
    pallas_call x10 -> x11, Pallas kernels: 5.69 us -> 5.84 us  [call(): pl.pallas_call(kernel, out_shape=[jax.ShapeDtypeStruct(s, d) for s, d in...]
  transfers between devices with their start and end apart: 2 -> 2, of which waited for: 2 -> 2; matrix products, arithmetic and copies ran while one was open for 1% -> 1% of each run, Pallas kernels for 1% -> 2%
where the time goes in v9:
time: 121 us; the launch traced here: 120 us
  blocking collectives  108 us (89%)
  Pallas kernels  5.84 us (5%)
  starting transfers between devices  3.84 us (3%)
    all_to_all x1, blocking collectives, body(): part = lax.all_to_all(grad.reshape(DP, rows, width), 'dp', 0, 0, tiled=True)  29.9 us
    all_to_all x2, blocking collectives, body(): pay = lax.all_to_all(pay, 'z', 0, 0, tiled=True, axis_index_groups=near)  26.5 us
    all_to_all x1, blocking collectives, body(): far = lax.all_to_all(far, 'z', 0, 0, tiled=True, axis_index_groups=across)  23.2 us
    all_to_all x1, blocking collectives, body(): part = lax.all_to_all(part, 'z', 0, 0, tiled=True)  16.6 us
    all_to_all x1, blocking collectives, body(): part = lax.all_to_all(part, 'dp', 0, 0, tiled=True)  11.4 us
    pallas_call x11, Pallas kernels, call(): pl.pallas_call(kernel, out_shape=[jax.ShapeDtypeStruct(s, d) for s, d in...  5.84 us
  transfers between devices with their start and end apart: 2, of which 2 were waited for; matrix products, arithmetic and copies ran while one was open for 1% of the time, Pallas kernels for 2%

profile of v9, /device:TPU:32, one launch (start us, length us, event | category | flops | bytes accessed | tf_op | source)
XLA Modules:
  0.0 120.2 jit_solution(11762745916082313304)
XLA Ops:
  0.6 1.0 shard_map.77
  1.7 1.9 %collective-permute-start = (f32[128,1408]{1,0:T(8,128)S(1)}, f32[128,1408]{1,0:T(8,128)S(1)}, u32[]{:S(2)}, u32[]{:S(2)}) collective-permute-start(f32[128,1408]{1,0:T(8,128)S(1)} %shard_map.77), channel_id=1, source_target_pairs={{0,1},{1,0},{2,3},{3,2},{4,5},{5,4},{6,7},{7,6},{8,9},{9,8},{10,11... | collective-permute-start | bytes 2162696 | tf_op jit(solution)/shard_map/ppermute | solution.py:275
  3.6 1.7 %shard_map.76 = (bf16[128,256]{1,0:T(8,128)(2,1)S(1)}, bf16[128,256]{1,0:T(8,128)(2,1)S(1)}, bf16[128,256]{1,0:T(8,128)(2,1)S(1)}, f32[8,128]{1,0:T(8,128)S(1)},...) custom-call(s32[1]{0:T(128)} %bitcast.c_ref.refs_0_, ...), custom_call_target="tpu_custom_call" | custom-call | tf_op jit(solution)/shard_map/pallas_call | solution.py:239
  5.3 0.4 collective-permute-done.refs_9_
  5.8 1.3 %shard_map.78 = (f32[4,136,128]{2,1,0:T(8,128)S(1)}, bf16[256,256]{1,0:T(8,128)(2,1)S(1)}, bf16[256,256]{1,0:T(8,128)(2,1)S(1)}, f32[256,256]{1,0:T(8,128)S(1)},...) custom-call(s32[1]{0:T(128)} %bitcast.c_ref.refs_0_, ...), custom_call_target="tpu_custom_call" | custom-call | tf_op jit(solution)/shard_map/pallas_call | solution.py:239
  7.0 16.1 %all_to_all.30.in_ref = f32[4,136,128]{2,1,0:T(8,128)S(1)} all-to-all(f32[4,136,128]{2,1,0:T(8,128)S(1)} %get-tuple-element.39), channel_id=1, replica_groups={{0,2,4,6},{8,10,12,14},{16,18,20,22},{24,26,28,30},{1,3,5,7},{9,11,13,1..., dimensions={0} | all-to-all | bytes 557056 | tf_op jit(solution)/shard_map/all_to_all | solution.py:292
  23.2 23.2 %all_to_all.31.far_ref = f32[4,72,128]{2,1,0:T(8,128)S(1)} all-to-all(f32[4,72,128]{2,1,0:T(8,128)S(1)} %shard_map.79), channel_id=1, replica_groups={{0,10,20,30},{2,12,22,24},{4,14,16,26},{6,8,18,28},{1,11,21,31},{3,13,2..., dimensions={0} | all-to-all | bytes 294912 | tf_op jit(solution)/shard_map/all_to_all | solution.py:294
  46.5 10.3 %all_to_all.32.refs_2_ = f32[4,128,128]{2,1,0:T(8,128)S(1)} all-to-all(f32[4,128,128]{2,1,0:T(8,128)S(1)} %shard_map.80), channel_id=1, replica_groups={{0,2,4,6},{8,10,12,14},{16,18,20,22},{24,26,28,30},{1,3,5,7},{9,11,13,1..., dimensions={0} | all-to-all | bytes 524288 | tf_op jit(solution)/shard_map/all_to_all | solution.py:296
  56.8 0.3 shard_map.81
  57.1 1.9 %collective-permute-start.1 = (f32[256,640]{1,0:T(8,128)S(1)}, f32[256,640]{1,0:T(8,128)S(1)}, u32[]{:S(2)}, u32[]{:S(2)}) collective-permute-start(f32[256,640]{1,0:T(8,128)S(1)} %get-tuple-element.50), channel_id=1, source_target_pairs={{0,1},{1,0},{2,3},{3,2},{4,5},{5,4},{6,7},{7,6},{8,9},{9,8},{10,11... | collective-permute-start | bytes 1966088 | tf_op jit(solution)/shard_map/ppermute | solution.py:302
  59.0 0.2 copy.9
  59.2 0.2 reshape.23
  59.5 0.5 copy.10
  60.0 0.2 reshape.24.xt_ref
  60.2 0.2 shard_map.82.near_ref
  60.4 0.7 collective-permute-done.1.recv_ref
  61.1 0.4 shard_map.83
  61.5 29.9 %all_to_all.33.in_ref = f32[16,32,768]{2,1,0:T(8,128)S(1)} all-to-all(f32[16,32,768]{2,1,0:T(8,128)S(1)} %bitcast.11), channel_id=1, replica_groups=mesh['dp'=16,'z'=16,'c'=2] {'dp'}, dimensions={0} | all-to-all | bytes 3145728 | tf_op jit(solution)/shard_map/all_to_all | solution.py:309
  91.3 0.1 shard_map.84
  91.4 16.6 %all_to_all.34.refs_2_ = f32[16,2,768]{2,1,0:T(2,128)S(1)} all-to-all(f32[16,2,768]{2,1,0:T(2,128)S(1)} %shard_map.84), channel_id=1, replica_groups=mesh['dp'=16,'z'=16,'c'=2] {'z'}, dimensions={0} | all-to-all | bytes 196608 | tf_op jit(solution)/shard_map/all_to_all | solution.py:311
  108.0 0.1 shard_map.85
  108.1 11.4 %all_to_all.35.in_ref = f32[16,2,768]{2,1,0:T(2,128)S(1)} all-to-all(f32[16,2,768]{2,1,0:T(2,128)S(1)} %shard_map.85), channel_id=1, replica_groups=mesh['dp'=16,'z'=16,'c'=2] {'dp'}, dimensions={0} | all-to-all | bytes 196608 | tf_op jit(solution)/shard_map/all_to_all | solution.py:313
  119.5 0.7 shard_map.86
  (2 shorter events, 0.1 us)
Async XLA Ops:
  1.7 4.1 %collective-permute-start = (f32[128,1408]{1,0:T(8,128)S(1)}, f32[128,1408]{1,0:T(8,128)S(1)}, u32[]{:S(2)}, u32[]{:S(2)}) collective-permute-start(f32[128,1408]{1,0:T(8,128)S(1)} %shard_map.77), channel_id=1, source_target_pairs={{0,1},{1,0},{2,3},{3,2},{4,5},{5,4},{6,7},{7,6},{8,9},{9,8},{10,11... | collective-permute-start | bytes 2162696 | tf_op jit(solution)/shard_map/ppermute | solution.py:275
  57.1 4.0 %collective-permute-start.1 = (f32[256,640]{1,0:T(8,128)S(1)}, f32[256,640]{1,0:T(8,128)S(1)}, u32[]{:S(2)}, u32[]{:S(2)}) collective-permute-start(f32[256,640]{1,0:T(8,128)S(1)} %get-tuple-element.50), channel_id=1, source_target_pairs={{0,1},{1,0},{2,3},{3,2},{4,5},{5,4},{6,7},{7,6},{8,9},{9,8},{10,11... | collective-permute-start | bytes 1966088 | tf_op jit(solution)/shard_map/ppermute | solution.py:302

commit v10 on v9

--- a/solution.py
+++ b/solution.py
@@ -16,6 +16,7 @@
 HALF = HEADS * HEAD // 2
 ZN = 16
 DP = 16
+SIDE = 4
 GROUP = 4
 CUTS = 4
 GROUPS = ZN // GROUP
@@ -190,19 +191,24 @@
     send_ref[LD:, 2 * HALF:] = there[:, LD:]
 
 
-def near_kernel(c_ref, group_ref, xt_ref, gm_ref, out_ref):
-    rows = out_ref.shape[0]
-    xt = xt_ref[pl.ds(pl.multiple_of(c_ref[0] * rows, rows), rows), :]
+def near_kernel(c_ref, group_ref, xa_ref, xb_ref, gm_ref, out_ref):
+    xt = jnp.where(c_ref[0] == 0, xa_ref[...], xb_ref[...])
     out_ref[...] = mm(xt, gm_ref[...])
 
 
-def weight_kernel(c_ref, group_ref, xt_ref, near_ref, pk_ref, recv_ref, out_ref):
+def weight_kernel(c_ref, group_ref, xa_ref, xb_ref, near_ref, pk_ref, recv_ref, out_ref):
     c = c_ref[0]
-    rows = out_ref.shape[0]
-    xt = xt_ref[pl.ds(pl.multiple_of(c * rows, rows), rows), :]
+    xt = jnp.where(c == 0, xa_ref[...], xb_ref[...])
     out_ref[:, pl.ds(pl.multiple_of(c * HALF, HALF), HALF)] = near_ref[...]
     out_ref[:, pl.ds(pl.multiple_of((1 - c) * HALF, HALF), HALF)] = mm(xt, recv_ref[:, :HALF].astype(bf16))
     out_ref[:, 2 * HALF:] = mm(xt, (pk_ref[...] + recv_ref[:, HALF:2 * HALF]).astype(bf16))
+
+
+def half_fold_kernel(c_ref, group_ref, in_ref, out_ref):
+    total = jnp.sum(in_ref[...], axis=0)
+    step = out_ref.shape[1]
+    for k in range(SIDE):
+        out_ref[k] = total[k * step:(k + 1) * step, :]
 
 
 def fold_kernel(c_ref, group_ref, in_ref, out_ref):
@@ -244,6 +250,22 @@
             out_specs=[whole(s) for s, _ in outs], scratch_shapes=list(scratch)),
         compiler_params=pltpu.CompilerParams(vmem_limit_bytes=16 * 1024 * 1024),
     )(*place, *ins)
+
+
+def lines(turn):
+    def device(x, y, z, core):
+        return ((x * SIDE + y) * ZN + z) * 2 + core
+
+    groups = []
+    for core in range(2):
+        for z in range(ZN):
+            for fixed in range(SIDE):
+                along = range(SIDE)
+                if core == turn:
+                    groups.append([device(k, fixed, z, core) for k in along])
+                else:
+                    groups.append([device(fixed, k, z, core) for k in along])
+    return groups
 
 
 def body(records, x_weight, bc_weight, decay_codes, out_grad):
@@ -300,13 +322,19 @@
         [(sq, bf16), ((CHIP, 2 * STATE), f32), ((LD, HALF), f32), ((CHIP, 2 * HALF + LD), f32)],
         (pay, ue, v, en, te, proj, yl, gml, gpl), [pltpu.VMEM(sq, f32)])
     recv = lax.ppermute(send, "c", swap)
-    xt = xc.T.reshape(ZN, 2, DP, 2, CHIP).transpose(1, 2, 0, 3, 4).reshape(d, CHIP)
+    xt = xc.T.reshape(ZN, 2, SIDE, SIDE, 2, CHIP)
+    xa = xt[:, 0].transpose(1, 2, 0, 3, 4).reshape(d // 2, CHIP)
+    xb = xt[:, 1].transpose(2, 1, 0, 3, 4).reshape(d // 2, CHIP)
     width = 2 * HALF + 2 * STATE
-    (near_part,) = call(near_kernel, place, [((d // 2, HALF), f32)], (xt, gm))
-    (grad,) = call(weight_kernel, place, [((d // 2, width), f32)], (xt, near_part, pk, recv))
+    (near_part,) = call(near_kernel, place, [((d // 2, HALF), f32)], (xa, xb, gm))
+    (grad,) = call(weight_kernel, place, [((d // 2, width), f32)], (xa, xb, near_part, pk, recv))
 
     rows = d // 2 // DP
-    part = lax.all_to_all(grad.reshape(DP, rows, width), "dp", 0, 0, tiled=True)
+    every = ("dp", "z", "c")
+    first, second = lines(0), lines(1)
+    part = lax.all_to_all(grad.reshape(SIDE, SIDE * rows, width), every, 0, 0, tiled=True, axis_index_groups=first)
+    (part,) = call(half_fold_kernel, place, [((SIDE, rows, width), f32)], (part,))
+    part = lax.all_to_all(part, every, 0, 0, tiled=True, axis_index_groups=second)
     (part,) = call(fold_kernel, place, [((ZN, rows // ZN, width), f32)], (part,))
     part = lax.all_to_all(part, "z", 0, 0, tiled=True)
     (part,) = call(lambda *refs: spread_kernel(grad_scale, *refs), place, [((DP, rows // ZN, width), f32)], (part,))

time: 121 us -> 120 us (level)
    all_to_all x1 -> x2, blocking collectives: 29.9 us -> 29.4 us  [the longest x1 17.8 us: body(): lax.all_to_all(grad.reshape(SIDE, SIDE * rows, width), every, 0, 0, tiled...]
    pallas_call x11 -> x12, Pallas kernels: 5.84 us -> 5.86 us  [call(): pl.pallas_call(kernel, out_shape=[jax.ShapeDtypeStruct(s, d) for s, d in...]
where the time goes in v10:
time: 120 us
  blocking collectives  107 us (89%)
  Pallas kernels  5.86 us (5%)
  starting transfers between devices  3.84 us (3%)
  local copies, waits for them, and re-layouts  1.52 us (1%)
    all_to_all x2, blocking collectives, body(): pay = lax.all_to_all(pay, 'z', 0, 0, tiled=True, axis_index_groups=near)  26.5 us
    all_to_all x1, blocking collectives, body(): far = lax.all_to_all(far, 'z', 0, 0, tiled=True, axis_index_groups=across)  23.2 us
    all_to_all x1, blocking collectives, body(): lax.all_to_all(grad.reshape(SIDE, SIDE * rows, width), every, 0, 0, tiled...  17.8 us
    all_to_all x1, blocking collectives, body(): part = lax.all_to_all(part, 'z', 0, 0, tiled=True)  17.1 us
    all_to_all x1, blocking collectives, body(): lax.all_to_all(part, every, 0, 0, tiled=True, axis_index_groups=second)  11.6 us
    all_to_all x1, blocking collectives, body(): part = lax.all_to_all(part, 'dp', 0, 0, tiled=True)  10.7 us
    pallas_call x12, Pallas kernels, call(): pl.pallas_call(kernel, out_shape=[jax.ShapeDtypeStruct(s, d) for s, d in...  5.86 us
  transfers between devices with their start and end apart: 2, of which 2 were waited for; matrix products, arithmetic and copies ran while one was open for 1% of the time, Pallas kernels for 2%

profile of v10, /device:TPU:32, one launch (start us, length us, event | category | flops | bytes accessed | tf_op | source)
XLA Modules:
  0.0 119.6 jit_solution(16122242055183830622)
XLA Ops:
  0.6 1.0 shard_map.77
  1.7 1.9 %collective-permute-start = (f32[128,1408]{1,0:T(8,128)S(1)}, f32[128,1408]{1,0:T(8,128)S(1)}, u32[]{:S(2)}, u32[]{:S(2)}) collective-permute-start(f32[128,1408]{1,0:T(8,128)S(1)} %shard_map.77), channel_id=1, source_target_pairs={{0,1},{1,0},{2,3},{3,2},{4,5},{5,4},{6,7},{7,6},{8,9},{9,8},{10,11... | collective-permute-start | bytes 2162696 | tf_op jit(solution)/shard_map/ppermute | solution.py:297
  3.6 1.7 %shard_map.76 = (bf16[128,256]{1,0:T(8,128)(2,1)S(1)}, bf16[128,256]{1,0:T(8,128)(2,1)S(1)}, bf16[128,256]{1,0:T(8,128)(2,1)S(1)}, f32[8,128]{1,0:T(8,128)S(1)},...) custom-call(s32[1]{0:T(128)} %bitcast.c_ref.refs_0_, ...), custom_call_target="tpu_custom_call" | custom-call | tf_op jit(solution)/shard_map/pallas_call | solution.py:245
  5.3 0.4 collective-permute-done.refs_9_
  5.8 1.3 %shard_map.78 = (f32[4,136,128]{2,1,0:T(8,128)S(1)}, bf16[256,256]{1,0:T(8,128)(2,1)S(1)}, bf16[256,256]{1,0:T(8,128)(2,1)S(1)}, f32[256,256]{1,0:T(8,128)S(1)},...) custom-call(s32[1]{0:T(128)} %bitcast.c_ref.refs_0_, ...), custom_call_target="tpu_custom_call" | custom-call | tf_op jit(solution)/shard_map/pallas_call | solution.py:245
  7.0 16.1 %all_to_all.35.in_ref = f32[4,136,128]{2,1,0:T(8,128)S(1)} all-to-all(f32[4,136,128]{2,1,0:T(8,128)S(1)} %get-tuple-element.39), channel_id=1, replica_groups={{0,2,4,6},{8,10,12,14},{16,18,20,22},{24,26,28,30},{1,3,5,7},{9,11,13,1..., dimensions={0} | all-to-all | bytes 557056 | tf_op jit(solution)/shard_map/all_to_all | solution.py:314
  23.2 23.2 %all_to_all.36.far_ref = f32[4,72,128]{2,1,0:T(8,128)S(1)} all-to-all(f32[4,72,128]{2,1,0:T(8,128)S(1)} %shard_map.79), channel_id=1, replica_groups={{0,10,20,30},{2,12,22,24},{4,14,16,26},{6,8,18,28},{1,11,21,31},{3,13,2..., dimensions={0} | all-to-all | bytes 294912 | tf_op jit(solution)/shard_map/all_to_all | solution.py:316
  46.5 10.3 %all_to_all.37.refs_2_ = f32[4,128,128]{2,1,0:T(8,128)S(1)} all-to-all(f32[4,128,128]{2,1,0:T(8,128)S(1)} %shard_map.80), channel_id=1, replica_groups={{0,2,4,6},{8,10,12,14},{16,18,20,22},{24,26,28,30},{1,3,5,7},{9,11,13,1..., dimensions={0} | all-to-all | bytes 524288 | tf_op jit(solution)/shard_map/all_to_all | solution.py:318
  56.8 0.3 shard_map.81
  57.1 1.9 %collective-permute-start.1 = (f32[256,640]{1,0:T(8,128)S(1)}, f32[256,640]{1,0:T(8,128)S(1)}, u32[]{:S(2)}, u32[]{:S(2)}) collective-permute-start(f32[256,640]{1,0:T(8,128)S(1)} %get-tuple-element.50), channel_id=1, source_target_pairs={{0,1},{1,0},{2,3},{3,2},{4,5},{5,4},{6,7},{7,6},{8,9},{9,8},{10,11... | collective-permute-start | bytes 1966088 | tf_op jit(solution)/shard_map/ppermute | solution.py:324
  59.0 0.2 copy.10
  59.2 0.2 reshape.26
  59.5 0.4 slice_bitcast_fusion
  59.9 0.2 copy.12
  60.1 0.1 reshape.28.xb_ref
  60.3 0.2 copy.11
  60.5 0.1 reshape.27.xa_ref
  60.6 0.2 shard_map.82.near_ref
  60.8 0.3 collective-permute-done.1.recv_ref
  61.1 0.4 shard_map.83
  61.5 17.8 %all_to_all.38.in_ref = f32[4,128,768]{2,1,0:T(8,128)S(1)} all-to-all(f32[4,128,768]{2,1,0:T(8,128)S(1)} %bitcast.18), channel_id=1, replica_groups={{0,128,256,384},{32,160,288,416},{64,192,320,448},{96,224,352,480},{2,1..., dimensions={0} | all-to-all | bytes 3145728 | tf_op jit(solution)/shard_map/all_to_all | solution.py:335
  79.3 0.1 shard_map.84
  79.3 11.6 %all_to_all.39.in_ref = f32[4,32,768]{2,1,0:T(8,128)S(1)} all-to-all(f32[4,32,768]{2,1,0:T(8,128)S(1)} %shard_map.84), channel_id=1, replica_groups={{0,32,64,96},{128,160,192,224},{256,288,320,352},{384,416,448,480},{2,3..., dimensions={0} | all-to-all | bytes 786432 | tf_op jit(solution)/shard_map/all_to_all | solution.py:337
  91.0 17.1 %all_to_all.40.refs_2_ = f32[16,2,768]{2,1,0:T(2,128)S(1)} all-to-all(f32[16,2,768]{2,1,0:T(2,128)S(1)} %shard_map.85), channel_id=1, replica_groups=mesh['dp'=16,'z'=16,'c'=2] {'z'}, dimensions={0} | all-to-all | bytes 196608 | tf_op jit(solution)/shard_map/all_to_all | solution.py:339
  108.1 0.1 shard_map.86
  108.2 10.7 %all_to_all.41.in_ref = f32[16,2,768]{2,1,0:T(2,128)S(1)} all-to-all(f32[16,2,768]{2,1,0:T(2,128)S(1)} %shard_map.86), channel_id=1, replica_groups=mesh['dp'=16,'z'=16,'c'=2] {'dp'}, dimensions={0} | all-to-all | bytes 196608 | tf_op jit(solution)/shard_map/all_to_all | solution.py:341
  118.9 0.7 shard_map.87
  (3 shorter events, 0.1 us)
Async XLA Ops:
  1.7 4.1 %collective-permute-start = (f32[128,1408]{1,0:T(8,128)S(1)}, f32[128,1408]{1,0:T(8,128)S(1)}, u32[]{:S(2)}, u32[]{:S(2)}) collective-permute-start(f32[128,1408]{1,0:T(8,128)S(1)} %shard_map.77), channel_id=1, source_target_pairs={{0,1},{1,0},{2,3},{3,2},{4,5},{5,4},{6,7},{7,6},{8,9},{9,8},{10,11... | collective-permute-start | bytes 2162696 | tf_op jit(solution)/shard_map/ppermute | solution.py:297
  57.1 4.0 %collective-permute-start.1 = (f32[256,640]{1,0:T(8,128)S(1)}, f32[256,640]{1,0:T(8,128)S(1)}, u32[]{:S(2)}, u32[]{:S(2)}) collective-permute-start(f32[256,640]{1,0:T(8,128)S(1)} %get-tuple-element.50), channel_id=1, source_target_pairs={{0,1},{1,0},{2,3},{3,2},{4,5},{5,4},{6,7},{7,6},{8,9},{9,8},{10,11... | collective-permute-start | bytes 1966088 | tf_op jit(solution)/shard_map/ppermute | solution.py:324

commit v11 on v10

--- a/solution.py
+++ b/solution.py
@@ -19,6 +19,10 @@
 SIDE = 4
 GROUP = 4
 CUTS = 4
+NEAR = (0, 3, 1, 2)
+NEAR_AT = (0, 2, 3, 1)
+FAR = (0, 2, 1, 3)
+FAR_AT = (0, 2, 1, 3)
 GROUPS = ZN // GROUP
 
 
@@ -32,6 +36,11 @@
 
 def mm_nt(a, b):
     return lax.dot_general(a, b, (((1,), (1,)), ((), ())), preferred_element_type=f32)
+
+
+def head_at(group_ref, h):
+    chip = (group_ref[0] + h) & (GROUP - 1)
+    return jnp.where(chip == 0, 0, jnp.where(chip == GROUP - 1, 1, chip + 1))
 
 
 def causal(shape):
@@ -119,7 +128,7 @@
     state = mm_tn(ue, inject)
     adjoint = mm_tn(v, readout)
     for h in range(GROUP):
-        at = (group_ref[0] + h) & (GROUP - 1)
+        at = head_at(group_ref, h)
         pay_ref[at, 0:HEAD, :] = state[h * HEAD:(h + 1) * HEAD, :]
         pay_ref[at, HEAD:2 * HEAD, :] = adjoint[h * HEAD:(h + 1) * HEAD, :]
         pay_ref[at, 2 * HEAD:, :] = jnp.broadcast_to(last[:, h * HEAD:h * HEAD + 1], (8, STATE))
@@ -133,44 +142,44 @@
 
 def total_kernel(c_ref, group_ref, in_ref, out_ref):
     group = group_ref[0]
-    logs = [in_ref[k, 2 * HEAD:, :] for k in range(GROUP)]
+    logs = [in_ref[NEAR_AT[k], 2 * HEAD:, :] for k in range(GROUP)]
     decay = [jnp.exp(-a[0:1, :]) for a in logs]
-    state = in_ref[0, 0:HEAD, :]
+    state = in_ref[NEAR_AT[0], 0:HEAD, :]
     for k in range(1, GROUP):
-        state = decay[k] * state + in_ref[k, 0:HEAD, :]
-    adjoint = in_ref[GROUP - 1, HEAD:2 * HEAD, :]
+        state = decay[k] * state + in_ref[NEAR_AT[k], 0:HEAD, :]
+    adjoint = in_ref[NEAR_AT[GROUP - 1], HEAD:2 * HEAD, :]
     for k in reversed(range(GROUP - 1)):
-        adjoint = decay[k] * adjoint + in_ref[k, HEAD:2 * HEAD, :]
+        adjoint = decay[k] * adjoint + in_ref[NEAR_AT[k], HEAD:2 * HEAD, :]
     total = logs[0] + logs[1] + logs[2] + logs[3]
     for k in range(GROUPS):
-        out_ref[k, 0:HEAD, :] = jnp.where(k > group, state, adjoint)
-        out_ref[k, HEAD:, :] = total
+        out_ref[FAR_AT[k], 0:HEAD, :] = jnp.where(k > group, state, adjoint)
+        out_ref[FAR_AT[k], HEAD:, :] = total
 
 
 def prefix_kernel(c_ref, group_ref, in_ref, far_ref, out_ref):
     group = group_ref[0]
-    far = [jnp.exp(-far_ref[k, HEAD:HEAD + 1, :]) for k in range(GROUPS)]
-    decay = [jnp.exp(-in_ref[k, 2 * HEAD:2 * HEAD + 1, :]) for k in range(GROUP)]
+    far = [jnp.exp(-far_ref[FAR_AT[k], HEAD:HEAD + 1, :]) for k in range(GROUPS)]
+    decay = [jnp.exp(-in_ref[NEAR_AT[k], 2 * HEAD:2 * HEAD + 1, :]) for k in range(GROUP)]
     carry = jnp.zeros((HEAD, STATE), f32)
     for k in range(GROUPS - 1):
-        carry = jnp.where(k < group, far[k] * carry + far_ref[k, 0:HEAD, :], carry)
+        carry = jnp.where(k < group, far[k] * carry + far_ref[FAR_AT[k], 0:HEAD, :], carry)
     for k in range(GROUP):
-        out_ref[k, 0:HEAD, :] = carry
+        out_ref[NEAR_AT[k], 0:HEAD, :] = carry
         if k + 1 < GROUP:
-            carry = decay[k] * carry + in_ref[k, 0:HEAD, :]
+            carry = decay[k] * carry + in_ref[NEAR_AT[k], 0:HEAD, :]
     carry = jnp.zeros((HEAD, STATE), f32)
     for k in reversed(range(1, GROUPS)):
-        carry = jnp.where(k > group, far[k] * carry + far_ref[k, 0:HEAD, :], carry)
+        carry = jnp.where(k > group, far[k] * carry + far_ref[FAR_AT[k], 0:HEAD, :], carry)
     for k in reversed(range(GROUP)):
-        out_ref[k, HEAD:, :] = carry
+        out_ref[NEAR_AT[k], HEAD:, :] = carry
         if k:
-            carry = decay[k] * carry + in_ref[k, HEAD:2 * HEAD, :]
+            carry = decay[k] * carry + in_ref[NEAR_AT[k], HEAD:2 * HEAD, :]
 
 
 def outer_kernel(scale, c_ref, group_ref, in_ref, u_ref, v_ref, en_ref, te_ref, proj_ref,
                  yl_ref, gml_ref, gp_ref, gm_ref, pk_ref, yk_ref, send_ref, y_ref):
     c = c_ref[0]
-    pieces = [in_ref[(group_ref[0] + h) & (GROUP - 1)] for h in range(GROUP)]
+    pieces = [in_ref[head_at(group_ref, h)] for h in range(GROUP)]
     carry = jnp.concatenate([a[:HEAD] for a in pieces], axis=0).astype(bf16)
     adjoint = jnp.concatenate([a[HEAD:] for a in pieces], axis=0).astype(bf16)
     inject = proj_ref[:, :STATE]
@@ -281,8 +290,8 @@
         lax.axis_index("c").astype(jnp.int32).reshape(1),
         lax.div(lax.axis_index("z"), GROUP).astype(jnp.int32).reshape(1)))
     swap = [(0, 1), (1, 0)]
-    near = [[GROUP * a + b for b in range(GROUP)] for a in range(GROUPS)]
-    across = [[GROUP * a + (a + b) % GROUP for a in range(GROUPS)] for b in range(GROUP)]
+    near = [[GROUP * a + b for b in NEAR] for a in range(GROUPS)]
+    across = [[GROUP * a + (a + b) % GROUP for a in FAR] for b in range(GROUP)]
 
     here = pl.BlockSpec((LD, HALF), lambda i, c, g: (0, c[0]))
     x, g, codes, wx, wbc = (

time: 120 us -> 120 us (level)
  no operation moved by 1% of the time
where the time goes in v11:
time: 120 us; the launch traced here: 119 us
  blocking collectives  107 us (89%)
  Pallas kernels  5.86 us (5%)
  starting transfers between devices  3.84 us (3%)
  local copies, waits for them, and re-layouts  1.52 us (1%)
    all_to_all x2, blocking collectives, body(): pay = lax.all_to_all(pay, 'z', 0, 0, tiled=True, axis_index_groups=near)  26.5 us
    all_to_all x1, blocking collectives, body(): far = lax.all_to_all(far, 'z', 0, 0, tiled=True, axis_index_groups=across)  23.8 us
    all_to_all x1, blocking collectives, body(): lax.all_to_all(grad.reshape(SIDE, SIDE * rows, width), every, 0, 0, tiled...  17.8 us
    all_to_all x1, blocking collectives, body(): part = lax.all_to_all(part, 'z', 0, 0, tiled=True)  16.1 us
    all_to_all x1, blocking collectives, body(): lax.all_to_all(part, every, 0, 0, tiled=True, axis_index_groups=second)  11.6 us
    all_to_all x1, blocking collectives, body(): part = lax.all_to_all(part, 'dp', 0, 0, tiled=True)  10.7 us
    pallas_call x12, Pallas kernels, call(): pl.pallas_call(kernel, out_shape=[jax.ShapeDtypeStruct(s, d) for s, d in...  5.86 us
  transfers between devices with their start and end apart: 2, of which 2 were waited for; matrix products, arithmetic and copies ran while one was open for 1% of the time, Pallas kernels for 2%

profile of v11, /device:TPU:32, one launch (start us, length us, event | category | flops | bytes accessed | tf_op | source)
XLA Modules:
  0.0 119.3 jit_solution(13973279599462758625)
XLA Ops:
  0.6 1.0 shard_map.77
  1.7 1.9 %collective-permute-start = (f32[128,1408]{1,0:T(8,128)S(1)}, f32[128,1408]{1,0:T(8,128)S(1)}, u32[]{:S(2)}, u32[]{:S(2)}) collective-permute-start(f32[128,1408]{1,0:T(8,128)S(1)} %shard_map.77), channel_id=1, source_target_pairs={{0,1},{1,0},{2,3},{3,2},{4,5},{5,4},{6,7},{7,6},{8,9},{9,8},{10,11... | collective-permute-start | bytes 2162696 | tf_op jit(solution)/shard_map/ppermute | solution.py:306
  3.6 1.7 %shard_map.76 = (bf16[128,256]{1,0:T(8,128)(2,1)S(1)}, bf16[128,256]{1,0:T(8,128)(2,1)S(1)}, bf16[128,256]{1,0:T(8,128)(2,1)S(1)}, f32[8,128]{1,0:T(8,128)S(1)},...) custom-call(s32[1]{0:T(128)} %bitcast.c_ref.refs_0_, ...), custom_call_target="tpu_custom_call" | custom-call | tf_op jit(solution)/shard_map/pallas_call | solution.py:254
  5.3 0.4 collective-permute-done.refs_9_
  5.8 1.3 %shard_map.78 = (f32[4,136,128]{2,1,0:T(8,128)S(1)}, bf16[256,256]{1,0:T(8,128)(2,1)S(1)}, bf16[256,256]{1,0:T(8,128)(2,1)S(1)}, f32[256,256]{1,0:T(8,128)S(1)},...) custom-call(s32[1]{0:T(128)} %bitcast.c_ref.refs_0_, ...), custom_call_target="tpu_custom_call" | custom-call | tf_op jit(solution)/shard_map/pallas_call | solution.py:254
  7.0 16.2 %all_to_all.35.in_ref = f32[4,136,128]{2,1,0:T(8,128)S(1)} all-to-all(f32[4,136,128]{2,1,0:T(8,128)S(1)} %get-tuple-element.39), channel_id=1, replica_groups={{0,6,2,4},{8,14,10,12},{16,22,18,20},{24,30,26,28},{1,7,3,5},{9,15,11,1..., dimensions={0} | all-to-all | bytes 557056 | tf_op jit(solution)/shard_map/all_to_all | solution.py:323
  23.2 23.8 %all_to_all.36.far_ref = f32[4,72,128]{2,1,0:T(8,128)S(1)} all-to-all(f32[4,72,128]{2,1,0:T(8,128)S(1)} %shard_map.79), channel_id=1, replica_groups={{0,20,10,30},{2,22,12,24},{4,16,14,26},{6,18,8,28},{1,21,11,31},{3,23,1..., dimensions={0} | all-to-all | bytes 294912 | tf_op jit(solution)/shard_map/all_to_all | solution.py:325
  47.1 0.1 shard_map.80
  47.1 10.3 %all_to_all.37.refs_2_ = f32[4,128,128]{2,1,0:T(8,128)S(1)} all-to-all(f32[4,128,128]{2,1,0:T(8,128)S(1)} %shard_map.80), channel_id=1, replica_groups={{0,6,2,4},{8,14,10,12},{16,22,18,20},{24,30,26,28},{1,7,3,5},{9,15,11,1..., dimensions={0} | all-to-all | bytes 524288 | tf_op jit(solution)/shard_map/all_to_all | solution.py:327
  57.5 0.3 shard_map.81
  57.8 1.9 %collective-permute-start.1 = (f32[256,640]{1,0:T(8,128)S(1)}, f32[256,640]{1,0:T(8,128)S(1)}, u32[]{:S(2)}, u32[]{:S(2)}) collective-permute-start(f32[256,640]{1,0:T(8,128)S(1)} %get-tuple-element.50), channel_id=1, source_target_pairs={{0,1},{1,0},{2,3},{3,2},{4,5},{5,4},{6,7},{7,6},{8,9},{9,8},{10,11... | collective-permute-start | bytes 1966088 | tf_op jit(solution)/shard_map/ppermute | solution.py:333
  59.7 0.2 copy.10
  59.9 0.2 reshape.26
  60.2 0.4 slice_bitcast_fusion
  60.6 0.2 copy.12
  60.8 0.1 reshape.28.xb_ref
  61.0 0.2 copy.11
  61.2 0.1 reshape.27.xa_ref
  61.3 0.2 shard_map.82.near_ref
  61.5 0.3 collective-permute-done.1.recv_ref
  61.8 0.4 shard_map.83
  62.2 17.8 %all_to_all.38.in_ref = f32[4,128,768]{2,1,0:T(8,128)S(1)} all-to-all(f32[4,128,768]{2,1,0:T(8,128)S(1)} %bitcast.18), channel_id=1, replica_groups={{0,128,256,384},{32,160,288,416},{64,192,320,448},{96,224,352,480},{2,1..., dimensions={0} | all-to-all | bytes 3145728 | tf_op jit(solution)/shard_map/all_to_all | solution.py:344
  80.0 0.1 shard_map.84
  80.0 11.6 %all_to_all.39.in_ref = f32[4,32,768]{2,1,0:T(8,128)S(1)} all-to-all(f32[4,32,768]{2,1,0:T(8,128)S(1)} %shard_map.84), channel_id=1, replica_groups={{0,32,64,96},{128,160,192,224},{256,288,320,352},{384,416,448,480},{2,3..., dimensions={0} | all-to-all | bytes 786432 | tf_op jit(solution)/shard_map/all_to_all | solution.py:346
  91.7 16.1 %all_to_all.40.refs_2_ = f32[16,2,768]{2,1,0:T(2,128)S(1)} all-to-all(f32[16,2,768]{2,1,0:T(2,128)S(1)} %shard_map.85), channel_id=1, replica_groups=mesh['dp'=16,'z'=16,'c'=2] {'z'}, dimensions={0} | all-to-all | bytes 196608 | tf_op jit(solution)/shard_map/all_to_all | solution.py:348
  107.8 0.1 shard_map.86
  107.9 10.7 %all_to_all.41.in_ref = f32[16,2,768]{2,1,0:T(2,128)S(1)} all-to-all(f32[16,2,768]{2,1,0:T(2,128)S(1)} %shard_map.86), channel_id=1, replica_groups=mesh['dp'=16,'z'=16,'c'=2] {'dp'}, dimensions={0} | all-to-all | bytes 196608 | tf_op jit(solution)/shard_map/all_to_all | solution.py:350
  118.6 0.7 shard_map.87
  (2 shorter events, 0.1 us)
Async XLA Ops:
  1.7 4.1 %collective-permute-start = (f32[128,1408]{1,0:T(8,128)S(1)}, f32[128,1408]{1,0:T(8,128)S(1)}, u32[]{:S(2)}, u32[]{:S(2)}) collective-permute-start(f32[128,1408]{1,0:T(8,128)S(1)} %shard_map.77), channel_id=1, source_target_pairs={{0,1},{1,0},{2,3},{3,2},{4,5},{5,4},{6,7},{7,6},{8,9},{9,8},{10,11... | collective-permute-start | bytes 2162696 | tf_op jit(solution)/shard_map/ppermute | solution.py:306
  57.8 4.0 %collective-permute-start.1 = (f32[256,640]{1,0:T(8,128)S(1)}, f32[256,640]{1,0:T(8,128)S(1)}, u32[]{:S(2)}, u32[]{:S(2)}) collective-permute-start(f32[256,640]{1,0:T(8,128)S(1)} %get-tuple-element.50), channel_id=1, source_target_pairs={{0,1},{1,0},{2,3},{3,2},{4,5},{5,4},{6,7},{7,6},{8,9},{9,8},{10,11... | collective-permute-start | bytes 1966088 | tf_op jit(solution)/shard_map/ppermute | solution.py:333

commit v12 on v11

--- a/solution.py
+++ b/solution.py
@@ -19,8 +19,8 @@
 SIDE = 4
 GROUP = 4
 CUTS = 4
-NEAR = (0, 3, 1, 2)
-NEAR_AT = (0, 2, 3, 1)
+NEAR = (0, 1, 2, 3)
+NEAR_AT = (0, 1, 2, 3)
 FAR = (0, 2, 1, 3)
 FAR_AT = (0, 2, 1, 3)
 GROUPS = ZN // GROUP
@@ -39,8 +39,7 @@
 
 
 def head_at(group_ref, h):
-    chip = (group_ref[0] + h) & (GROUP - 1)
-    return jnp.where(chip == 0, 0, jnp.where(chip == GROUP - 1, 1, chip + 1))
+    return (group_ref[0] + h) & (GROUP - 1)
 
 
 def causal(shape):

time: 120 us -> 120 us (level)
  no operation moved by 1% of the time
where the time goes in v12:
time: 120 us
  blocking collectives  107 us (89%)
  Pallas kernels  5.85 us (5%)
  starting transfers between devices  3.84 us (3%)
  local copies, waits for them, and re-layouts  1.52 us (1%)
    all_to_all x2, blocking collectives, body(): pay = lax.all_to_all(pay, 'z', 0, 0, tiled=True, axis_index_groups=near)  26.1 us
    all_to_all x1, blocking collectives, body(): far = lax.all_to_all(far, 'z', 0, 0, tiled=True, axis_index_groups=across)  23.9 us
    all_to_all x1, blocking collectives, body(): lax.all_to_all(grad.reshape(SIDE, SIDE * rows, width), every, 0, 0, tiled...  17.8 us
    all_to_all x1, blocking collectives, body(): part = lax.all_to_all(part, 'z', 0, 0, tiled=True)  17.1 us
    all_to_all x1, blocking collectives, body(): lax.all_to_all(part, every, 0, 0, tiled=True, axis_index_groups=second)  11.6 us
    all_to_all x1, blocking collectives, body(): part = lax.all_to_all(part, 'dp', 0, 0, tiled=True)  10.7 us
    pallas_call x12, Pallas kernels, call(): pl.pallas_call(kernel, out_shape=[jax.ShapeDtypeStruct(s, d) for s, d in...  5.85 us
  transfers between devices with their start and end apart: 2, of which 2 were waited for; matrix products, arithmetic and copies ran while one was open for 1% of the time, Pallas kernels for 2%

profile of v12, /device:TPU:32, one launch (start us, length us, event | category | flops | bytes accessed | tf_op | source)
XLA Modules:
  0.0 119.9 jit_solution(4482995703062793116)
XLA Ops:
  0.6 1.0 shard_map.77
  1.7 1.9 %collective-permute-start = (f32[128,1408]{1,0:T(8,128)S(1)}, f32[128,1408]{1,0:T(8,128)S(1)}, u32[]{:S(2)}, u32[]{:S(2)}) collective-permute-start(f32[128,1408]{1,0:T(8,128)S(1)} %shard_map.77), channel_id=1, source_target_pairs={{0,1},{1,0},{2,3},{3,2},{4,5},{5,4},{6,7},{7,6},{8,9},{9,8},{10,11... | collective-permute-start | bytes 2162696 | tf_op jit(solution)/shard_map/ppermute | solution.py:305
  3.6 1.7 %shard_map.76 = (bf16[128,256]{1,0:T(8,128)(2,1)S(1)}, bf16[128,256]{1,0:T(8,128)(2,1)S(1)}, bf16[128,256]{1,0:T(8,128)(2,1)S(1)}, f32[8,128]{1,0:T(8,128)S(1)},...) custom-call(s32[1]{0:T(128)} %bitcast.c_ref.refs_0_, ...), custom_call_target="tpu_custom_call" | custom-call | tf_op jit(solution)/shard_map/pallas_call | solution.py:253
  5.3 0.4 collective-permute-done.refs_9_
  5.8 1.3 %shard_map.78 = (f32[4,136,128]{2,1,0:T(8,128)S(1)}, bf16[256,256]{1,0:T(8,128)(2,1)S(1)}, bf16[256,256]{1,0:T(8,128)(2,1)S(1)}, f32[256,256]{1,0:T(8,128)S(1)},...) custom-call(s32[1]{0:T(128)} %bitcast.c_ref.refs_0_, ...), custom_call_target="tpu_custom_call" | custom-call | tf_op jit(solution)/shard_map/pallas_call | solution.py:253
  7.0 16.1 %all_to_all.35.in_ref = f32[4,136,128]{2,1,0:T(8,128)S(1)} all-to-all(f32[4,136,128]{2,1,0:T(8,128)S(1)} %get-tuple-element.39), channel_id=1, replica_groups={{0,2,4,6},{8,10,12,14},{16,18,20,22},{24,26,28,30},{1,3,5,7},{9,11,13,1..., dimensions={0} | all-to-all | bytes 557056 | tf_op jit(solution)/shard_map/all_to_all | solution.py:322
  23.2 23.9 %all_to_all.36.far_ref = f32[4,72,128]{2,1,0:T(8,128)S(1)} all-to-all(f32[4,72,128]{2,1,0:T(8,128)S(1)} %shard_map.79), channel_id=1, replica_groups={{0,20,10,30},{2,22,12,24},{4,16,14,26},{6,18,8,28},{1,21,11,31},{3,23,1..., dimensions={0} | all-to-all | bytes 294912 | tf_op jit(solution)/shard_map/all_to_all | solution.py:324
  47.1 0.1 shard_map.80
  47.2 10.0 %all_to_all.37.refs_2_ = f32[4,128,128]{2,1,0:T(8,128)S(1)} all-to-all(f32[4,128,128]{2,1,0:T(8,128)S(1)} %shard_map.80), channel_id=1, replica_groups={{0,2,4,6},{8,10,12,14},{16,18,20,22},{24,26,28,30},{1,3,5,7},{9,11,13,1..., dimensions={0} | all-to-all | bytes 524288 | tf_op jit(solution)/shard_map/all_to_all | solution.py:326
  57.1 0.3 shard_map.81
  57.4 1.9 %collective-permute-start.1 = (f32[256,640]{1,0:T(8,128)S(1)}, f32[256,640]{1,0:T(8,128)S(1)}, u32[]{:S(2)}, u32[]{:S(2)}) collective-permute-start(f32[256,640]{1,0:T(8,128)S(1)} %get-tuple-element.50), channel_id=1, source_target_pairs={{0,1},{1,0},{2,3},{3,2},{4,5},{5,4},{6,7},{7,6},{8,9},{9,8},{10,11... | collective-permute-start | bytes 1966088 | tf_op jit(solution)/shard_map/ppermute | solution.py:332
  59.4 0.2 copy.10
  59.6 0.2 reshape.26
  59.8 0.4 slice_bitcast_fusion
  60.2 0.2 copy.12
  60.5 0.1 reshape.28.xb_ref
  60.6 0.2 copy.11
  60.8 0.1 reshape.27.xa_ref
  60.9 0.2 shard_map.82.near_ref
  61.2 0.3 collective-permute-done.1.recv_ref
  61.4 0.4 shard_map.83
  61.8 17.8 %all_to_all.38.in_ref = f32[4,128,768]{2,1,0:T(8,128)S(1)} all-to-all(f32[4,128,768]{2,1,0:T(8,128)S(1)} %bitcast.18), channel_id=1, replica_groups={{0,128,256,384},{32,160,288,416},{64,192,320,448},{96,224,352,480},{2,1..., dimensions={0} | all-to-all | bytes 3145728 | tf_op jit(solution)/shard_map/all_to_all | solution.py:343
  79.6 0.1 shard_map.84
  79.7 11.6 %all_to_all.39.in_ref = f32[4,32,768]{2,1,0:T(8,128)S(1)} all-to-all(f32[4,32,768]{2,1,0:T(8,128)S(1)} %shard_map.84), channel_id=1, replica_groups={{0,32,64,96},{128,160,192,224},{256,288,320,352},{384,416,448,480},{2,3..., dimensions={0} | all-to-all | bytes 786432 | tf_op jit(solution)/shard_map/all_to_all | solution.py:345
  91.3 17.1 %all_to_all.40.refs_2_ = f32[16,2,768]{2,1,0:T(2,128)S(1)} all-to-all(f32[16,2,768]{2,1,0:T(2,128)S(1)} %shard_map.85), channel_id=1, replica_groups=mesh['dp'=16,'z'=16,'c'=2] {'z'}, dimensions={0} | all-to-all | bytes 196608 | tf_op jit(solution)/shard_map/all_to_all | solution.py:347
  108.4 0.1 shard_map.86
  108.5 10.7 %all_to_all.41.in_ref = f32[16,2,768]{2,1,0:T(2,128)S(1)} all-to-all(f32[16,2,768]{2,1,0:T(2,128)S(1)} %shard_map.86), channel_id=1, replica_groups=mesh['dp'=16,'z'=16,'c'=2] {'dp'}, dimensions={0} | all-to-all | bytes 196608 | tf_op jit(solution)/shard_map/all_to_all | solution.py:349
  119.2 0.7 shard_map.87
  (2 shorter events, 0.1 us)
Async XLA Ops:
  1.7 4.1 %collective-permute-start = (f32[128,1408]{1,0:T(8,128)S(1)}, f32[128,1408]{1,0:T(8,128)S(1)}, u32[]{:S(2)}, u32[]{:S(2)}) collective-permute-start(f32[128,1408]{1,0:T(8,128)S(1)} %shard_map.77), channel_id=1, source_target_pairs={{0,1},{1,0},{2,3},{3,2},{4,5},{5,4},{6,7},{7,6},{8,9},{9,8},{10,11... | collective-permute-start | bytes 2162696 | tf_op jit(solution)/shard_map/ppermute | solution.py:305
  57.4 4.0 %collective-permute-start.1 = (f32[256,640]{1,0:T(8,128)S(1)}, f32[256,640]{1,0:T(8,128)S(1)}, u32[]{:S(2)}, u32[]{:S(2)}) collective-permute-start(f32[256,640]{1,0:T(8,128)S(1)} %get-tuple-element.50), channel_id=1, source_target_pairs={{0,1},{1,0},{2,3},{3,2},{4,5},{5,4},{6,7},{7,6},{8,9},{9,8},{10,11... | collective-permute-start | bytes 1966088 | tf_op jit(solution)/shard_map/ppermute | solution.py:332

commit v13 on v11

--- a/solution.py
+++ b/solution.py
@@ -19,8 +19,8 @@
 SIDE = 4
 GROUP = 4
 CUTS = 4
-NEAR = (0, 3, 1, 2)
-NEAR_AT = (0, 2, 3, 1)
+NEAR = (0, 2, 1, 3)
+NEAR_AT = (0, 2, 1, 3)
 FAR = (0, 2, 1, 3)
 FAR_AT = (0, 2, 1, 3)
 GROUPS = ZN // GROUP
@@ -40,7 +40,7 @@
 
 def head_at(group_ref, h):
     chip = (group_ref[0] + h) & (GROUP - 1)
-    return jnp.where(chip == 0, 0, jnp.where(chip == GROUP - 1, 1, chip + 1))
+    return jnp.where((chip == 1) | (chip == 2), GROUP - 1 - chip, chip)
 
 
 def causal(shape):

time: 120 us -> 120 us (level)
  no operation moved by 1% of the time
where the time goes in v13:
time: 120 us; the launch traced here: 119 us
  blocking collectives  107 us (89%)
  Pallas kernels  5.86 us (5%)
  starting transfers between devices  3.84 us (3%)
  local copies, waits for them, and re-layouts  1.52 us (1%)
    all_to_all x2, blocking collectives, body(): pay = lax.all_to_all(pay, 'z', 0, 0, tiled=True, axis_index_groups=near)  26.1 us
    all_to_all x1, blocking collectives, body(): far = lax.all_to_all(far, 'z', 0, 0, tiled=True, axis_index_groups=across)  23.7 us
    all_to_all x1, blocking collectives, body(): lax.all_to_all(grad.reshape(SIDE, SIDE * rows, width), every, 0, 0, tiled...  17.8 us
    all_to_all x1, blocking collectives, body(): part = lax.all_to_all(part, 'z', 0, 0, tiled=True)  16.8 us
    all_to_all x1, blocking collectives, body(): lax.all_to_all(part, every, 0, 0, tiled=True, axis_index_groups=second)  11.6 us
    all_to_all x1, blocking collectives, body(): part = lax.all_to_all(part, 'dp', 0, 0, tiled=True)  10.7 us
    pallas_call x12, Pallas kernels, call(): pl.pallas_call(kernel, out_shape=[jax.ShapeDtypeStruct(s, d) for s, d in...  5.86 us
  transfers between devices with their start and end apart: 2, of which 2 were waited for; matrix products, arithmetic and copies ran while one was open for 1% of the time, Pallas kernels for 2%

profile of v13, /device:TPU:32, one launch (start us, length us, event | category | flops | bytes accessed | tf_op | source)
XLA Modules:
  0.0 119.5 jit_solution(7716544369516508385)
XLA Ops:
  0.6 1.0 shard_map.77
  1.7 1.9 %collective-permute-start = (f32[128,1408]{1,0:T(8,128)S(1)}, f32[128,1408]{1,0:T(8,128)S(1)}, u32[]{:S(2)}, u32[]{:S(2)}) collective-permute-start(f32[128,1408]{1,0:T(8,128)S(1)} %shard_map.77), channel_id=1, source_target_pairs={{0,1},{1,0},{2,3},{3,2},{4,5},{5,4},{6,7},{7,6},{8,9},{9,8},{10,11... | collective-permute-start | bytes 2162696 | tf_op jit(solution)/shard_map/ppermute | solution.py:306
  3.6 1.7 %shard_map.76 = (bf16[128,256]{1,0:T(8,128)(2,1)S(1)}, bf16[128,256]{1,0:T(8,128)(2,1)S(1)}, bf16[128,256]{1,0:T(8,128)(2,1)S(1)}, f32[8,128]{1,0:T(8,128)S(1)},...) custom-call(s32[1]{0:T(128)} %bitcast.c_ref.refs_0_, ...), custom_call_target="tpu_custom_call" | custom-call | tf_op jit(solution)/shard_map/pallas_call | solution.py:254
  5.3 0.4 collective-permute-done.refs_9_
  5.8 1.3 %shard_map.78 = (f32[4,136,128]{2,1,0:T(8,128)S(1)}, bf16[256,256]{1,0:T(8,128)(2,1)S(1)}, bf16[256,256]{1,0:T(8,128)(2,1)S(1)}, f32[256,256]{1,0:T(8,128)S(1)},...) custom-call(s32[1]{0:T(128)} %bitcast.c_ref.refs_0_, ...), custom_call_target="tpu_custom_call" | custom-call | tf_op jit(solution)/shard_map/pallas_call | solution.py:254
  7.0 16.1 %all_to_all.35.in_ref = f32[4,136,128]{2,1,0:T(8,128)S(1)} all-to-all(f32[4,136,128]{2,1,0:T(8,128)S(1)} %get-tuple-element.39), channel_id=1, replica_groups={{0,4,2,6},{8,12,10,14},{16,20,18,22},{24,28,26,30},{1,5,3,7},{9,13,11,1..., dimensions={0} | all-to-all | bytes 557056 | tf_op jit(solution)/shard_map/all_to_all | solution.py:323
  23.2 23.7 %all_to_all.36.far_ref = f32[4,72,128]{2,1,0:T(8,128)S(1)} all-to-all(f32[4,72,128]{2,1,0:T(8,128)S(1)} %shard_map.79), channel_id=1, replica_groups={{0,20,10,30},{2,22,12,24},{4,16,14,26},{6,18,8,28},{1,21,11,31},{3,23,1..., dimensions={0} | all-to-all | bytes 294912 | tf_op jit(solution)/shard_map/all_to_all | solution.py:325
  46.9 0.1 shard_map.80
  47.0 10.0 %all_to_all.37.refs_2_ = f32[4,128,128]{2,1,0:T(8,128)S(1)} all-to-all(f32[4,128,128]{2,1,0:T(8,128)S(1)} %shard_map.80), channel_id=1, replica_groups={{0,4,2,6},{8,12,10,14},{16,20,18,22},{24,28,26,30},{1,5,3,7},{9,13,11,1..., dimensions={0} | all-to-all | bytes 524288 | tf_op jit(solution)/shard_map/all_to_all | solution.py:327
  57.0 0.3 shard_map.81
  57.3 1.9 %collective-permute-start.1 = (f32[256,640]{1,0:T(8,128)S(1)}, f32[256,640]{1,0:T(8,128)S(1)}, u32[]{:S(2)}, u32[]{:S(2)}) collective-permute-start(f32[256,640]{1,0:T(8,128)S(1)} %get-tuple-element.50), channel_id=1, source_target_pairs={{0,1},{1,0},{2,3},{3,2},{4,5},{5,4},{6,7},{7,6},{8,9},{9,8},{10,11... | collective-permute-start | bytes 1966088 | tf_op jit(solution)/shard_map/ppermute | solution.py:333
  59.2 0.2 copy.10
  59.4 0.2 reshape.26
  59.6 0.4 slice_bitcast_fusion
  60.1 0.2 copy.12
  60.3 0.1 reshape.28.xb_ref
  60.4 0.2 copy.11
  60.7 0.1 reshape.27.xa_ref
  60.8 0.2 shard_map.82.near_ref
  61.0 0.3 collective-permute-done.1.recv_ref
  61.3 0.4 shard_map.83
  61.7 17.8 %all_to_all.38.in_ref = f32[4,128,768]{2,1,0:T(8,128)S(1)} all-to-all(f32[4,128,768]{2,1,0:T(8,128)S(1)} %bitcast.18), channel_id=1, replica_groups={{0,128,256,384},{32,160,288,416},{64,192,320,448},{96,224,352,480},{2,1..., dimensions={0} | all-to-all | bytes 3145728 | tf_op jit(solution)/shard_map/all_to_all | solution.py:344
  79.4 0.1 shard_map.84
  79.5 11.6 %all_to_all.39.in_ref = f32[4,32,768]{2,1,0:T(8,128)S(1)} all-to-all(f32[4,32,768]{2,1,0:T(8,128)S(1)} %shard_map.84), channel_id=1, replica_groups={{0,32,64,96},{128,160,192,224},{256,288,320,352},{384,416,448,480},{2,3..., dimensions={0} | all-to-all | bytes 786432 | tf_op jit(solution)/shard_map/all_to_all | solution.py:346
  91.2 16.8 %all_to_all.40.refs_2_ = f32[16,2,768]{2,1,0:T(2,128)S(1)} all-to-all(f32[16,2,768]{2,1,0:T(2,128)S(1)} %shard_map.85), channel_id=1, replica_groups=mesh['dp'=16,'z'=16,'c'=2] {'z'}, dimensions={0} | all-to-all | bytes 196608 | tf_op jit(solution)/shard_map/all_to_all | solution.py:348
  108.0 0.1 shard_map.86
  108.0 10.7 %all_to_all.41.in_ref = f32[16,2,768]{2,1,0:T(2,128)S(1)} all-to-all(f32[16,2,768]{2,1,0:T(2,128)S(1)} %shard_map.86), channel_id=1, replica_groups=mesh['dp'=16,'z'=16,'c'=2] {'dp'}, dimensions={0} | all-to-all | bytes 196608 | tf_op jit(solution)/shard_map/all_to_all | solution.py:350
  118.7 0.7 shard_map.87
  (2 shorter events, 0.1 us)
Async XLA Ops:
  1.7 4.1 %collective-permute-start = (f32[128,1408]{1,0:T(8,128)S(1)}, f32[128,1408]{1,0:T(8,128)S(1)}, u32[]{:S(2)}, u32[]{:S(2)}) collective-permute-start(f32[128,1408]{1,0:T(8,128)S(1)} %shard_map.77), channel_id=1, source_target_pairs={{0,1},{1,0},{2,3},{3,2},{4,5},{5,4},{6,7},{7,6},{8,9},{9,8},{10,11... | collective-permute-start | bytes 2162696 | tf_op jit(solution)/shard_map/ppermute | solution.py:306
  57.3 4.0 %collective-permute-start.1 = (f32[256,640]{1,0:T(8,128)S(1)}, f32[256,640]{1,0:T(8,128)S(1)}, u32[]{:S(2)}, u32[]{:S(2)}) collective-permute-start(f32[256,640]{1,0:T(8,128)S(1)} %get-tuple-element.50), channel_id=1, source_target_pairs={{0,1},{1,0},{2,3},{3,2},{4,5},{5,4},{6,7},{7,6},{8,9},{9,8},{10,11... | collective-permute-start | bytes 1966088 | tf_op jit(solution)/shard_map/ppermute | solution.py:333

commit v14 on v13

--- a/solution.py
+++ b/solution.py
@@ -21,8 +21,8 @@
 CUTS = 4
 NEAR = (0, 2, 1, 3)
 NEAR_AT = (0, 2, 1, 3)
-FAR = (0, 2, 1, 3)
-FAR_AT = (0, 2, 1, 3)
+FAR = (0, 1, 2, 3)
+FAR_AT = (0, 1, 2, 3)
 GROUPS = ZN // GROUP
 
 

time: 120 us -> 120 us (level)
  no operation moved by 1% of the time
where the time goes in v14:
time: 120 us; the launch traced here: 119 us
  blocking collectives  106 us (88%)
  Pallas kernels  5.85 us (5%)
  starting transfers between devices  3.84 us (3%)
  local copies, waits for them, and re-layouts  1.52 us (1%)
    all_to_all x2, blocking collectives, body(): pay = lax.all_to_all(pay, 'z', 0, 0, tiled=True, axis_index_groups=near)  26.3 us
    all_to_all x1, blocking collectives, body(): far = lax.all_to_all(far, 'z', 0, 0, tiled=True, axis_index_groups=across)  23 us
    all_to_all x1, blocking collectives, body(): lax.all_to_all(grad.reshape(SIDE, SIDE * rows, width), every, 0, 0, tiled...  17.8 us
    all_to_all x1, blocking collectives, body(): part = lax.all_to_all(part, 'z', 0, 0, tiled=True)  16.9 us
    all_to_all x1, blocking collectives, body(): lax.all_to_all(part, every, 0, 0, tiled=True, axis_index_groups=second)  11.6 us
    all_to_all x1, blocking collectives, body(): part = lax.all_to_all(part, 'dp', 0, 0, tiled=True)  10.7 us
    pallas_call x12, Pallas kernels, call(): pl.pallas_call(kernel, out_shape=[jax.ShapeDtypeStruct(s, d) for s, d in...  5.85 us
  transfers between devices with their start and end apart: 2, of which 2 were waited for; matrix products, arithmetic and copies ran while one was open for 1% of the time, Pallas kernels for 2%

profile of v14, /device:TPU:32, one launch (start us, length us, event | category | flops | bytes accessed | tf_op | source)
XLA Modules:
  0.0 119.1 jit_solution(18259011567340961238)
XLA Ops:
  0.6 1.0 shard_map.77
  1.7 1.9 %collective-permute-start = (f32[128,1408]{1,0:T(8,128)S(1)}, f32[128,1408]{1,0:T(8,128)S(1)}, u32[]{:S(2)}, u32[]{:S(2)}) collective-permute-start(f32[128,1408]{1,0:T(8,128)S(1)} %shard_map.77), channel_id=1, source_target_pairs={{0,1},{1,0},{2,3},{3,2},{4,5},{5,4},{6,7},{7,6},{8,9},{9,8},{10,11... | collective-permute-start | bytes 2162696 | tf_op jit(solution)/shard_map/ppermute | solution.py:306
  3.6 1.7 %shard_map.76 = (bf16[128,256]{1,0:T(8,128)(2,1)S(1)}, bf16[128,256]{1,0:T(8,128)(2,1)S(1)}, bf16[128,256]{1,0:T(8,128)(2,1)S(1)}, f32[8,128]{1,0:T(8,128)S(1)},...) custom-call(s32[1]{0:T(128)} %bitcast.c_ref.refs_0_, ...), custom_call_target="tpu_custom_call" | custom-call | tf_op jit(solution)/shard_map/pallas_call | solution.py:254
  5.3 0.4 collective-permute-done.refs_9_
  5.8 1.3 %shard_map.78 = (f32[4,136,128]{2,1,0:T(8,128)S(1)}, bf16[256,256]{1,0:T(8,128)(2,1)S(1)}, bf16[256,256]{1,0:T(8,128)(2,1)S(1)}, f32[256,256]{1,0:T(8,128)S(1)},...) custom-call(s32[1]{0:T(128)} %bitcast.c_ref.refs_0_, ...), custom_call_target="tpu_custom_call" | custom-call | tf_op jit(solution)/shard_map/pallas_call | solution.py:254
  7.0 16.1 %all_to_all.35.in_ref = f32[4,136,128]{2,1,0:T(8,128)S(1)} all-to-all(f32[4,136,128]{2,1,0:T(8,128)S(1)} %get-tuple-element.39), channel_id=1, replica_groups={{0,4,2,6},{8,12,10,14},{16,20,18,22},{24,28,26,30},{1,5,3,7},{9,13,11,1..., dimensions={0} | all-to-all | bytes 557056 | tf_op jit(solution)/shard_map/all_to_all | solution.py:323
  23.2 23.0 %all_to_all.36.far_ref = f32[4,72,128]{2,1,0:T(8,128)S(1)} all-to-all(f32[4,72,128]{2,1,0:T(8,128)S(1)} %shard_map.79), channel_id=1, replica_groups={{0,10,20,30},{2,12,22,24},{4,14,16,26},{6,8,18,28},{1,11,21,31},{3,13,2..., dimensions={0} | all-to-all | bytes 294912 | tf_op jit(solution)/shard_map/all_to_all | solution.py:325
  46.3 10.2 %all_to_all.37.refs_2_ = f32[4,128,128]{2,1,0:T(8,128)S(1)} all-to-all(f32[4,128,128]{2,1,0:T(8,128)S(1)} %shard_map.80), channel_id=1, replica_groups={{0,4,2,6},{8,12,10,14},{16,20,18,22},{24,28,26,30},{1,5,3,7},{9,13,11,1..., dimensions={0} | all-to-all | bytes 524288 | tf_op jit(solution)/shard_map/all_to_all | solution.py:327
  56.5 0.3 shard_map.81
  56.8 1.9 %collective-permute-start.1 = (f32[256,640]{1,0:T(8,128)S(1)}, f32[256,640]{1,0:T(8,128)S(1)}, u32[]{:S(2)}, u32[]{:S(2)}) collective-permute-start(f32[256,640]{1,0:T(8,128)S(1)} %get-tuple-element.50), channel_id=1, source_target_pairs={{0,1},{1,0},{2,3},{3,2},{4,5},{5,4},{6,7},{7,6},{8,9},{9,8},{10,11... | collective-permute-start | bytes 1966088 | tf_op jit(solution)/shard_map/ppermute | solution.py:333
  58.7 0.2 copy.10
  58.9 0.2 reshape.26
  59.1 0.4 slice_bitcast_fusion
  59.6 0.2 copy.12
  59.8 0.1 reshape.28.xb_ref
  59.9 0.2 copy.11
  60.2 0.1 reshape.27.xa_ref
  60.3 0.2 shard_map.82.near_ref
  60.5 0.3 collective-permute-done.1.recv_ref
  60.8 0.4 shard_map.83
  61.1 17.8 %all_to_all.38.in_ref = f32[4,128,768]{2,1,0:T(8,128)S(1)} all-to-all(f32[4,128,768]{2,1,0:T(8,128)S(1)} %bitcast.18), channel_id=1, replica_groups={{0,128,256,384},{32,160,288,416},{64,192,320,448},{96,224,352,480},{2,1..., dimensions={0} | all-to-all | bytes 3145728 | tf_op jit(solution)/shard_map/all_to_all | solution.py:344
  78.9 0.1 shard_map.84
  79.0 11.6 %all_to_all.39.in_ref = f32[4,32,768]{2,1,0:T(8,128)S(1)} all-to-all(f32[4,32,768]{2,1,0:T(8,128)S(1)} %shard_map.84), channel_id=1, replica_groups={{0,32,64,96},{128,160,192,224},{256,288,320,352},{384,416,448,480},{2,3..., dimensions={0} | all-to-all | bytes 786432 | tf_op jit(solution)/shard_map/all_to_all | solution.py:346
  90.7 16.9 %all_to_all.40.refs_2_ = f32[16,2,768]{2,1,0:T(2,128)S(1)} all-to-all(f32[16,2,768]{2,1,0:T(2,128)S(1)} %shard_map.85), channel_id=1, replica_groups=mesh['dp'=16,'z'=16,'c'=2] {'z'}, dimensions={0} | all-to-all | bytes 196608 | tf_op jit(solution)/shard_map/all_to_all | solution.py:348
  107.6 0.1 shard_map.86
  107.7 10.7 %all_to_all.41.in_ref = f32[16,2,768]{2,1,0:T(2,128)S(1)} all-to-all(f32[16,2,768]{2,1,0:T(2,128)S(1)} %shard_map.86), channel_id=1, replica_groups=mesh['dp'=16,'z'=16,'c'=2] {'dp'}, dimensions={0} | all-to-all | bytes 196608 | tf_op jit(solution)/shard_map/all_to_all | solution.py:350
  118.4 0.7 shard_map.87
  (3 shorter events, 0.1 us)
Async XLA Ops:
  1.7 4.1 %collective-permute-start = (f32[128,1408]{1,0:T(8,128)S(1)}, f32[128,1408]{1,0:T(8,128)S(1)}, u32[]{:S(2)}, u32[]{:S(2)}) collective-permute-start(f32[128,1408]{1,0:T(8,128)S(1)} %shard_map.77), channel_id=1, source_target_pairs={{0,1},{1,0},{2,3},{3,2},{4,5},{5,4},{6,7},{7,6},{8,9},{9,8},{10,11... | collective-permute-start | bytes 2162696 | tf_op jit(solution)/shard_map/ppermute | solution.py:306
  56.8 4.0 %collective-permute-start.1 = (f32[256,640]{1,0:T(8,128)S(1)}, f32[256,640]{1,0:T(8,128)S(1)}, u32[]{:S(2)}, u32[]{:S(2)}) collective-permute-start(f32[256,640]{1,0:T(8,128)S(1)} %get-tuple-element.50), channel_id=1, source_target_pairs={{0,1},{1,0},{2,3},{3,2},{4,5},{5,4},{6,7},{7,6},{8,9},{9,8},{10,11... | collective-permute-start | bytes 1966088 | tf_op jit(solution)/shard_map/ppermute | solution.py:333
